TPU v7x, 512 devices: a whole 4x4x16 slice. The times are simulated.
512 devices in a mesh: ctx: 64 (over z, y), head: 8 (over x, core).
Axes of the slice: x: 4, y: 4, z: 16, core: 2. Of those that a mesh axis runs over, the one named last changes fastest.
Arguments:
- hidden_states: bfloat16 [8192, 8192], P('ctx'), may hold values from -16 to 16
- queries: bfloat16 [8192, 8192], P('ctx', 'head'), may hold values from -110 to 110
- keys: bfloat16 [8192, 1024], P('ctx', 'head'), may hold values from -6 to 6
- values: bfloat16 [8192, 1024], P('ctx', 'head'), may hold values from -6 to 6
- output_gradient: bfloat16 [8192, 8192], P('ctx', 'head'), may hold values from -12 to 12
- doc_blocks: int32 [5], replicated, may hold values from 1 to 24, 64 in all
Outputs:
- ascent_key: float32 [8192, 1024], P('ctx', 'head')
- ascent_value: float32 [8192, 1024], P('ctx', 'head')
Inputs may be any that keep to these rules, and one draw needn't show every extreme that they name: `doc_blocks`: document lengths count blocks of 128 tokens; they sum to 64, and the longest holds exactly 24 blocks.
All inputs are finite; a program needn't handle non-finite values.
Results may differ from a plain program's by a relative error of at most 0.029.
Values may be sent and summed in bfloat16 or wider, within the bound.
No kernel may reach another device: no remote copies, remote signals or barrier semaphores. Data moves between devices by JAX's collectives and lax.ppermute only.
A program may use at most 64 MiB of HBM per device.

v0:
```python
import jax
import jax.numpy as jnp
from jax import lax
from jax.sharding import PartitionSpec as P

MODEL_WIDTH = 8192
QUERY_HEADS = 64
KEY_VALUE_HEADS = 8
HEAD_SIZE = 128
BLOCK_TOKENS = 128


def shifted(value, axis, steps):
    count = lax.axis_size(axis)
    initial, last = (max(0, -steps), min(count, count - steps))
    return lax.ppermute(value, axis, [(source, source + steps) for source in range(initial, last)])


def doc_ids(positions, doc_blocks):
    ends = jnp.cumsum(doc_blocks) * BLOCK_TOKENS
    found = jnp.sum((positions[:, None] >= ends[None, :]).astype(jnp.int32), axis=1)
    return jnp.where(positions >= 0, found, -1)


def undo_rotary(grads, positions):
    half = HEAD_SIZE // 2
    freqs = 500000.0 ** (-(jnp.arange(half, dtype=jnp.float32) * 2.0) / HEAD_SIZE)
    angles = positions.astype(jnp.float32)[:, None] * freqs[None, :]
    cosine = jnp.concatenate([jnp.cos(angles), jnp.cos(angles)], axis=-1)[:, None, :]
    sine = jnp.concatenate([jnp.sin(angles), jnp.sin(angles)], axis=-1)[:, None, :]
    shaped = grads.reshape(grads.shape[0], -1, HEAD_SIZE)
    rotated = jnp.concatenate([-shaped[..., half:], shaped[..., :half]], axis=-1)
    return (shaped * cosine - rotated * sine).reshape(grads.shape)


def per_device(hidden_states, queries, keys, values, output_gradient, doc_blocks):
    tok = keys.shape[0]
    kv_cols = keys.shape[1]
    heads = kv_cols // HEAD_SIZE
    query_group = QUERY_HEADS // KEY_VALUE_HEADS
    scale = HEAD_SIZE ** (-0.5)
    cycle = lax.axis_size("ctx")
    reach = min(24, cycle // 2)
    here = lax.axis_index("ctx")
    local = jnp.arange(tok, dtype=jnp.int32)
    q_pos = here * tok + local
    q_ids = doc_ids(q_pos, doc_blocks)

    def advance(index, carry):
        cur_keys, cur_values, key_stack, value_stack = carry
        cur_keys, cur_values = shifted((cur_keys, cur_values), "ctx", 1)
        key_stack = lax.dynamic_update_index_in_dim(key_stack, cur_keys, index + 1, 0)
        value_stack = lax.dynamic_update_index_in_dim(value_stack, cur_values, index + 1, 0)
        return (cur_keys, cur_values, key_stack, value_stack)

    empty = jnp.zeros((reach + 1, tok, kv_cols), jnp.bfloat16)
    start_state = (keys, values, empty.at[0].set(keys), empty.at[0].set(values))
    _, _, key_stack, value_stack = lax.fori_loop(0, reach, advance, start_state)
    q_four = queries.reshape(tok, heads, query_group, HEAD_SIZE)
    g_four = output_gradient.reshape(tok, heads, query_group, HEAD_SIZE)
    offsets = jnp.arange(reach + 1, dtype=jnp.int32)

    def block_mask(offset):
        k_pos = (here - offset) * tok + local
        k_ids = doc_ids(k_pos, doc_blocks)
        return (
            (q_ids[:, None] == k_ids[None, :])
            & (k_pos[None, :] <= q_pos[:, None])
            & (k_pos[None, :] >= 0)
        )

    def block_scores(key_blk):
        return (
            jnp.einsum(
                "tkgd,ukd->kgtu",
                q_four,
                key_blk.reshape(tok, heads, HEAD_SIZE),
                preferred_element_type=jnp.float32,
            )
            * scale
        )

    def softmax_stats(carry, inputs):
        top, total = carry
        key_blk, offset = inputs
        score = block_scores(key_blk)
        mask = block_mask(offset)
        new_top = jnp.maximum(top, jnp.max(jnp.where(mask, score, -1e30), axis=-1, keepdims=True))
        total = total * jnp.exp(top - new_top) + jnp.sum(
            jnp.where(mask, jnp.exp(score - new_top), 0.0), axis=-1, keepdims=True
        )
        return ((new_top, total), None)

    start_top = jnp.full((heads, query_group, tok, 1), -1e30, jnp.float32)
    start_total = jnp.zeros((heads, query_group, tok, 1), jnp.float32)
    (top, total), _ = lax.scan(softmax_stats, (start_top, start_total), (key_stack, offsets))
    lse = top + jnp.log(total)

    def probabilities(key_blk, offset):
        score = block_scores(key_blk)
        return jnp.where(block_mask(offset), jnp.exp(score - lse), 0.0)

    def output_pass(acc, inputs):
        key_blk, value_blk, offset = inputs
        prob16 = probabilities(key_blk, offset).astype(jnp.bfloat16)
        acc = acc + jnp.einsum(
            "kgtu,ukd->tkgd",
            prob16,
            value_blk.reshape(tok, heads, HEAD_SIZE),
            preferred_element_type=jnp.float32,
        )
        return (acc, None)

    attn_acc, _ = lax.scan(
        output_pass,
        jnp.zeros((tok, heads, query_group, HEAD_SIZE), jnp.float32),
        (key_stack, value_stack, offsets),
    )
    attn_out = attn_acc.astype(jnp.bfloat16)
    delta = jnp.sum(g_four.astype(jnp.float32) * attn_out.astype(jnp.float32), axis=-1)
    delta = jnp.transpose(delta, (1, 2, 0))[..., None]

    def gradient_pass(carry, inputs):
        key_blk, value_blk, offset = inputs
        value_four = value_blk.reshape(tok, heads, HEAD_SIZE)
        prob = probabilities(key_blk, offset)
        prob16 = prob.astype(jnp.bfloat16)
        dprob = jnp.einsum("tkgd,ukd->kgtu", g_four, value_four, preferred_element_type=jnp.float32)
        dscore = (prob * (dprob - delta)).astype(jnp.bfloat16)
        key_portion = (
            jnp.einsum("kgtu,tkgd->ukd", dscore, q_four, preferred_element_type=jnp.float32) * scale
        )
        value_portion = jnp.einsum(
            "kgtu,tkgd->ukd", prob16, g_four, preferred_element_type=jnp.float32
        )
        return (carry, (key_portion.reshape(tok, kv_cols), value_portion.reshape(tok, kv_cols)))

    _, (key_parts, value_parts) = lax.scan(gradient_pass, 0, (key_stack, value_stack, offsets))

    def return_step(index, carry):
        key_running, value_running = carry
        key_running, value_running = shifted((key_running, value_running), "ctx", -1)
        slot = reach - 1 - index
        key_running = key_running + lax.dynamic_index_in_dim(key_parts, slot, 0, keepdims=False)
        value_running = value_running + lax.dynamic_index_in_dim(
            value_parts, slot, 0, keepdims=False
        )
        return (key_running, value_running)

    key_total, value_total = lax.fori_loop(
        0, reach, return_step, (key_parts[reach], value_parts[reach])
    )
    pre_key = undo_rotary(key_total, q_pos).astype(jnp.bfloat16)
    pre_value = value_total.astype(jnp.bfloat16)
    columns = lax.all_to_all(hidden_states, "ctx", split_axis=1, concat_axis=0, tiled=True)
    inputs = columns
    dims = (((0,), (0,)), ((), ()))
    key_sum = lax.dot_general(
        inputs,
        lax.all_gather(pre_key, "ctx", axis=0, tiled=True),
        dims,
        preferred_element_type=jnp.float32,
    )
    value_sum = lax.dot_general(
        inputs,
        lax.all_gather(pre_value, "ctx", axis=0, tiled=True),
        dims,
        preferred_element_type=jnp.float32,
    )
    squared_entries = jnp.sum(key_sum * key_sum) + jnp.sum(value_sum * value_sum)
    squared_entries = lax.psum(squared_entries, ("ctx", "head"))
    squared_mean = squared_entries / (2.0 * MODEL_WIDTH * KEY_VALUE_HEADS * HEAD_SIZE)
    factor = 1.0 / jnp.sqrt(squared_mean + 1e-06)
    return (key_sum * factor, value_sum * factor)


def solution(mesh):
    placed = (
        P("ctx", None),
        P("ctx", "head"),
        P("ctx", "head"),
        P("ctx", "head"),
        P("ctx", "head"),
        P(),
    )
    return jax.shard_map(
        per_device,
        mesh=mesh,
        in_specs=placed,
        out_specs=(P("ctx", "head"), P("ctx", "head")),
        check_vma=False,
    )
```

profile of v0, /device:TPU:1, one launch (start us, length us, event | category | flops | bytes accessed | tf_op | source)
XLA Modules:
  0.0 1260.5 jit_solution(5850820216458060114)
XLA Ops:
  8.7 4.1 copy.44
  12.8 19.7 %all-to-all-start = ((bf16[128,64,128]{0,2,1:T(8,128)(2,1)}), bf16[128,64,128]{0,2,1:T(8,128)(2,1)}, u32[]{:S(2)}, u32[]{:S(2)}) async-start(bf16[128,64,128]{0,2,1:T(8,128)(2,1)} %bitcast.18), calls=%async_computation | async-start | bytes 4194304 | tf_op jit(solution)/shard_map/all_to_all | solution.py:155
  33.6 302.5 %while.81 = (s32[]{:T(128)}, bf16[128,128]{1,0:T(8,128)(2,1)S(1)}, bf16[128,128]{1,0:T(8,128)(2,1)S(1)}, bf16[25,128,128]{2,1,0:T(8,128)(2,1)S(1)}, bf16[25,128,...) while((s32[]{:T(128)}, bf16[128,128]{1,0:T(8,128)(2,1)S(1)}, bf16[128,128]{1,0:T(8,128)(2,1)S(1)}, ...), condition=%wide.region_1.2_spmd, body=%wide.region_0.0_spmd.sunk | while | flops 5 | bytes 524503 | solution.py:58
  40.6 4.0 collective-permute-start
  48.2 77.4 %collective-permute-start = (bf16[128,128]{1,0:T(8,128)(2,1)S(1)}, bf16[128,128]{1,0:T(8,128)(2,1)S(1)}, u32[]{:S(2)}, u32[]{:S(2)}) collective-permute-start(bf16[128,128]{1,0:T(8,128)(2,1)S(1)} %get-tuple-element.1358), channel_id=1, source_target_pairs={{0,8},{8,16},{16,24},{24,32},{32,40},{40,48},{48,56},{56,64},{64,7... | collective-permute-start | bytes 98312 | tf_op jit(solution)/shard_map/while/body/eval_jaxpr/ppermute | solution.py:16
  125.6 8.6 collective-permute-start.1
  135.3 4.0 collective-permute-start
  139.4 4.0 collective-permute-start.1
  156.9 5.4 collective-permute-start.1
  166.9 4.6 collective-permute-start.1
  185.0 4.5 collective-permute-start.1
  220.5 4.5 collective-permute-start.1
  230.1 5.1 collective-permute-start.1
  240.0 5.6 collective-permute-start.1
  250.4 4.8 collective-permute-start.1
  259.9 4.7 collective-permute-start.1
  269.3 5.7 collective-permute-start.1
  279.7 5.7 collective-permute-start.1
  290.1 4.9 collective-permute-start.1
  299.8 5.2 collective-permute-start.1
  309.7 5.2 collective-permute-start.1
  319.7 4.9 collective-permute-start.1
  329.3 5.8 collective-permute-start.1
  336.1 44.4 %while.84 = (s32[]{:T(128)}, f32[1,8,128,1]{2,1,3,0:T(8,128)S(1)}, f32[1,8,128,1]{2,1,3,0:T(8,128)S(1)}, s32[128]{0:T(128)S(1)}, s32[25]{0:T(128)S(1)}, /*index=...) while((s32[]{:T(128)}, f32[1,8,128,1]{2,1,3,0:T(8,128)S(1)}, ...), condition=%wide.region_8.9_spmd.clone, body=%wide.region_4.8_spmd.clone.sunk | while | flops 34414216 | bytes 1451516 | solution.py:96
  380.6 49.7 %while.85 = (s32[]{:T(128)}, f32[128,1,8,128]{0,3,2,1:T(8,128)S(1)}, bf16[25,128,128]{2,1,0:T(8,128)(2,1)S(1)}, s32[128]{0:T(128)S(1)}, s32[25]{0:T(128)S(1)}, /...) while((s32[]{:T(128)}, ...), condition=%wide.region_11.12_spmd.clone, body=%wide.region_9.11_spmd.clone.sunk | while | flops 67963528 | bytes 1419775 | solution.py:114
  430.7 92.0 %while.83 = (s32[]{:T(128)}, f32[25,128,128]{2,1,0:T(8,128)}, f32[25,128,128]{2,1,0:T(8,128)}, s32[128]{0:T(128)S(1)}, s32[25]{0:T(128)S(1)}, /*index=5*/s32[]{:...) while((s32[]{:T(128)}, f32[25,128,128]{2,1,0:T(8,128)}, ...), condition=%wide.region_15.16_spmd.clone, body=%wide.region_13.15_spmd.clone.sunk | while | flops 135219840 | bytes 2866185 | solution.py:138
  524.4 239.1 %while.82 = (s32[]{:T(128)}, f32[128,128]{1,0:T(8,128)S(1)}, f32[128,128]{1,0:T(8,128)S(1)}, f32[25,128,128]{2,1,0:T(8,128)}, f32[25,128,128]{2,1,0:T(8,128)}, /*index=5*/s32[]{:T(128)}, s32[]{:T(128)}, s32[]{:T(128)}, s32[]{:T(128)}) while((s32[]{:T(128)}, f32[128,128]{1,0:T(8,128)S(1)}, f32[128,128]{1,0:T(8,128)S(1)}, ...), condition=%wide.region_17.18_spmd, body=%wide.region_16.17_spmd.sunk | while | flops 32774 | bytes 917731 | solution.py:150
  535.4 4.7 collective-permute-done.3
  553.5 5.2 collective-permute-done.3
  564.1 4.6 collective-permute-done.3
  574.1 4.6 collective-permute-done.3
  584.0 4.5 collective-permute-done.3
  593.9 5.0 collective-permute-done.3
  605.2 4.6 collective-permute-done.3
  616.1 4.8 collective-permute-done.3
  644.9 4.5 collective-permute-done.3
  654.8 4.5 collective-permute-done.3
  664.7 4.9 collective-permute-done.3
  674.6 4.7 collective-permute-done.3
  684.7 5.2 collective-permute-done.3
  695.2 4.5 collective-permute-done.3
  705.2 5.0 collective-permute-done.3
  716.5 4.6 collective-permute-done.3
  727.4 4.8 collective-permute-done.3
  756.2 4.5 collective-permute-done.3
  768.7 228.7 %all-gather.3.cloned.1.call-done = bf16[8192,128]{1,0:T(8,128)(2,1)} async-done(((bf16[128,128]{1,0:T(8,128)(2,1)}), bf16[8192,128]{1,0:T(8,128)(2,1)}) %all-gather.3.cloned.1.call-update) | async-done | bytes 2097168 | tf_op jit(solution)/shard_map/all_gather | solution.py:160
  1000.3 137.6 %all-gather.5.cloned.1.call-done = bf16[8192,128]{1,0:T(8,128)(2,1)} async-done(((bf16[128,128]{1,0:T(8,128)(2,1)}), bf16[8192,128]{1,0:T(8,128)(2,1)}) %all-gather.5.cloned.1.call-update) | async-done | bytes 2097168 | tf_op jit(solution)/shard_map/all_gather | solution.py:166
  1142.1 109.4 %psum.7 = f32[]{:T(128)} all-reduce(f32[]{:T(128)S(6)} %add.229), channel_id=1, replica_groups=mesh['ctx'=64,'head'=8] {'ctx','head'}, use_global_device_ids=true, to_apply=%region_20.21 | all-reduce | flops 1 | bytes 8 | tf_op jit(solution)/shard_map/psum | solution.py:171
  (1096 shorter events, 432.8 us)
Async XLA Ops:
  12.8 752.7 %all-to-all-start = ((bf16[128,64,128]{0,2,1:T(8,128)(2,1)}), bf16[128,64,128]{0,2,1:T(8,128)(2,1)}, u32[]{:S(2)}, u32[]{:S(2)}) async-start(bf16[128,64,128]{0,2,1:T(8,128)(2,1)} %bitcast.18), calls=%async_computation | async-start | bytes 4194304 | tf_op jit(solution)/shard_map/all_to_all | solution.py:155
  32.4 964.9 %all-gather.3.cloned.1.call-start = ((), (), s32[]{:S(2)}) async-start(), calls=%async_computation.1 | async-start | bytes 2129920 | tf_op jit(solution)/shard_map/all_gather | solution.py:160
  48.2 86.1 %collective-permute-start = (bf16[128,128]{1,0:T(8,128)(2,1)S(1)}, bf16[128,128]{1,0:T(8,128)(2,1)S(1)}, u32[]{:S(2)}, u32[]{:S(2)}) collective-permute-start(bf16[128,128]{1,0:T(8,128)(2,1)S(1)} %get-tuple-element.1358), channel_id=1, source_target_pairs={{0,8},{8,16},{16,24},{24,32},{32,40},{40,48},{48,56},{56,64},{64,7... | collective-permute-start | bytes 98312 | tf_op jit(solution)/shard_map/while/body/eval_jaxpr/ppermute | solution.py:16
  125.6 9.6 collective-permute-start.1
  135.3 8.1 collective-permute-start
  144.5 7.7 collective-permute-start
  153.2 9.0 collective-permute-start
  163.3 8.3 collective-permute-start
  172.6 7.7 collective-permute-start
  181.4 8.2 collective-permute-start
  190.6 7.7 collective-permute-start
  199.4 7.7 collective-permute-start
  208.1 7.7 collective-permute-start
  216.8 8.1 collective-permute-start
  226.2 9.1 collective-permute-start
  236.3 9.4 collective-permute-start
  246.7 8.5 collective-permute-start
  256.2 8.4 collective-permute-start
  265.6 9.4 collective-permute-start
  276.1 9.4 collective-permute-start
  286.5 8.6 collective-permute-start
  296.1 8.9 collective-permute-start
  306.1 8.9 collective-permute-start
  316.0 8.6 collective-permute-start
  325.6 9.4 collective-permute-start
  534.0 7.9 collective-permute-start.2
  550.9 7.8 collective-permute-start.3
  552.2 8.4 collective-permute-start.2
  562.8 7.8 collective-permute-start.2
  572.8 7.8 collective-permute-start.2
  582.7 7.7 collective-permute-start.2
  591.3 7.6 collective-permute-start.3
  592.6 9.2 collective-permute-start.2
  603.9 8.8 collective-permute-start.2
  614.8 8.9 collective-permute-start.2
  643.6 7.7 collective-permute-start.2
  653.5 7.7 collective-permute-start.2
  663.4 7.7 collective-permute-start.2
  673.3 7.9 collective-permute-start.2
  682.1 7.8 collective-permute-start.3
  683.4 8.4 collective-permute-start.2
  693.9 7.8 collective-permute-start.2
  702.5 7.6 collective-permute-start.3
  703.8 9.2 collective-permute-start.2
  715.2 8.8 collective-permute-start.2
  726.1 8.9 collective-permute-start.2
  754.9 7.7 collective-permute-start.2
  764.7 373.2 %all-gather.5.cloned.1.call-start = ((), (), s32[]{:S(2)}) async-start(), calls=%async_computation.2 | async-start | bytes 2129920 | tf_op jit(solution)/shard_map/all_gather | solution.py:166
  (54 other events, 408.0 us)
Sparse Core Ops, SparseCore 0:
  764.8 232.5 all-gather.2
  1000.9 136.9 all-gather.4
where the time goes:
time: 1270 us; the launch traced here: 1260 us
  waiting for transfers between devices  526 us (41%)
  starting transfers between devices  358 us (28%)
  blocking collectives  109 us (9%)
  matrix products  76.2 us (6%)
  other arithmetic  62.9 us (5%)
  local copies, waits for them, and re-layouts  59.3 us (5%)
  loops' own time  52.2 us (4%)
  between operations  16.3 us (1%)
    ppermute x96, starting transfers between devices, shifted(): lax.ppermute(value, axis, [(source, source + steps) for source in range(i...  339 us
    all_gather x1, waiting for transfers between devices, per_device(): lax.all_gather(pre_key, 'ctx', axis=0, tiled=True)  229 us
    ppermute x96, waiting for transfers between devices, shifted(): lax.ppermute(value, axis, [(source, source + steps) for source in range(i...  160 us
    all_gather x1, waiting for transfers between devices, per_device(): lax.all_gather(pre_value, 'ctx', axis=0, tiled=True)  138 us
    psum x1, blocking collectives, per_device(): squared_entries = lax.psum(squared_entries, ('ctx', 'head'))  109 us
    dynamic_slice x75, local copies, waits for them, and re-layouts, per_device(): lax.scan(softmax_stats, (start_top, start_total), (key_stack, offsets))  45.5 us
  transfers between devices with their start and end apart: 99, of which 74 were waited for; matrix products, arithmetic and copies ran while one was open for 15% of the time, Pallas kernels for 0%

commit v1 on v0

v1 whole, which is shorter than its diff:
```python
import functools

import jax
import jax.numpy as jnp
from jax import lax
from jax.experimental import pallas as pl
from jax.experimental.pallas import tpu as pltpu
from jax.sharding import Mesh, PartitionSpec as P

MODEL_WIDTH = 8192
QUERY_HEADS = 64
KEY_VALUE_HEADS = 8
HEAD_SIZE = 128
BLOCK_TOKENS = 128
GROUP = QUERY_HEADS // KEY_VALUE_HEADS
ROWS = GROUP * BLOCK_TOKENS
PLANES = 7
SIDE = 4
NEGATIVE = -1e30
SCALE = HEAD_SIZE ** (-0.5)
LOG2E = 1.4426950408889634
EXP_SCALE = SCALE * LOG2E
Z = ("z_hi", "z_lo")
CTX = ("z_hi", "z_lo", "y")

NT = (((1,), (1,)), ((), ()))
NN = (((1,), (0,)), ((), ()))
TN = (((0,), (0,)), ((), ()))


def axis_total(axis):
    names = axis if isinstance(axis, tuple) else (axis,)
    total = 1
    for name in names:
        total *= lax.axis_size(name)
    return total


def rotate(value, axis, steps):
    count = axis_total(axis)
    return lax.ppermute(value, axis, [(at, (at + steps) % count) for at in range(count)])


def stack_heads(src_ref, dst_ref):
    for head in range(GROUP):
        dst_ref[head * BLOCK_TOKENS:(head + 1) * BLOCK_TOKENS, :] = src_ref[
            :, head * HEAD_SIZE:(head + 1) * HEAD_SIZE
        ]


def causal_mask():
    token = lax.broadcasted_iota(jnp.int32, (BLOCK_TOKENS, ROWS), 0)
    query = lax.broadcasted_iota(jnp.int32, (BLOCK_TOKENS, ROWS), 1)
    return token <= (query & (BLOCK_TOKENS - 1))


def block_valid(info_ref, plane, turn):
    row = info_ref[2]
    other = (row + turn) & (SIDE - 1)
    offset = SIDE * plane + row - other
    return (offset >= 0) & (info_ref[0] - offset >= info_ref[1])


def stats_kernel(turn, info_ref, q_ref, g_ref, kv_ref, *rest):
    if turn == 0:
        out_ref, qs_ref, gs_ref = rest
        out_ref[0:1, :] = jnp.full((1, ROWS), NEGATIVE, jnp.float32)
        out_ref[1:, :] = jnp.zeros((7, ROWS), jnp.float32)
    else:
        in_ref, out_ref, qs_ref, gs_ref = rest
        out_ref[...] = in_ref[...]
    stack_heads(q_ref, qs_ref)
    stack_heads(g_ref, gs_ref)
    for plane in range(PLANES):

        @pl.when(block_valid(info_ref, plane, turn))
        def _():
            score = lax.dot_general(
                kv_ref[plane, :, :HEAD_SIZE], qs_ref[...], NT, preferred_element_type=jnp.float32
            )
            if turn == 0 and plane == 0:
                score = jnp.where(causal_mask(), score, NEGATIVE)
            dprob = lax.dot_general(
                kv_ref[plane, :, HEAD_SIZE:], gs_ref[...], NT, preferred_element_type=jnp.float32
            )
            old = out_ref[0:1, :]
            top = jnp.maximum(old, jnp.max(score, axis=0, keepdims=True))
            weight = jnp.exp2((score - top) * EXP_SCALE)
            keep = jnp.exp2((old - top) * EXP_SCALE)
            out_ref[0:1, :] = top
            out_ref[1:2, :] = out_ref[1:2, :] * keep + jnp.sum(weight, axis=0, keepdims=True)
            out_ref[2:3, :] = out_ref[2:3, :] * keep + jnp.sum(
                weight * dprob, axis=0, keepdims=True
            )


def grads_kernel(turn, info_ref, q_ref, g_ref, kv_ref, stats_ref, out_ref, qs_ref, gs_ref):
    stack_heads(q_ref, qs_ref)
    stack_heads(g_ref, gs_ref)
    total = stats_ref[1:2, :]
    lse = stats_ref[0:1, :] * EXP_SCALE + jnp.log2(total)
    delta = stats_ref[2:3, :] / total
    for plane in range(PLANES):
        valid = block_valid(info_ref, plane, turn)

        @pl.when(valid)
        def _():
            score = lax.dot_general(
                kv_ref[plane, :, :HEAD_SIZE], qs_ref[...], NT, preferred_element_type=jnp.float32
            )
            dprob = lax.dot_general(
                kv_ref[plane, :, HEAD_SIZE:], gs_ref[...], NT, preferred_element_type=jnp.float32
            )
            prob = jnp.exp2(score * EXP_SCALE - lse)
            if turn == 0 and plane == 0:
                prob = jnp.where(causal_mask(), prob, 0.0)
            dscore = (prob * (dprob - delta)).astype(jnp.bfloat16)
            key_part = lax.dot_general(
                dscore, qs_ref[...], NN, preferred_element_type=jnp.float32
            )
            value_part = lax.dot_general(
                prob.astype(jnp.bfloat16), gs_ref[...], NN, preferred_element_type=jnp.float32
            )
            out_ref[plane, :, :HEAD_SIZE] = (key_part * SCALE).astype(out_ref.dtype)
            out_ref[plane, :, HEAD_SIZE:] = value_part.astype(out_ref.dtype)

        @pl.when(jnp.logical_not(valid))
        def _():
            out_ref[plane] = jnp.zeros(out_ref.shape[1:], out_ref.dtype)


SMEM_SPEC = pl.BlockSpec(memory_space=pltpu.SMEM)
VMEM_SPEC = pl.BlockSpec(memory_space=pltpu.VMEM)
STACKS = [
    pltpu.VMEM((ROWS, HEAD_SIZE), jnp.bfloat16),
    pltpu.VMEM((ROWS, HEAD_SIZE), jnp.bfloat16),
]
PARAMS = pltpu.CompilerParams(vmem_limit_bytes=48 * 1024 * 1024)


def stats_pass(turn, info, q, g, kv, stats):
    extra = [] if turn == 0 else [stats]
    return pl.pallas_call(
        functools.partial(stats_kernel, turn),
        out_shape=jax.ShapeDtypeStruct((8, ROWS), jnp.float32),
        in_specs=[SMEM_SPEC] + [VMEM_SPEC] * (3 + len(extra)),
        out_specs=VMEM_SPEC,
        scratch_shapes=STACKS,
        compiler_params=PARAMS,
        name=f"stats{turn}",
    )(info, q, g, kv, *extra)


def grads_pass(turn, info, q, g, kv, stats):
    return pl.pallas_call(
        functools.partial(grads_kernel, turn),
        out_shape=jax.ShapeDtypeStruct((PLANES, BLOCK_TOKENS, 2 * HEAD_SIZE), jnp.bfloat16),
        in_specs=[SMEM_SPEC] + [VMEM_SPEC] * 4,
        out_specs=VMEM_SPEC,
        scratch_shapes=STACKS,
        compiler_params=PARAMS,
        name=f"grads{turn}",
    )(info, q, g, kv, stats)


def pick_kernel(pick_ref, src_ref, out_ref):
    out_ref[0] = src_ref[...]


def pick_features(hidden, head):
    pick = jnp.stack([2 * (head % 2), head // 2]).astype(jnp.int32)
    spec = pltpu.PrefetchScalarGridSpec(
        num_scalar_prefetch=1,
        grid=(SIDE, 2),
        in_specs=[
            pl.BlockSpec(
                (BLOCK_TOKENS, 128),
                lambda lo, half, pick: (0, (pick[0] + half) * 16 + lo * 4 + pick[1]),
            )
        ],
        out_specs=pl.BlockSpec((1, BLOCK_TOKENS, 128), lambda lo, half, pick: (lo, 0, half)),
    )
    return pl.pallas_call(
        pick_kernel,
        out_shape=jax.ShapeDtypeStruct((SIDE, BLOCK_TOKENS, 256), hidden.dtype),
        grid_spec=spec,
        name="pick",
    )(pick, hidden)


def rotary_tables(positions):
    half = HEAD_SIZE // 2
    freqs = 500000.0 ** (-(jnp.arange(half, dtype=jnp.float32) * 2.0) / HEAD_SIZE)
    angles = positions.astype(jnp.float32)[:, None] * freqs[None, :]
    cosine, sine = jnp.cos(angles), jnp.sin(angles)
    return jnp.concatenate([cosine, cosine], -1), jnp.concatenate([sine, sine], -1)


def exchange(value, axis):
    return lax.all_to_all(value, axis, split_axis=0, concat_axis=0, tiled=True)


def small_sum(value, axis):
    count = axis_total(axis)
    spread = jnp.broadcast_to(value, (count, 8, 128))
    return jnp.sum(exchange(spread, axis), axis=0)[0:1, 0:1]


def per_device(hidden, queries, keys, values, output_gradient, doc_blocks):
    z = lax.axis_index(Z)
    row = lax.axis_index("y")
    head = lax.axis_index("head")
    here = SIDE * z + row
    ends = jnp.cumsum(doc_blocks)
    first = jnp.max(jnp.where(ends <= here, ends, 0))
    info = jnp.stack([here, first, row]).astype(jnp.int32)
    f32 = jnp.float32

    own = jnp.concatenate([keys, values], axis=1)[None]
    four = rotate(own, Z, 4)
    even = jnp.concatenate([own, four])
    two = rotate(even, Z, 2)
    odd = rotate(jnp.concatenate([own, two[0:1], four]), Z, 1)
    column = jnp.concatenate([own, odd[0:1], two[0:1], odd[1:2], four, odd[2:3], two[1:2]])

    columns = [column] + [rotate(column, "y", -turn) for turn in (1, 2, 3)]

    picked = pick_features(hidden, head)
    picked, _ = lax.optimization_barrier((picked, odd))
    tokens = exchange(picked, "z_lo")
    features = lax.all_gather(tokens.reshape(SIDE * BLOCK_TOKENS, 256), "head", axis=0)

    stats = None
    for turn in range(4):
        stats = stats_pass(turn, info, queries, output_gradient, columns[turn], stats)
    summed = None
    parts = {}
    for turn in (1, 2, 3, 0):
        part = grads_pass(turn, info, queries, output_gradient, columns[turn], stats)
        parts[turn] = rotate(part, "y", turn) if turn else part
    summed = sum(parts[turn].astype(f32) for turn in (0, 1, 2, 3))

    odd_back = rotate(
        jnp.concatenate([summed[1:2], summed[3:4], summed[5:6]]).astype(jnp.bfloat16), Z, -1
    ).astype(f32)
    s0 = summed[0] + odd_back[0]
    s2 = summed[2] + odd_back[1]
    s4 = summed[4] + odd_back[2]
    two_back = rotate(jnp.stack([s2, summed[6]]).astype(jnp.bfloat16), Z, -2).astype(f32)
    s0 = s0 + two_back[0]
    s4 = s4 + two_back[1]
    four_back = rotate(s4.astype(jnp.bfloat16), Z, -4).astype(f32)
    s0 = s0 + four_back

    cosine, sine = rotary_tables(here * BLOCK_TOKENS + jnp.arange(BLOCK_TOKENS))
    key_grad = s0[:, :HEAD_SIZE]
    half = HEAD_SIZE // 2
    turned = jnp.concatenate([-key_grad[:, half:], key_grad[:, :half]], axis=-1)
    pre = jnp.concatenate([key_grad * cosine - turned * sine, s0[:, HEAD_SIZE:]], axis=1)
    pre = pre.astype(jnp.bfloat16)
    gathered = exchange(jnp.broadcast_to(pre, (SIDE,) + pre.shape), "z_lo")
    gathered = gathered.reshape(SIDE * BLOCK_TOKENS, 2 * HEAD_SIZE)

    weight = lax.dot_general(
        features, gathered, (((1,), (0,)), ((), ())), preferred_element_type=f32
    ).astype(jnp.bfloat16)
    weight = exchange(weight.reshape(SIDE, SIDE * BLOCK_TOKENS, 256), "y")
    weight = jnp.sum(weight.astype(f32), axis=0).astype(jnp.bfloat16)
    weight = exchange(weight.reshape(SIDE, BLOCK_TOKENS, 256), "z_hi")
    weight = jnp.sum(weight.astype(f32), axis=0)

    squares = jnp.sum(weight * weight).reshape(1, 1)
    squares = lax.psum(squares, "z_lo")
    squares = lax.psum(squares, "z_hi")
    squares = small_sum(squares, "y")
    squares = small_sum(squares, "head")
    mean_square = squares / (2.0 * MODEL_WIDTH * KEY_VALUE_HEADS * HEAD_SIZE)
    factor = 1.0 / jnp.sqrt(mean_square + 1e-06)
    scaled = weight * factor
    return (scaled[:, :HEAD_SIZE], scaled[:, HEAD_SIZE:])


def solution(mesh):
    devices = mesh.devices.reshape(4, 4, 4, 8)
    split = Mesh(devices, ("z_hi", "z_lo", "y", "head"))
    placed = (P(CTX, None),) + (P(CTX, "head"),) * 4 + (P(),)
    return jax.shard_map(
        per_device,
        mesh=split,
        in_specs=placed,
        out_specs=(P(CTX, "head"), P(CTX, "head")),
        check_vma=False,
    )
```

time: 1270 us -> 262 us (0.21)
  waiting for transfers between devices: 526 us -> 51.3 us
  starting transfers between devices: 358 us -> 64.6 us
  matrix products: 76.2 us -> 2.35 us
  other arithmetic: 62.9 us -> 6.02 us
  local copies, waits for them, and re-layouts: 59.3 us -> 3.78 us
  loops' own time: 52.2 us -> 0 us
    all_gather x2 -> x1, waiting for transfers between devices: 366 us -> 0.01 us  [per_device(): lax.all_gather(tokens.reshape(SIDE * BLOCK_TOKENS, 256), 'head', axis=0)]
    ppermute x96 -> x12, starting transfers between devices: 339 us -> 61.1 us  [rotate(): lax.ppermute(value, axis, [(at, (at + steps) % count) for at in range(cou...]
    ppermute x96 -> x12, waiting for transfers between devices: 160 us -> 51.3 us  [rotate(): lax.ppermute(value, axis, [(at, (at + steps) % count) for at in range(cou...]
    psum x1 -> x2, blocking collectives: 109 us -> 24.3 us  [the longest x1 12.5 us: per_device(): squares = lax.psum(squares, 'z_hi')]
    all_to_all x0 -> x5, blocking collectives: none -> 81.1 us  [exchange(): return lax.all_to_all(value, axis, split_axis=0, concat_axis=0, tiled=True)]
    dot_general x127 -> x1, matrix products: 76.2 us -> 2.35 us  [per_device(): lax.dot_general(features, gathered, (((1,), (0,)), ((), ())), preferred_e...]
    another operation x5 -> x0, loops' own time: 52.2 us -> none  [the longest x1 17.9 us: per_device(): lax.scan(gradient_pass, 0, (key_stack, value_stack, offsets))]
    dynamic_slice x75 -> x0, local copies, waits for them, and re-layouts: 45.5 us -> none  [per_device(): lax.scan(softmax_stats, (start_top, start_total), (key_stack, offsets))]
  transfers between devices with their start and end apart: 99 -> 14, of which waited for: 74 -> 10; matrix products, arithmetic and copies ran while one was open for 15% -> 2% of each run, Pallas kernels for 0% -> 5%
where the time goes in v1:
time: 262 us; the launch traced here: 261 us
  blocking collectives  105 us (40%)
  starting transfers between devices  64.6 us (25%)
  waiting for transfers between devices  51.3 us (20%)
  between operations  15.2 us (6%)
  Pallas kernels  11.9 us (5%)
  other arithmetic  6.02 us (2%)
  local copies, waits for them, and re-layouts  3.78 us (1%)
    all_to_all x5, blocking collectives, exchange(): return lax.all_to_all(value, axis, split_axis=0, concat_axis=0, tiled=True)  81.1 us
    ppermute x12, starting transfers between devices, rotate(): lax.ppermute(value, axis, [(at, (at + steps) % count) for at in range(cou...  61.1 us
    ppermute x12, waiting for transfers between devices, rotate(): lax.ppermute(value, axis, [(at, (at + steps) % count) for at in range(cou...  51.3 us
    psum x1, blocking collectives, per_device(): squares = lax.psum(squares, 'z_hi')  12.5 us
    psum x1, blocking collectives, per_device(): squares = lax.psum(squares, 'z_lo')  11.7 us
  transfers between devices with their start and end apart: 14, of which 10 were waited for; matrix products, arithmetic and copies ran while one was open for 2% of the time, Pallas kernels for 5%

profile of v1, /device:TPU:1, one launch (start us, length us, event | category | flops | bytes accessed | tf_op | source)
XLA Modules:
  0.0 260.5 jit_solution(10676332623046605779)
XLA Ops:
  7.2 0.8 maximum_bitcast_fusion
  8.0 9.6 %collective-permute-start = (bf16[1,128,256]{2,1,0:T(8,128)(2,1)S(1)}, bf16[1,128,256]{2,1,0:T(8,128)(2,1)S(1)}, u32[]{:S(2)}, u32[]{:S(2)}) collective-permute-start(bf16[1,128,256]{2,1,0:T(8,128)(2,1)S(1)} %maximum_bitcast_fusion), channel_id=1, source_target_pairs={{0,128},{32,160},{64,192},{96,224},{128,256},{160,288},{192,320},{... | collective-permute-start | bytes 196616 | tf_op jit(solution)/shard_map/ppermute | solution.py:41
  17.7 5.6 %collective-permute-done = bf16[1,128,256]{2,1,0:T(8,128)(2,1)S(1)} collective-permute-done((bf16[1,128,256]{2,1,0:T(8,128)(2,1)S(1)}, bf16[1,128,256]{2,1,0:T(8,128)(2,1)S(1)}, u32[]{:S(2)}, u32[]{:S(2)}) %collective-permute-start) | collective-permute-done | bytes 65568 | tf_op jit(solution)/shard_map/ppermute | solution.py:41
  23.3 6.1 %collective-permute-start.1 = (bf16[2,128,256]{2,1,0:T(8,128)(2,1)S(1)}, bf16[2,128,256]{2,1,0:T(8,128)(2,1)S(1)}, u32[]{:S(2)}, u32[]{:S(2)}) collective-permute-start(bf16[2,128,256]{2,1,0:T(8,128)(2,1)S(1)} %pad_maximum_fusion.2), channel_id=1, source_target_pairs={{0,64},{32,96},{64,128},{96,160},{128,192},{160,224},{192,256},{22... | collective-permute-start | bytes 393224 | tf_op jit(solution)/shard_map/ppermute | solution.py:41
  29.4 5.5 %collective-permute-done.1 = bf16[2,128,256]{2,1,0:T(8,128)(2,1)S(1)} collective-permute-done((bf16[2,128,256]{2,1,0:T(8,128)(2,1)S(1)}, bf16[2,128,256]{2,1,0:T(8,128)(2,1)S(1)}, u32[]{:S(2)}, u32[]{:S(2)}) %collective-permute-start.1) | collective-permute-done | bytes 131104 | tf_op jit(solution)/shard_map/ppermute | solution.py:41
  35.0 6.2 %collective-permute-start.2 = (bf16[3,128,256]{2,1,0:T(8,128)(2,1)S(1)}, bf16[3,128,256]{2,1,0:T(8,128)(2,1)S(1)}, u32[]{:S(2)}, u32[]{:S(2)}) collective-permute-start(bf16[3,128,256]{2,1,0:T(8,128)(2,1)S(1)} %pad_maximum_fusion), channel_id=1, source_target_pairs={{0,32},{32,64},{64,96},{96,128},{128,160},{160,192},{192,224},{224... | collective-permute-start | bytes 589832 | tf_op jit(solution)/shard_map/ppermute | solution.py:41
  41.7 5.0 %pick.1 = bf16[4,128,256]{2,1,0:T(8,128)(2,1)} custom-call(s32[2]{0:T(128)} %pad_add_fusion.pick_ref, bf16[128,8192]{1,0:T(8,128)(2,1)} %src_ref.1), custom_call_target="tpu_custom_call" | custom-call | tf_op jit(solution)/shard_map/pick/pallas_call | solution.py:183
  46.8 3.4 %all-to-all-start = ((bf16[4,128,256]{2,1,0:T(8,128)(2,1)}), bf16[4,128,256]{2,1,0:T(8,128)(2,1)S(1)}, u32[]{:S(2)}, u32[]{:S(2)}) async-start(bf16[4,128,256]{2,1,0:T(8,128)(2,1)} %pick.1), calls=%async_computation | async-start | bytes 524288 | tf_op jit(solution)/shard_map/all_to_all | solution.py:200
  50.3 4.6 %collective-permute-start.5 = (bf16[7,128,256]{2,1,0:T(8,128)(2,1)S(1)}, bf16[7,128,256]{2,1,0:T(8,128)(2,1)S(1)}, u32[]{:S(2)}, u32[]{:S(2)}) collective-permute-start(bf16[7,128,256]{2,1,0:T(8,128)(2,1)S(1)} %slice_dynamic-update-slice_fusion.kv_ref), channel_id=1, source_target_pairs={{0,24},{8,0},{16,8},{24,16},{1,25},{9,1},{17,9},{25,17},{2,26},{10... | collective-permute-start | bytes 1376264 | tf_op jit(solution)/shard_map/ppermute | solution.py:41
  55.0 2.3 collective-permute-start.4
  57.2 2.6 collective-permute-start.3
  60.6 0.6 pad_add_fusion.1.info_ref
  61.3 1.1 stats0.1.rest_0_
  62.4 1.2 collective-permute-done.5.kv_ref
  63.6 0.7 stats1.1.rest_0_
  64.3 3.6 %collective-permute-done.4.kv_ref = bf16[7,128,256]{2,1,0:T(8,128)(2,1)S(1)} collective-permute-done((bf16[7,128,256]{2,1,0:T(8,128)(2,1)S(1)}, bf16[7,128,256]{2,1,0:T(8,128)(2,1)S(1)}, u32[]{:S(2)}, u32[]{:S(2)}) %collective-permute-start.4) | collective-permute-done | bytes 458784 | tf_op jit(solution)/shard_map/ppermute | solution.py:41
  67.9 0.7 stats2.1.rest_0_
  68.6 12.0 %collective-permute-done.3.kv_ref = bf16[7,128,256]{2,1,0:T(8,128)(2,1)S(1)} collective-permute-done((bf16[7,128,256]{2,1,0:T(8,128)(2,1)S(1)}, bf16[7,128,256]{2,1,0:T(8,128)(2,1)S(1)}, u32[]{:S(2)}, u32[]{:S(2)}) %collective-permute-start.3) | collective-permute-done | bytes 458784 | tf_op jit(solution)/shard_map/ppermute | solution.py:41
  80.6 0.7 stats3.1.stats_ref
  81.3 0.9 grads1.1
  82.3 1.9 collective-permute-start.6
  84.2 0.7 grads2.1
  84.9 3.7 %collective-permute-start.7 = (bf16[7,128,256]{2,1,0:T(8,128)(2,1)S(1)}, bf16[7,128,256]{2,1,0:T(8,128)(2,1)}, u32[]{:S(2)}, u32[]{:S(2)}) collective-permute-start(bf16[7,128,256]{2,1,0:T(8,128)(2,1)S(1)} %grads2.1), channel_id=1, source_target_pairs={{0,16},{8,24},{16,0},{24,8},{1,17},{9,25},{17,1},{25,9},{2,18},{10... | collective-permute-start | bytes 1376264 | tf_op jit(solution)/shard_map/ppermute | solution.py:41
  88.7 0.7 grads3.1
  89.4 3.8 %collective-permute-start.8 = (bf16[7,128,256]{2,1,0:T(8,128)(2,1)S(1)}, bf16[7,128,256]{2,1,0:T(8,128)(2,1)}, u32[]{:S(2)}, u32[]{:S(2)}) collective-permute-start(bf16[7,128,256]{2,1,0:T(8,128)(2,1)S(1)} %grads3.1), channel_id=1, source_target_pairs={{0,24},{8,0},{16,8},{24,16},{1,25},{9,1},{17,9},{25,17},{2,26},{10... | collective-permute-start | bytes 1376264 | tf_op jit(solution)/shard_map/ppermute | solution.py:41
  93.3 0.7 copy-done.2
  94.0 1.3 grads0.1
  95.3 11.6 %collective-permute-done.6 = bf16[7,128,256]{2,1,0:T(8,128)(2,1)} collective-permute-done((bf16[7,128,256]{2,1,0:T(8,128)(2,1)S(1)}, bf16[7,128,256]{2,1,0:T(8,128)(2,1)}, u32[]{:S(2)}, u32[]{:S(2)}) %collective-permute-start.6) | collective-permute-done | bytes 458784 | tf_op jit(solution)/shard_map/ppermute | solution.py:41
  106.9 3.5 %collective-permute-done.8 = bf16[7,128,256]{2,1,0:T(8,128)(2,1)} collective-permute-done((bf16[7,128,256]{2,1,0:T(8,128)(2,1)S(1)}, bf16[7,128,256]{2,1,0:T(8,128)(2,1)}, u32[]{:S(2)}, u32[]{:S(2)}) %collective-permute-start.8) | collective-permute-done | bytes 458784 | tf_op jit(solution)/shard_map/ppermute | solution.py:41
  110.4 1.5 fusion.8
  112.0 5.7 %collective-permute-start.9 = (bf16[3,128,256]{2,1,0:T(8,128)(2,1)S(1)}, bf16[3,128,256]{2,1,0:T(8,128)(2,1)S(1)}, u32[]{:S(2)}, u32[]{:S(2)}) collective-permute-start(bf16[3,128,256]{2,1,0:T(8,128)(2,1)S(1)} %pad_maximum_fusion.1), channel_id=1, source_target_pairs={{0,480},{32,0},{64,32},{96,64},{128,96},{160,128},{192,160},{224,1... | collective-permute-start | bytes 589832 | tf_op jit(solution)/shard_map/ppermute | solution.py:41
  117.7 2.6 collective-permute-done.9
  120.4 8.1 %collective-permute-start.10 = (bf16[2,128,256]{2,1,0:T(8,128)(2,1)S(1)}, bf16[2,128,256]{2,1,0:T(8,128)(2,1)S(1)}, u32[]{:S(2)}, u32[]{:S(2)}) collective-permute-start(bf16[2,128,256]{2,1,0:T(8,128)(2,1)S(1)} %pad_maximum_fusion.3), channel_id=1, source_target_pairs={{0,448},{32,480},{64,0},{96,32},{128,64},{160,96},{192,128},{224,1... | collective-permute-start | bytes 393224 | tf_op jit(solution)/shard_map/ppermute | solution.py:41
  128.5 2.6 collective-permute-done.10
  131.1 6.4 %collective-permute-start.11 = (bf16[128,256]{1,0:T(8,128)(2,1)S(1)}, bf16[128,256]{1,0:T(8,128)(2,1)S(1)}, u32[]{:S(2)}, u32[]{:S(2)}) collective-permute-start(bf16[128,256]{1,0:T(8,128)(2,1)S(1)} %fusion.4), channel_id=1, source_target_pairs={{0,384},{32,416},{64,448},{96,480},{128,0},{160,32},{192,64},{224,... | collective-permute-start | bytes 196616 | tf_op jit(solution)/shard_map/ppermute | solution.py:41
  137.9 3.1 %collective-permute-done.11 = bf16[128,256]{1,0:T(8,128)(2,1)S(1)} collective-permute-done((bf16[128,256]{1,0:T(8,128)(2,1)S(1)}, bf16[128,256]{1,0:T(8,128)(2,1)S(1)}, u32[]{:S(2)}, u32[]{:S(2)}) %collective-permute-start.11) | collective-permute-done | bytes 65568 | tf_op jit(solution)/shard_map/ppermute | solution.py:41
  141.3 9.5 %all_to_all.30 = bf16[4,128,256]{2,1,0:T(8,128)(2,1)S(1)} all-to-all(bf16[4,128,256]{2,1,0:T(8,128)(2,1)S(1)} %broadcast_in_dim.24), channel_id=1, replica_groups=mesh['z_hi'=4,'z_lo'=4,'y'=4,'head'=8] {'z_lo'}, dimensions={0} | all-to-all | bytes 524288 | tf_op jit(solution)/shard_map/all_to_all | solution.py:200
  150.8 2.3 convolution_convert_fusion
  153.1 16.3 %all_to_all.31 = bf16[4,512,256]{2,1,0:T(8,128)(2,1)S(1)} all-to-all(bf16[4,512,256]{2,1,0:T(8,128)(2,1)S(1)} %bitcast.31), channel_id=1, replica_groups=mesh['z_hi'=4,'z_lo'=4,'y'=4,'head'=8] {'y'}, dimensions={0} | all-to-all | bytes 2097152 | tf_op jit(solution)/shard_map/all_to_all | solution.py:200
  169.7 33.4 %all_to_all.32 = bf16[4,128,256]{2,1,0:T(8,128)(2,1)S(1)} all-to-all(bf16[4,128,256]{2,1,0:T(8,128)(2,1)S(1)} %bitcast.30), channel_id=1, replica_groups=mesh['z_hi'=4,'z_lo'=4,'y'=4,'head'=8] {'z_hi'}, dimensions={0} | all-to-all | bytes 524288 | tf_op jit(solution)/shard_map/all_to_all | solution.py:200
  203.1 0.6 multiply_reduce_fusion
  203.7 11.7 %psum.16 = f32[1,1]{1,0:T(1,128)} all-reduce(f32[1,1]{1,0:T(1,128)} %bitcast.15), channel_id=1, replica_groups=mesh['z_hi'=4,'z_lo'=4,'y'=4,'head'=8] {'z_lo'}, use_global_device_ids=true, to_apply=%region_5.6 | all-reduce | flops 1 | bytes 8 | tf_op jit(solution)/shard_map/psum | solution.py:273
  215.4 12.5 %psum.18 = f32[]{:T(128)} all-reduce(f32[]{:T(128)} %bitcast.16), channel_id=1, replica_groups=mesh['z_hi'=4,'z_lo'=4,'y'=4,'head'=8] {'z_hi'}, use_global_device_ids=true, to_apply=%region_6.7 | all-reduce | flops 1 | bytes 8 | tf_op jit(solution)/shard_map/psum | solution.py:274
  228.0 0.6 broadcast_in_dim.25
  228.6 6.6 %all_to_all.33 = f32[4,8,128]{2,1,0:T(8,128)S(1)} all-to-all(f32[4,8,128]{2,1,0:T(8,128)S(1)} %broadcast_in_dim.25), channel_id=1, replica_groups=mesh['z_hi'=4,'z_lo'=4,'y'=4,'head'=8] {'y'}, dimensions={0} | all-to-all | bytes 32768 | tf_op jit(solution)/shard_map/all_to_all | solution.py:200
  235.8 0.6 broadcast_in_dim.26
  236.4 15.4 %all_to_all.34 = f32[8,8,128]{2,1,0:T(8,128)S(1)} all-to-all(f32[8,8,128]{2,1,0:T(8,128)S(1)} %broadcast_in_dim.26), channel_id=1, replica_groups=mesh['z_hi'=4,'z_lo'=4,'y'=4,'head'=8] {'head'}, dimensions={0} | all-to-all | bytes 65536 | tf_op jit(solution)/shard_map/all_to_all | solution.py:200
  253.0 0.7 fusion.10
  (53 shorter events, 3.6 us)
Async XLA Ops:
  7.2 39.6 %copy-start.4 = (bf16[128,128]{1,0:T(8,128)(2,1)S(1)}, bf16[128,128]{1,0:T(8,128)(2,1)}, u32[]{:S(2)}) copy-start(bf16[128,128]{1,0:T(8,128)(2,1)} %param.8) | copy-start | bytes 98308
  7.2 39.6 %copy-start.3 = (bf16[128,128]{1,0:T(8,128)(2,1)S(1)}, bf16[128,128]{1,0:T(8,128)(2,1)}, u32[]{:S(2)}) copy-start(bf16[128,128]{1,0:T(8,128)(2,1)} %param.9) | copy-start | bytes 98308
  8.0 15.2 %collective-permute-start = (bf16[1,128,256]{2,1,0:T(8,128)(2,1)S(1)}, bf16[1,128,256]{2,1,0:T(8,128)(2,1)S(1)}, u32[]{:S(2)}, u32[]{:S(2)}) collective-permute-start(bf16[1,128,256]{2,1,0:T(8,128)(2,1)S(1)} %maximum_bitcast_fusion), channel_id=1, source_target_pairs={{0,128},{32,160},{64,192},{96,224},{128,256},{160,288},{192,320},{... | collective-permute-start | bytes 196616 | tf_op jit(solution)/shard_map/ppermute | solution.py:41
  23.3 11.7 %collective-permute-start.1 = (bf16[2,128,256]{2,1,0:T(8,128)(2,1)S(1)}, bf16[2,128,256]{2,1,0:T(8,128)(2,1)S(1)}, u32[]{:S(2)}, u32[]{:S(2)}) collective-permute-start(bf16[2,128,256]{2,1,0:T(8,128)(2,1)S(1)} %pad_maximum_fusion.2), channel_id=1, source_target_pairs={{0,64},{32,96},{64,128},{96,160},{128,192},{160,224},{192,256},{22... | collective-permute-start | bytes 393224 | tf_op jit(solution)/shard_map/ppermute | solution.py:41
  34.9 24.9 %copy-start.5 = (s32[5]{0:T(128)S(1)}, s32[5]{0:T(128)}, u32[]{:S(2)}) copy-start(s32[5]{0:T(128)} %param.11) | copy-start | bytes 64
  35.0 26.3 %copy-start = (bf16[128,1024]{1,0:T(8,128)(2,1)S(1)}, bf16[128,1024]{1,0:T(8,128)(2,1)}, u32[]{:S(2)}) copy-start(bf16[128,1024]{1,0:T(8,128)(2,1)} %q_ref.15) | copy-start | bytes 786436
  35.0 26.3 %copy-start.1 = (bf16[128,1024]{1,0:T(8,128)(2,1)S(1)}, bf16[128,1024]{1,0:T(8,128)(2,1)}, u32[]{:S(2)}) copy-start(bf16[128,1024]{1,0:T(8,128)(2,1)} %g_ref.15) | copy-start | bytes 786436
  35.0 11.7 %collective-permute-start.2 = (bf16[3,128,256]{2,1,0:T(8,128)(2,1)S(1)}, bf16[3,128,256]{2,1,0:T(8,128)(2,1)S(1)}, u32[]{:S(2)}, u32[]{:S(2)}) collective-permute-start(bf16[3,128,256]{2,1,0:T(8,128)(2,1)S(1)} %pad_maximum_fusion), channel_id=1, source_target_pairs={{0,32},{32,64},{64,96},{96,128},{128,160},{160,192},{192,224},{224... | collective-permute-start | bytes 589832 | tf_op jit(solution)/shard_map/ppermute | solution.py:41
  46.8 46.5 %all-to-all-start = ((bf16[4,128,256]{2,1,0:T(8,128)(2,1)}), bf16[4,128,256]{2,1,0:T(8,128)(2,1)S(1)}, u32[]{:S(2)}, u32[]{:S(2)}) async-start(bf16[4,128,256]{2,1,0:T(8,128)(2,1)} %pick.1), calls=%async_computation | async-start | bytes 524288 | tf_op jit(solution)/shard_map/all_to_all | solution.py:200
  50.2 100.6 %all-gather.2.cloned.1.call-start = ((), (), s32[]{:S(2)}) async-start(), calls=%async_computation.6 | async-start | bytes 2359296 | tf_op jit(solution)/shard_map/all_gather | solution.py:231
  50.3 13.3 %collective-permute-start.5 = (bf16[7,128,256]{2,1,0:T(8,128)(2,1)S(1)}, bf16[7,128,256]{2,1,0:T(8,128)(2,1)S(1)}, u32[]{:S(2)}, u32[]{:S(2)}) collective-permute-start(bf16[7,128,256]{2,1,0:T(8,128)(2,1)S(1)} %slice_dynamic-update-slice_fusion.kv_ref), channel_id=1, source_target_pairs={{0,24},{8,0},{16,8},{24,16},{1,25},{9,1},{17,9},{25,17},{2,26},{10... | collective-permute-start | bytes 1376264 | tf_op jit(solution)/shard_map/ppermute | solution.py:41
  55.0 12.9 %collective-permute-start.4 = (bf16[7,128,256]{2,1,0:T(8,128)(2,1)S(1)}, bf16[7,128,256]{2,1,0:T(8,128)(2,1)S(1)}, u32[]{:S(2)}, u32[]{:S(2)}) collective-permute-start(bf16[7,128,256]{2,1,0:T(8,128)(2,1)S(1)} %slice_dynamic-update-slice_fusion.kv_ref), channel_id=1, source_target_pairs={{0,16},{8,24},{16,0},{24,8},{1,17},{9,25},{17,1},{25,9},{2,18},{10... | collective-permute-start | bytes 1376264 | tf_op jit(solution)/shard_map/ppermute | solution.py:41
  57.2 23.4 %collective-permute-start.3 = (bf16[7,128,256]{2,1,0:T(8,128)(2,1)S(1)}, bf16[7,128,256]{2,1,0:T(8,128)(2,1)S(1)}, u32[]{:S(2)}, u32[]{:S(2)}) collective-permute-start(bf16[7,128,256]{2,1,0:T(8,128)(2,1)S(1)} %slice_dynamic-update-slice_fusion.kv_ref), channel_id=1, source_target_pairs={{0,8},{8,16},{16,24},{24,0},{1,9},{9,17},{17,25},{25,1},{2,10},{10... | collective-permute-start | bytes 1376264 | tf_op jit(solution)/shard_map/ppermute | solution.py:41
  82.3 24.6 %collective-permute-start.6 = (bf16[7,128,256]{2,1,0:T(8,128)(2,1)S(1)}, bf16[7,128,256]{2,1,0:T(8,128)(2,1)}, u32[]{:S(2)}, u32[]{:S(2)}) collective-permute-start(bf16[7,128,256]{2,1,0:T(8,128)(2,1)S(1)} %grads1.1), channel_id=1, source_target_pairs={{0,8},{8,16},{16,24},{24,0},{1,9},{9,17},{17,25},{25,1},{2,10},{10... | collective-permute-start | bytes 1376264 | tf_op jit(solution)/shard_map/ppermute | solution.py:41
  84.9 22.0 %collective-permute-start.7 = (bf16[7,128,256]{2,1,0:T(8,128)(2,1)S(1)}, bf16[7,128,256]{2,1,0:T(8,128)(2,1)}, u32[]{:S(2)}, u32[]{:S(2)}) collective-permute-start(bf16[7,128,256]{2,1,0:T(8,128)(2,1)S(1)} %grads2.1), channel_id=1, source_target_pairs={{0,16},{8,24},{16,0},{24,8},{1,17},{9,25},{17,1},{25,9},{2,18},{10... | collective-permute-start | bytes 1376264 | tf_op jit(solution)/shard_map/ppermute | solution.py:41
  89.4 21.0 %collective-permute-start.8 = (bf16[7,128,256]{2,1,0:T(8,128)(2,1)S(1)}, bf16[7,128,256]{2,1,0:T(8,128)(2,1)}, u32[]{:S(2)}, u32[]{:S(2)}) collective-permute-start(bf16[7,128,256]{2,1,0:T(8,128)(2,1)S(1)} %grads3.1), channel_id=1, source_target_pairs={{0,24},{8,0},{16,8},{24,16},{1,25},{9,1},{17,9},{25,17},{2,26},{10... | collective-permute-start | bytes 1376264 | tf_op jit(solution)/shard_map/ppermute | solution.py:41
  93.2 0.7 copy-start.2
  112.0 8.3 %collective-permute-start.9 = (bf16[3,128,256]{2,1,0:T(8,128)(2,1)S(1)}, bf16[3,128,256]{2,1,0:T(8,128)(2,1)S(1)}, u32[]{:S(2)}, u32[]{:S(2)}) collective-permute-start(bf16[3,128,256]{2,1,0:T(8,128)(2,1)S(1)} %pad_maximum_fusion.1), channel_id=1, source_target_pairs={{0,480},{32,0},{64,32},{96,64},{128,96},{160,128},{192,160},{224,1... | collective-permute-start | bytes 589832 | tf_op jit(solution)/shard_map/ppermute | solution.py:41
  120.4 10.7 %collective-permute-start.10 = (bf16[2,128,256]{2,1,0:T(8,128)(2,1)S(1)}, bf16[2,128,256]{2,1,0:T(8,128)(2,1)S(1)}, u32[]{:S(2)}, u32[]{:S(2)}) collective-permute-start(bf16[2,128,256]{2,1,0:T(8,128)(2,1)S(1)} %pad_maximum_fusion.3), channel_id=1, source_target_pairs={{0,448},{32,480},{64,0},{96,32},{128,64},{160,96},{192,128},{224,1... | collective-permute-start | bytes 393224 | tf_op jit(solution)/shard_map/ppermute | solution.py:41
  131.1 9.8 %collective-permute-start.11 = (bf16[128,256]{1,0:T(8,128)(2,1)S(1)}, bf16[128,256]{1,0:T(8,128)(2,1)S(1)}, u32[]{:S(2)}, u32[]{:S(2)}) collective-permute-start(bf16[128,256]{1,0:T(8,128)(2,1)S(1)} %fusion.4), channel_id=1, source_target_pairs={{0,384},{32,416},{64,448},{96,480},{128,0},{160,32},{192,64},{224,... | collective-permute-start | bytes 196616 | tf_op jit(solution)/shard_map/ppermute | solution.py:41
Sparse Core Ops, SparseCore 0:
  94.1 36.2 all-gather.1

commit v2 on v1

v2 whole, which is shorter than its diff:
```python
import functools

import jax
import jax.numpy as jnp
from jax import lax
from jax.experimental import pallas as pl
from jax.experimental.pallas import tpu as pltpu
from jax.sharding import Mesh, PartitionSpec as P

MODEL_WIDTH = 8192
QUERY_HEADS = 64
KEY_VALUE_HEADS = 8
HEAD_SIZE = 128
BLOCK_TOKENS = 128
GROUP = QUERY_HEADS // KEY_VALUE_HEADS
ROWS = GROUP * BLOCK_TOKENS
PLANES = 7
SIDE = 4
STATS = 2
ODD = (1, 3, 5)
EVEN = (0, 2, 4, 6)
NEGATIVE = -1e30
SCALE = HEAD_SIZE ** (-0.5)
LOG2E = 1.4426950408889634
EXP_SCALE = SCALE * LOG2E
Z = ("z_hi", "z_lo")
CTX = ("z_hi", "z_lo", "y")

NT = (((1,), (1,)), ((), ()))
NN = (((1,), (0,)), ((), ()))
TN = (((0,), (0,)), ((), ()))


def axis_total(axis):
    names = axis if isinstance(axis, tuple) else (axis,)
    total = 1
    for name in names:
        total *= lax.axis_size(name)
    return total


def rotate(value, axis, steps):
    count = axis_total(axis)
    return lax.ppermute(value, axis, [(at, (at + steps) % count) for at in range(count)])


def stack_heads(src_ref, which, dst_ref):
    for head in range(GROUP):
        dst_ref[head * BLOCK_TOKENS:(head + 1) * BLOCK_TOKENS, :] = src_ref[
            0, which, :, head * HEAD_SIZE:(head + 1) * HEAD_SIZE
        ]


def causal_mask(offset):
    token = lax.broadcasted_iota(jnp.int32, (BLOCK_TOKENS, ROWS), 0)
    query = lax.broadcasted_iota(jnp.int32, (BLOCK_TOKENS, ROWS), 1)
    return token <= (query & (BLOCK_TOKENS - 1)) + BLOCK_TOKENS * offset


def block_offset(info_ref, plane, query_row):
    offset = SIDE * plane + query_row - info_ref[1]
    position = SIDE * info_ref[0] + query_row
    return offset, (offset >= 0) & (position - offset >= info_ref[2 + query_row])


def stats_kernel(info_ref, qg_ref, kv_ref, out_ref, qs_ref, gs_ref, run_ref):
    query_row = pl.program_id(0)
    run_ref[0:1, :] = jnp.full((1, ROWS), NEGATIVE, jnp.float32)
    run_ref[1:, :] = jnp.zeros((7, ROWS), jnp.float32)
    stack_heads(qg_ref, 0, qs_ref)
    stack_heads(qg_ref, 1, gs_ref)
    for plane in range(PLANES):
        offset, valid = block_offset(info_ref, plane, query_row)

        @pl.when(valid)
        def _():
            score = lax.dot_general(
                kv_ref[plane, :, :HEAD_SIZE], qs_ref[...], NT, preferred_element_type=jnp.float32
            )
            if plane == 0:
                score = jnp.where(causal_mask(offset), score, NEGATIVE)
            dprob = lax.dot_general(
                kv_ref[plane, :, HEAD_SIZE:], gs_ref[...], NT, preferred_element_type=jnp.float32
            )
            old = run_ref[0:1, :]
            top = jnp.maximum(old, jnp.max(score, axis=0, keepdims=True))
            weight = jnp.exp2((score - top) * EXP_SCALE)
            keep = jnp.exp2((old - top) * EXP_SCALE)
            run_ref[0:1, :] = top
            run_ref[1:2, :] = run_ref[1:2, :] * keep + jnp.sum(weight, axis=0, keepdims=True)
            run_ref[2:3, :] = run_ref[2:3, :] * keep + jnp.sum(
                weight * dprob, axis=0, keepdims=True
            )
    total = run_ref[1:2, :]
    some = total > 0.0
    safe = jnp.where(some, total, 1.0)
    out_ref[0, 0:1, :] = jnp.where(
        some, run_ref[0:1, :] * EXP_SCALE + jnp.log2(safe), NEGATIVE
    )
    out_ref[0, 1:2, :] = run_ref[2:3, :] / safe


def grads_kernel(
    planes, info_ref, qg_ref, kv_ref, stats_ref, out_ref, qs_ref, gs_ref, acc_ref
):
    query_row = pl.program_id(0)

    @pl.when(query_row == 0)
    def _():
        acc_ref[...] = jnp.zeros(acc_ref.shape, jnp.float32)

    stack_heads(qg_ref, 0, qs_ref)
    stack_heads(qg_ref, 1, gs_ref)
    parts = [stats_ref[source, 0, 0:1, :] for source in range(SIDE)]
    top = functools.reduce(jnp.maximum, parts)
    shares = [jnp.exp2(part - top) for part in parts]
    total = sum(shares)
    lse = top + jnp.log2(total)
    inner = sum(stats_ref[source, 0, 1:2, :] * shares[source] for source in range(SIDE))
    delta = inner / total
    for slot, plane in enumerate(planes):
        offset, valid = block_offset(info_ref, plane, query_row)

        @pl.when(valid)
        def _():
            score = lax.dot_general(
                kv_ref[plane, :, :HEAD_SIZE], qs_ref[...], NT, preferred_element_type=jnp.float32
            )
            dprob = lax.dot_general(
                kv_ref[plane, :, HEAD_SIZE:], gs_ref[...], NT, preferred_element_type=jnp.float32
            )
            prob = jnp.exp2(score * EXP_SCALE - lse)
            if plane == 0:
                prob = jnp.where(causal_mask(offset), prob, 0.0)
            dscore = (prob * (dprob - delta)).astype(jnp.bfloat16)
            key_part = lax.dot_general(
                dscore, qs_ref[...], NN, preferred_element_type=jnp.float32
            )
            value_part = lax.dot_general(
                prob.astype(jnp.bfloat16), gs_ref[...], NN, preferred_element_type=jnp.float32
            )
            acc_ref[slot, :, :HEAD_SIZE] += key_part * SCALE
            acc_ref[slot, :, HEAD_SIZE:] += value_part

    @pl.when(query_row == SIDE - 1)
    def _():
        out_ref[...] = acc_ref[...].astype(out_ref.dtype)


SMEM_SPEC = pl.BlockSpec(memory_space=pltpu.SMEM)
ROW_SPEC = pl.BlockSpec((1, 2, BLOCK_TOKENS, GROUP * HEAD_SIZE), lambda row: (row, 0, 0, 0))
KV_SHAPE = (PLANES, BLOCK_TOKENS, 2 * HEAD_SIZE)
KV_SPEC = pl.BlockSpec(KV_SHAPE, lambda row: (0, 0, 0))
STACKS = [
    pltpu.VMEM((ROWS, HEAD_SIZE), jnp.bfloat16),
    pltpu.VMEM((ROWS, HEAD_SIZE), jnp.bfloat16),
]
PARAMS = pltpu.CompilerParams(vmem_limit_bytes=40 * 1024 * 1024)


def stats_pass(info, qg, kv):
    return pl.pallas_call(
        stats_kernel,
        grid=(SIDE,),
        out_shape=jax.ShapeDtypeStruct((SIDE, STATS, ROWS), jnp.float32),
        in_specs=[SMEM_SPEC, ROW_SPEC, KV_SPEC],
        out_specs=pl.BlockSpec((1, STATS, ROWS), lambda row: (row, 0, 0)),
        scratch_shapes=STACKS + [pltpu.VMEM((8, ROWS), jnp.float32)],
        compiler_params=PARAMS,
        name="stats",
    )(info, qg, kv)


def grads_pass(planes, dtype, info, qg, kv, stats):
    shape = (len(planes), BLOCK_TOKENS, 2 * HEAD_SIZE)
    return pl.pallas_call(
        functools.partial(grads_kernel, planes),
        grid=(SIDE,),
        out_shape=jax.ShapeDtypeStruct(shape, dtype),
        in_specs=[
            SMEM_SPEC,
            ROW_SPEC,
            KV_SPEC,
            pl.BlockSpec((SIDE, 1, STATS, ROWS), lambda row: (0, row, 0, 0)),
        ],
        out_specs=pl.BlockSpec(shape, lambda row: (0, 0, 0)),
        scratch_shapes=STACKS + [pltpu.VMEM(shape, jnp.float32)],
        compiler_params=PARAMS,
        name="grads" + str(planes[0]),
    )(info, qg, kv, stats)


def pick_kernel(pick_ref, src_ref, out_ref):
    out_ref[0] = src_ref[...]


def pick_features(hidden, head):
    pick = jnp.stack([2 * (head % 2), head // 2]).astype(jnp.int32)
    spec = pltpu.PrefetchScalarGridSpec(
        num_scalar_prefetch=1,
        grid=(SIDE, 2),
        in_specs=[
            pl.BlockSpec(
                (BLOCK_TOKENS, 128),
                lambda lo, half, pick: (0, (pick[0] + half) * 16 + lo * 4 + pick[1]),
            )
        ],
        out_specs=pl.BlockSpec((1, BLOCK_TOKENS, 128), lambda lo, half, pick: (lo, 0, half)),
    )
    return pl.pallas_call(
        pick_kernel,
        out_shape=jax.ShapeDtypeStruct((SIDE, BLOCK_TOKENS, 256), hidden.dtype),
        grid_spec=spec,
        name="pick",
    )(pick, hidden)


def rotary_tables(positions):
    half = HEAD_SIZE // 2
    freqs = 500000.0 ** (-(jnp.arange(half, dtype=jnp.float32) * 2.0) / HEAD_SIZE)
    angles = positions.astype(jnp.float32)[:, None] * freqs[None, :]
    cosine, sine = jnp.cos(angles), jnp.sin(angles)
    return jnp.concatenate([cosine, cosine], -1), jnp.concatenate([sine, sine], -1)


def exchange(value, axis):
    return lax.all_to_all(value, axis, split_axis=0, concat_axis=0, tiled=True)


def small_sum(value, axis):
    count = axis_total(axis)
    spread = jnp.broadcast_to(value, (count, 8, 128))
    return jnp.sum(exchange(spread, axis), axis=0)[0:1, 0:1]


def per_device(hidden, queries, keys, values, output_gradient, doc_blocks):
    z = lax.axis_index(Z)
    row = lax.axis_index("y")
    head = lax.axis_index("head")
    ends = jnp.cumsum(doc_blocks)
    rows = SIDE * z + jnp.arange(SIDE)
    firsts = jnp.max(jnp.where(ends[None, :] <= rows[:, None], ends[None, :], 0), axis=1)
    info = jnp.concatenate([jnp.stack([z, row]), firsts]).astype(jnp.int32)
    here = SIDE * z + row
    f32 = jnp.float32

    paired = lax.all_gather(jnp.stack([queries, output_gradient]), "y")
    paired = pltpu.with_memory_space_constraint(paired, pltpu.HBM)

    own = jnp.concatenate([keys, values], axis=1)[None]
    four = rotate(own, Z, 4)
    even = jnp.concatenate([own, four])
    two = rotate(even, Z, 2)
    odd = rotate(jnp.concatenate([own, two[0:1], four]), Z, 1)
    column = jnp.concatenate([own, odd[0:1], two[0:1], odd[1:2], four, odd[2:3], two[1:2]])

    picked = pick_features(hidden, head)
    picked, _ = lax.optimization_barrier((picked, odd))
    tokens = exchange(picked, "z_lo")
    features = lax.all_gather(tokens.reshape(SIDE * BLOCK_TOKENS, 256), "head", axis=0)

    stats = stats_pass(info, paired, column)
    stats = exchange(jnp.broadcast_to(stats, (SIDE,) + stats.shape), "y")
    odd_grads = grads_pass(ODD, jnp.bfloat16, info, paired, column, stats)
    odd_back = rotate(odd_grads, Z, -1)
    even_grads = grads_pass(EVEN, f32, info, paired, column, stats)
    odd_back = odd_back.astype(f32)
    s0 = even_grads[0] + odd_back[0]
    s2 = even_grads[1] + odd_back[1]
    s4 = even_grads[2] + odd_back[2]
    two_back = rotate(jnp.stack([s2, even_grads[3]]).astype(jnp.bfloat16), Z, -2).astype(f32)
    s0 = s0 + two_back[0]
    s4 = s4 + two_back[1]
    four_back = rotate(s4.astype(jnp.bfloat16), Z, -4).astype(f32)
    s0 = s0 + four_back

    cosine, sine = rotary_tables(here * BLOCK_TOKENS + jnp.arange(BLOCK_TOKENS))
    key_grad = s0[:, :HEAD_SIZE]
    half = HEAD_SIZE // 2
    turned = jnp.concatenate([-key_grad[:, half:], key_grad[:, :half]], axis=-1)
    pre = jnp.concatenate([key_grad * cosine - turned * sine, s0[:, HEAD_SIZE:]], axis=1)
    pre = pre.astype(jnp.bfloat16)
    gathered = exchange(jnp.broadcast_to(pre, (SIDE,) + pre.shape), "z_lo")
    gathered = gathered.reshape(SIDE * BLOCK_TOKENS, 2 * HEAD_SIZE)

    weight = lax.dot_general(
        features, gathered, (((1,), (0,)), ((), ())), preferred_element_type=f32
    ).astype(jnp.bfloat16)
    weight = exchange(weight.reshape(SIDE, SIDE * BLOCK_TOKENS, 256), "y")
    weight = jnp.sum(weight.astype(f32), axis=0).astype(jnp.bfloat16)
    weight = exchange(weight.reshape(SIDE, BLOCK_TOKENS, 256), "z_hi")
    weight = jnp.sum(weight.astype(f32), axis=0)

    squares = jnp.sum(weight * weight).reshape(1, 1)
    squares = small_sum(squares, ("y", "head"))
    squares = small_sum(squares, Z)
    mean_square = squares / (2.0 * MODEL_WIDTH * KEY_VALUE_HEADS * HEAD_SIZE)
    factor = 1.0 / jnp.sqrt(mean_square + 1e-06)
    scaled = weight * factor
    return (scaled[:, :HEAD_SIZE], scaled[:, HEAD_SIZE:])


def solution(mesh):
    devices = mesh.devices.reshape(4, 4, 4, 8)
    split = Mesh(devices, ("z_hi", "z_lo", "y", "head"))
    placed = (P(CTX, None),) + (P(CTX, "head"),) * 4 + (P(),)
    return jax.shard_map(
        per_device,
        mesh=split,
        in_specs=placed,
        out_specs=(P(CTX, "head"), P(CTX, "head")),
        check_vma=False,
    )
```

time: 262 us -> 208 us (0.79)
  waiting for transfers between devices: 51.3 us -> 21.8 us
  starting transfers between devices: 64.6 us -> 51.2 us
  blocking collectives: 105 us -> 91.7 us
  Pallas kernels: 11.9 us -> 15.1 us
    ppermute x12 -> x6, waiting for transfers between devices: 51.3 us -> 16.5 us  [rotate(): lax.ppermute(value, axis, [(at, (at + steps) % count) for at in range(cou...]
    psum x2 -> x0, blocking collectives: 24.3 us -> none  [the longest x1 12.5 us: per_device(): squares = lax.psum(squares, 'z_hi')]
    ppermute x12 -> x6, starting transfers between devices: 61.1 us -> 47.7 us  [rotate(): lax.ppermute(value, axis, [(at, (at + steps) % count) for at in range(cou...]
    all_to_all x5 -> x6, blocking collectives: 81.1 us -> 91.7 us  [exchange(): return lax.all_to_all(value, axis, split_axis=0, concat_axis=0, tiled=True)]
    all_to_all x1, waiting for transfers between devices: 0.01 us -> 5.25 us  [exchange(): return lax.all_to_all(value, axis, split_axis=0, concat_axis=0, tiled=True)]
    pallas_call x8 -> x3, Pallas kernels: 6.88 us -> 10.1 us  [the longest x2 6.63 us: grads_pass(): pl.pallas_call(functools.partial(grads_kernel, planes), grid=(SIDE,), out...]
  transfers between devices with their start and end apart: 14 -> 9, of which waited for: 10 -> 6; matrix products, arithmetic and copies ran while one was open for 2% -> 2% of each run, Pallas kernels for 5% -> 7%
where the time goes in v2:
time: 208 us; the launch traced here: 207 us
  blocking collectives  91.7 us (44%)
  starting transfers between devices  51.2 us (25%)
  waiting for transfers between devices  21.8 us (10%)
  Pallas kernels  15.1 us (7%)
  between operations  15 us (7%)
  other arithmetic  6.16 us (3%)
  local copies, waits for them, and re-layouts  3.82 us (2%)
  matrix products  2.35 us (1%)
    all_to_all x6, blocking collectives, exchange(): return lax.all_to_all(value, axis, split_axis=0, concat_axis=0, tiled=True)  91.7 us
    ppermute x6, starting transfers between devices, rotate(): lax.ppermute(value, axis, [(at, (at + steps) % count) for at in range(cou...  47.7 us
    ppermute x6, waiting for transfers between devices, rotate(): lax.ppermute(value, axis, [(at, (at + steps) % count) for at in range(cou...  16.5 us
    pallas_call x2, Pallas kernels, grads_pass(): pl.pallas_call(functools.partial(grads_kernel, planes), grid=(SIDE,), out...  6.63 us
    all_to_all x1, waiting for transfers between devices, exchange(): return lax.all_to_all(value, axis, split_axis=0, concat_axis=0, tiled=True)  5.25 us
    pallas_call x1, Pallas kernels, pick_features(): pl.pallas_call(pick_kernel, out_shape=jax.ShapeDtypeStruct((SIDE, BLOCK_T...  4.99 us
  transfers between devices with their start and end apart: 9, of which 6 were waited for; matrix products, arithmetic and copies ran while one was open for 2% of the time, Pallas kernels for 7%

profile of v2, /device:TPU:1, one launch (start us, length us, event | category | flops | bytes accessed | tf_op | source)
XLA Modules:
  0.0 207.2 jit_solution(18303453553990090784)
XLA Ops:
  7.2 0.0 all-gather.6.cloned.1.call-start
  7.2 1.9 pad_maximum_fusion
  9.1 0.0 all-gather.6.cloned.1.call-update
  9.1 0.8 maximum_bitcast_fusion
  9.9 9.6 %collective-permute-start = (bf16[1,128,256]{2,1,0:T(8,128)(2,1)S(1)}, bf16[1,128,256]{2,1,0:T(8,128)(2,1)S(1)}, u32[]{:S(2)}, u32[]{:S(2)}) collective-permute-start(bf16[1,128,256]{2,1,0:T(8,128)(2,1)S(1)} %maximum_bitcast_fusion), channel_id=1, source_target_pairs={{0,128},{32,160},{64,192},{96,224},{128,256},{160,288},{192,320},{... | collective-permute-start | bytes 196616 | tf_op jit(solution)/shard_map/ppermute | solution.py:44
  19.6 5.6 %collective-permute-done = bf16[1,128,256]{2,1,0:T(8,128)(2,1)S(1)} collective-permute-done((bf16[1,128,256]{2,1,0:T(8,128)(2,1)S(1)}, bf16[1,128,256]{2,1,0:T(8,128)(2,1)S(1)}, u32[]{:S(2)}, u32[]{:S(2)}) %collective-permute-start) | collective-permute-done | bytes 65568 | tf_op jit(solution)/shard_map/ppermute | solution.py:44
  25.2 6.1 %collective-permute-start.1 = (bf16[2,128,256]{2,1,0:T(8,128)(2,1)S(1)}, bf16[2,128,256]{2,1,0:T(8,128)(2,1)S(1)}, u32[]{:S(2)}, u32[]{:S(2)}) collective-permute-start(bf16[2,128,256]{2,1,0:T(8,128)(2,1)S(1)} %pad_maximum_fusion.2), channel_id=1, source_target_pairs={{0,64},{32,96},{64,128},{96,160},{128,192},{160,224},{192,256},{22... | collective-permute-start | bytes 393224 | tf_op jit(solution)/shard_map/ppermute | solution.py:44
  31.3 0.8 reduce-window.8
  32.2 4.7 %collective-permute-done.1 = bf16[2,128,256]{2,1,0:T(8,128)(2,1)S(1)} collective-permute-done((bf16[2,128,256]{2,1,0:T(8,128)(2,1)S(1)}, bf16[2,128,256]{2,1,0:T(8,128)(2,1)S(1)}, u32[]{:S(2)}, u32[]{:S(2)}) %collective-permute-start.1) | collective-permute-done | bytes 131104 | tf_op jit(solution)/shard_map/ppermute | solution.py:44
  36.9 6.0 %collective-permute-start.2 = (bf16[3,128,256]{2,1,0:T(8,128)(2,1)S(1)}, bf16[3,128,256]{2,1,0:T(8,128)(2,1)S(1)}, u32[]{:S(2)}, u32[]{:S(2)}) collective-permute-start(bf16[3,128,256]{2,1,0:T(8,128)(2,1)S(1)} %pad_maximum_fusion.1), channel_id=1, source_target_pairs={{0,32},{32,64},{64,96},{96,128},{128,160},{160,192},{192,224},{224... | collective-permute-start | bytes 589832 | tf_op jit(solution)/shard_map/ppermute | solution.py:44
  42.9 0.7 pad_add_fusion.pick_ref
  43.6 5.0 %pick.1 = bf16[4,128,256]{2,1,0:T(8,128)(2,1)} custom-call(s32[2]{0:T(128)} %pad_add_fusion.pick_ref, bf16[128,8192]{1,0:T(8,128)(2,1)} %src_ref.1), custom_call_target="tpu_custom_call" | custom-call | tf_op jit(solution)/shard_map/pick/pallas_call | solution.py:210
  48.6 0.0 collective-permute-done.2
  48.6 3.4 %all-to-all-start = ((bf16[4,128,256]{2,1,0:T(8,128)(2,1)}), bf16[4,128,256]{2,1,0:T(8,128)(2,1)S(1)}, u32[]{:S(2)}, u32[]{:S(2)}) async-start(bf16[4,128,256]{2,1,0:T(8,128)(2,1)} %pick.1), calls=%async_computation | async-start | bytes 524288 | tf_op jit(solution)/shard_map/all_to_all | solution.py:227
  52.0 0.0 all-gather.4.cloned.1.call-start
  52.0 0.2 select_reduce_fusion
  52.2 0.1 pad_add_fusion.1.info_ref
  52.3 0.0 copy-done.1
  52.4 5.2 %all-to-all-done = bf16[4,128,256]{2,1,0:T(8,128)(2,1)S(1)} async-done(((bf16[4,128,256]{2,1,0:T(8,128)(2,1)}), bf16[4,128,256]{2,1,0:T(8,128)(2,1)S(1)}, u32[]{:S(2)}, u32[]{:S(2)}) %all-to-all-start) | async-done | bytes 262176 | tf_op jit(solution)/shard_map/all_to_all | solution.py:227
  57.6 0.7 copy-done
  58.3 0.0 all-gather.4.cloned.1.call-update
  58.4 0.0 all-gather.6.cloned.1.call-done
  58.4 3.5 %stats.1 = f32[4,2,1024]{2,1,0:T(2,128)S(1)} custom-call(s32[6]{0:T(128)S(1)} %pad_add_fusion.1.info_ref, bf16[4,2,128,1024]{3,2,1,0:T(8,128)(2,1)} %bitcast.29, bf16[7,128,256]{2,1,0:T(8,128)(2,1)S(1)} %slice_dynamic-update-slice_fusion.kv_ref), custom_call_target="tpu_custom_call" | custom-call | tf_op jit(solution)/shard_map/stats/pallas_call | solution.py:162
  62.0 8.4 %all_to_all.35.stats_ref = f32[4,4,2,1024]{3,2,1,0:T(2,128)S(1)} all-to-all(f32[4,4,2,1024]{3,2,1,0:T(2,128)S(1)} %broadcast_in_dim.36), channel_id=1, replica_groups=mesh['z_hi'=4,'z_lo'=4,'y'=4,'head'=8] {'y'}, dimensions={0} | all-to-all | bytes 262144 | tf_op jit(solution)/shard_map/all_to_all | solution.py:227
  70.3 2.6 %grads1.1 = bf16[3,128,256]{2,1,0:T(8,128)(2,1)S(1)} custom-call(s32[6]{0:T(128)S(1)} %pad_add_fusion.1.info_ref, bf16[4,2,128,1024]{3,2,1,0:T(8,128)(2,1)} %bitcast.30, bf16[7,128,256]{2,1,0:T(8,128)(2,1)S(1)} %slice_dynamic-update-slice_fusion.kv_ref, f32[4,4,2,1024]{3,2,1,0:T(2,128)S(1)} %all_to_all.35.stats_ref), custom_call_target="tpu_custom_call" | custom-call | tf_op jit(solution)/shard_map/grads1/pallas_call | solution.py:176
  73.0 3.4 %collective-permute-start.3 = (bf16[3,128,256]{2,1,0:T(8,128)(2,1)S(1)}, bf16[3,128,256]{2,1,0:T(8,128)(2,1)S(1)}, u32[]{:S(2)}, u32[]{:S(2)}) collective-permute-start(bf16[3,128,256]{2,1,0:T(8,128)(2,1)S(1)} %grads1.1), channel_id=1, source_target_pairs={{0,480},{32,0},{64,32},{96,64},{128,96},{160,128},{192,160},{224,1... | collective-permute-start | bytes 589832 | tf_op jit(solution)/shard_map/ppermute | solution.py:44
  76.4 4.0 %grads0.1 = f32[4,128,256]{2,1,0:T(8,128)S(1)} custom-call(s32[6]{0:T(128)S(1)} %pad_add_fusion.1.info_ref, bf16[4,2,128,1024]{3,2,1,0:T(8,128)(2,1)} %bitcast.31, bf16[7,128,256]{2,1,0:T(8,128)(2,1)S(1)} %slice_dynamic-update-slice_fusion.kv_ref, f32[4,4,2,1024]{3,2,1,0:T(2,128)S(1)} %all_to_all.35.stats_ref), custom_call_target="tpu_custom_call" | custom-call | tf_op jit(solution)/shard_map/grads0/pallas_call | solution.py:176
  80.4 0.1 collective-permute-done.3
  80.6 17.4 %collective-permute-start.4 = (bf16[2,128,256]{2,1,0:T(8,128)(2,1)S(1)}, bf16[2,128,256]{2,1,0:T(8,128)(2,1)S(1)}, u32[]{:S(2)}, u32[]{:S(2)}) collective-permute-start(bf16[2,128,256]{2,1,0:T(8,128)(2,1)S(1)} %pad_maximum_fusion.3), channel_id=1, source_target_pairs={{0,448},{32,480},{64,0},{96,32},{128,64},{160,96},{192,128},{224,1... | collective-permute-start | bytes 393224 | tf_op jit(solution)/shard_map/ppermute | solution.py:44
  98.0 1.9 collective-permute-done.4
  99.9 5.1 %collective-permute-start.5 = (bf16[128,256]{1,0:T(8,128)(2,1)S(1)}, bf16[128,256]{1,0:T(8,128)(2,1)S(1)}, u32[]{:S(2)}, u32[]{:S(2)}) collective-permute-start(bf16[128,256]{1,0:T(8,128)(2,1)S(1)} %fusion.4), channel_id=1, source_target_pairs={{0,384},{32,416},{64,448},{96,480},{128,0},{160,32},{192,64},{224,... | collective-permute-start | bytes 196616 | tf_op jit(solution)/shard_map/ppermute | solution.py:44
  105.0 0.3 multiply_sine_fusion
  105.4 4.3 %collective-permute-done.5 = bf16[128,256]{1,0:T(8,128)(2,1)S(1)} collective-permute-done((bf16[128,256]{1,0:T(8,128)(2,1)S(1)}, bf16[128,256]{1,0:T(8,128)(2,1)S(1)}, u32[]{:S(2)}, u32[]{:S(2)}) %collective-permute-start.5) | collective-permute-done | bytes 65568 | tf_op jit(solution)/shard_map/ppermute | solution.py:44
  109.7 0.1 slice_negate_fusion
  109.8 0.1 fusion.6
  110.0 10.5 %all_to_all.36 = bf16[4,128,256]{2,1,0:T(8,128)(2,1)S(1)} all-to-all(bf16[4,128,256]{2,1,0:T(8,128)(2,1)S(1)} %broadcast_in_dim.37), channel_id=1, replica_groups=mesh['z_hi'=4,'z_lo'=4,'y'=4,'head'=8] {'z_lo'}, dimensions={0} | all-to-all | bytes 524288 | tf_op jit(solution)/shard_map/all_to_all | solution.py:227
  120.5 2.3 %convolution_convert_fusion = bf16[8,256,256]{2,1,0:T(8,128)(2,1)S(1)} fusion(bf16[8,512,256]{2,1,0:T(8,128)(2,1)} %all-gather.4.cloned.1.call-done, bf16[512,256,1]{1,0,2:T(8,128)(2,1)S(1)} %bitcast.35), kind=kOutput, calls=%fused_computation | convolution fusion | flops 537395200 | bytes 3407872 | tf_op jit(solution)/shard_map/dot_general | solution.py:286
  122.9 12.2 %all_to_all.37 = bf16[4,512,256]{2,1,0:T(8,128)(2,1)S(1)} all-to-all(bf16[4,512,256]{2,1,0:T(8,128)(2,1)S(1)} %bitcast.33), channel_id=1, replica_groups=mesh['z_hi'=4,'z_lo'=4,'y'=4,'head'=8] {'y'}, dimensions={0} | all-to-all | bytes 2097152 | tf_op jit(solution)/shard_map/all_to_all | solution.py:227
  135.0 0.3 reduce_sum.48
  135.3 25.1 %all_to_all.38 = bf16[4,128,256]{2,1,0:T(8,128)(2,1)S(1)} all-to-all(bf16[4,128,256]{2,1,0:T(8,128)(2,1)S(1)} %bitcast.32), channel_id=1, replica_groups=mesh['z_hi'=4,'z_lo'=4,'y'=4,'head'=8] {'z_hi'}, dimensions={0} | all-to-all | bytes 524288 | tf_op jit(solution)/shard_map/all_to_all | solution.py:227
  160.4 0.6 multiply_reduce_fusion
  161.0 0.7 broadcast_in_dim.38
  161.7 20.1 %all_to_all.39 = f32[32,8,128]{2,1,0:T(8,128)S(1)} all-to-all(f32[32,8,128]{2,1,0:T(8,128)S(1)} %broadcast_in_dim.38), channel_id=1, replica_groups=mesh['z_hi'=4,'z_lo'=4,'y'=4,'head'=8] {'y','head'}, dimensions={0} | all-to-all | bytes 262144 | tf_op jit(solution)/shard_map/all_to_all | solution.py:227
  181.8 0.5 slice.91
  182.3 0.6 broadcast_in_dim.39
  183.0 15.4 %all_to_all.40 = f32[16,8,128]{2,1,0:T(8,128)S(1)} all-to-all(f32[16,8,128]{2,1,0:T(8,128)S(1)} %broadcast_in_dim.39), channel_id=1, replica_groups=mesh['z_hi'=4,'z_lo'=4,'y'=4,'head'=8] {'z_hi','z_lo'}, dimensions={0} | all-to-all | bytes 131072 | tf_op jit(solution)/shard_map/all_to_all | solution.py:227
  198.4 0.5 slice.93
  199.7 0.7 fusion.7
  (33 shorter events, 0.4 us)
Async XLA Ops:
  7.2 51.3 %all-gather.6.cloned.1.call-start = ((), (), s32[]{:S(2)}) async-start(), calls=%async_computation.8 | async-start | bytes 2621440 | tf_op jit(solution)/shard_map/all_gather | solution.py:247
  9.1 43.2 %copy-start.1 = (bf16[128,128]{1,0:T(8,128)(2,1)S(1)}, bf16[128,128]{1,0:T(8,128)(2,1)}, u32[]{:S(2)}) copy-start(bf16[128,128]{1,0:T(8,128)(2,1)} %param.9) | copy-start | bytes 98308
  9.1 43.2 %copy-start.2 = (bf16[128,128]{1,0:T(8,128)(2,1)S(1)}, bf16[128,128]{1,0:T(8,128)(2,1)}, u32[]{:S(2)}) copy-start(bf16[128,128]{1,0:T(8,128)(2,1)} %param.8) | copy-start | bytes 98308
  9.9 15.2 %collective-permute-start = (bf16[1,128,256]{2,1,0:T(8,128)(2,1)S(1)}, bf16[1,128,256]{2,1,0:T(8,128)(2,1)S(1)}, u32[]{:S(2)}, u32[]{:S(2)}) collective-permute-start(bf16[1,128,256]{2,1,0:T(8,128)(2,1)S(1)} %maximum_bitcast_fusion), channel_id=1, source_target_pairs={{0,128},{32,160},{64,192},{96,224},{128,256},{160,288},{192,320},{... | collective-permute-start | bytes 196616 | tf_op jit(solution)/shard_map/ppermute | solution.py:44
  25.2 11.7 %collective-permute-start.1 = (bf16[2,128,256]{2,1,0:T(8,128)(2,1)S(1)}, bf16[2,128,256]{2,1,0:T(8,128)(2,1)S(1)}, u32[]{:S(2)}, u32[]{:S(2)}) collective-permute-start(bf16[2,128,256]{2,1,0:T(8,128)(2,1)S(1)} %pad_maximum_fusion.2), channel_id=1, source_target_pairs={{0,64},{32,96},{64,128},{96,160},{128,192},{160,224},{192,256},{22... | collective-permute-start | bytes 393224 | tf_op jit(solution)/shard_map/ppermute | solution.py:44
  36.9 11.7 %collective-permute-start.2 = (bf16[3,128,256]{2,1,0:T(8,128)(2,1)S(1)}, bf16[3,128,256]{2,1,0:T(8,128)(2,1)S(1)}, u32[]{:S(2)}, u32[]{:S(2)}) collective-permute-start(bf16[3,128,256]{2,1,0:T(8,128)(2,1)S(1)} %pad_maximum_fusion.1), channel_id=1, source_target_pairs={{0,32},{32,64},{64,96},{96,128},{128,160},{160,192},{192,224},{224... | collective-permute-start | bytes 589832 | tf_op jit(solution)/shard_map/ppermute | solution.py:44
  48.6 9.0 %all-to-all-start = ((bf16[4,128,256]{2,1,0:T(8,128)(2,1)}), bf16[4,128,256]{2,1,0:T(8,128)(2,1)S(1)}, u32[]{:S(2)}, u32[]{:S(2)}) async-start(bf16[4,128,256]{2,1,0:T(8,128)(2,1)} %pick.1), calls=%async_computation | async-start | bytes 524288 | tf_op jit(solution)/shard_map/all_to_all | solution.py:227
  52.0 68.5 %all-gather.4.cloned.1.call-start = ((), (), s32[]{:S(2)}) async-start(), calls=%async_computation.7 | async-start | bytes 2359296 | tf_op jit(solution)/shard_map/all_gather | solution.py:260
  57.6 0.7 copy-start
  73.0 7.5 %collective-permute-start.3 = (bf16[3,128,256]{2,1,0:T(8,128)(2,1)S(1)}, bf16[3,128,256]{2,1,0:T(8,128)(2,1)S(1)}, u32[]{:S(2)}, u32[]{:S(2)}) collective-permute-start(bf16[3,128,256]{2,1,0:T(8,128)(2,1)S(1)} %grads1.1), channel_id=1, source_target_pairs={{0,480},{32,0},{64,32},{96,64},{128,96},{160,128},{192,160},{224,1... | collective-permute-start | bytes 589832 | tf_op jit(solution)/shard_map/ppermute | solution.py:44
  80.6 19.3 %collective-permute-start.4 = (bf16[2,128,256]{2,1,0:T(8,128)(2,1)S(1)}, bf16[2,128,256]{2,1,0:T(8,128)(2,1)S(1)}, u32[]{:S(2)}, u32[]{:S(2)}) collective-permute-start(bf16[2,128,256]{2,1,0:T(8,128)(2,1)S(1)} %pad_maximum_fusion.3), channel_id=1, source_target_pairs={{0,448},{32,480},{64,0},{96,32},{128,64},{160,96},{192,128},{224,1... | collective-permute-start | bytes 393224 | tf_op jit(solution)/shard_map/ppermute | solution.py:44
  99.9 9.7 %collective-permute-start.5 = (bf16[128,256]{1,0:T(8,128)(2,1)S(1)}, bf16[128,256]{1,0:T(8,128)(2,1)S(1)}, u32[]{:S(2)}, u32[]{:S(2)}) collective-permute-start(bf16[128,256]{1,0:T(8,128)(2,1)S(1)} %fusion.4), channel_id=1, source_target_pairs={{0,384},{32,416},{64,448},{96,480},{128,0},{160,32},{192,64},{224,... | collective-permute-start | bytes 196616 | tf_op jit(solution)/shard_map/ppermute | solution.py:44
Sparse Core Ops, SparseCore 0:
  10.1 43.7 all-gather.5
  58.5 33.5 all-gather.3

commit v3 on v2

v3 whole, which is shorter than its diff:
```python
import functools

import jax
import jax.numpy as jnp
from jax import lax
from jax.experimental import pallas as pl
from jax.experimental.pallas import tpu as pltpu
from jax.sharding import Mesh, PartitionSpec as P

MODEL_WIDTH = 8192
QUERY_HEADS = 64
KEY_VALUE_HEADS = 8
HEAD_SIZE = 128
BLOCK_TOKENS = 128
GROUP = QUERY_HEADS // KEY_VALUE_HEADS
ROWS = GROUP * BLOCK_TOKENS
PLANES = 7
SIDE = 4
STATS = 2
ORDER = (0, 2, 4, 6, 1, 3, 5)
EVEN_GROUPS = ((0, 2), (2, 4))
ODD_GROUPS = ((4, 6), (6, 7))
NEGATIVE = -1e30
SCALE = HEAD_SIZE ** (-0.5)
LOG2E = 1.4426950408889634
EXP_SCALE = SCALE * LOG2E
Z = ("z_hi", "z_lo")
CTX = ("z_hi", "z_lo", "y")

NT = (((1,), (1,)), ((), ()))
NN = (((1,), (0,)), ((), ()))
TN = (((0,), (0,)), ((), ()))


def axis_total(axis):
    names = axis if isinstance(axis, tuple) else (axis,)
    total = 1
    for name in names:
        total *= lax.axis_size(name)
    return total


def rotate(value, axis, steps):
    count = axis_total(axis)
    return lax.ppermute(value, axis, [(at, (at + steps) % count) for at in range(count)])


def stack_heads(row_ref, which, dst_ref):
    for head in range(GROUP):
        dst_ref[head * BLOCK_TOKENS:(head + 1) * BLOCK_TOKENS, :] = row_ref[
            0, which, :, head * HEAD_SIZE:(head + 1) * HEAD_SIZE
        ]


def causal_mask(offset):
    token = lax.broadcasted_iota(jnp.int32, (BLOCK_TOKENS, ROWS), 0)
    query = lax.broadcasted_iota(jnp.int32, (BLOCK_TOKENS, ROWS), 1)
    return token <= (query & (BLOCK_TOKENS - 1)) + BLOCK_TOKENS * offset


def block_offset(info_ref, plane, query_row):
    offset = SIDE * plane + query_row - info_ref[1]
    position = SIDE * info_ref[0] + query_row
    return offset, (offset >= 0) & (position - offset >= info_ref[2 + query_row])


def group_valid(info_ref, first, last, query_row):
    return [block_offset(info_ref, ORDER[slot], query_row) for slot in range(first, last)]


def masked(value, checks, first, fill):
    parts = []
    for index, (offset, valid) in enumerate(checks):
        part = value[index * BLOCK_TOKENS:(index + 1) * BLOCK_TOKENS]
        keep = valid if ORDER[first + index] else valid & causal_mask(offset)
        parts.append(jnp.where(keep, part, fill))
    return parts[0] if len(parts) == 1 else jnp.concatenate(parts, axis=0)


def products(kv_ref, first, last, qs, gs):
    rows = (last - first) * BLOCK_TOKENS
    key = kv_ref[first:last, :, :HEAD_SIZE].reshape(rows, HEAD_SIZE)
    value = kv_ref[first:last, :, HEAD_SIZE:].reshape(rows, HEAD_SIZE)
    score = lax.dot_general(key, qs, NT, preferred_element_type=jnp.float32)
    dprob = lax.dot_general(value, gs, NT, preferred_element_type=jnp.float32)
    return score, dprob


def stats_kernel(info_ref, row_ref, kv_ref, out_ref, qs_ref, gs_ref, run_ref):
    query_row = pl.program_id(0)
    stack_heads(row_ref, 0, qs_ref)
    stack_heads(row_ref, 1, gs_ref)
    run_ref[0:1, :] = jnp.full((1, ROWS), NEGATIVE, jnp.float32)
    run_ref[1:, :] = jnp.zeros((7, ROWS), jnp.float32)
    for first, last in EVEN_GROUPS + ODD_GROUPS:
        checks = group_valid(info_ref, first, last, query_row)

        @pl.when(functools.reduce(jnp.logical_or, [valid for _, valid in checks]))
        def _():
            score, dprob = products(kv_ref, first, last, qs_ref[...], gs_ref[...])
            score = masked(score, checks, first, NEGATIVE)
            old = run_ref[0:1, :]
            top = jnp.maximum(old, jnp.max(score, axis=0, keepdims=True))
            weight = jnp.exp2((score - top) * EXP_SCALE)
            keep = jnp.exp2((old - top) * EXP_SCALE)
            run_ref[0:1, :] = top
            run_ref[1:2, :] = run_ref[1:2, :] * keep + jnp.sum(weight, axis=0, keepdims=True)
            run_ref[2:3, :] = run_ref[2:3, :] * keep + jnp.sum(
                weight * dprob, axis=0, keepdims=True
            )

    total = run_ref[1:2, :]
    some = total > 0.0
    safe = jnp.where(some, total, 1.0)
    lse = jnp.where(some, run_ref[0:1, :] * EXP_SCALE + jnp.log2(safe), NEGATIVE)
    mean = run_ref[2:3, :] / safe
    for target in range(SIDE):
        out_ref[target, 0, 0:1, :] = lse
        out_ref[target, 0, 1:2, :] = mean


def grads_kernel(groups, info_ref, row_ref, kv_ref, stats_ref, out_ref, qs_ref, gs_ref, acc_ref):
    query_row = pl.program_id(0)
    base = groups[0][0]

    @pl.when(query_row == 0)
    def _():
        acc_ref[...] = jnp.zeros(acc_ref.shape, jnp.float32)

    stack_heads(row_ref, 0, qs_ref)
    stack_heads(row_ref, 1, gs_ref)
    parts = [stats_ref[source, 0, 0:1, :] for source in range(SIDE)]
    top = functools.reduce(jnp.maximum, parts)
    shares = [jnp.exp2(part - top) for part in parts]
    total = sum(shares)
    lse = top + jnp.log2(total)
    inner = sum(stats_ref[source, 0, 1:2, :] * shares[source] for source in range(SIDE))
    delta = inner / total
    for first, last in groups:
        checks = group_valid(info_ref, first, last, query_row)

        @pl.when(functools.reduce(jnp.logical_or, [valid for _, valid in checks]))
        def _():
            qs, gs = qs_ref[...], gs_ref[...]
            score, dprob = products(kv_ref, first, last, qs, gs)
            prob = masked(jnp.exp2(score * EXP_SCALE - lse), checks, first, 0.0)
            dscore = (prob * (dprob - delta)).astype(jnp.bfloat16)
            key_part = lax.dot_general(dscore, qs, NN, preferred_element_type=jnp.float32)
            value_part = lax.dot_general(
                prob.astype(jnp.bfloat16), gs, NN, preferred_element_type=jnp.float32
            )
            shape = (last - first, BLOCK_TOKENS, HEAD_SIZE)
            at = slice(first - base, last - base)
            acc_ref[at, :, :HEAD_SIZE] += (key_part * SCALE).reshape(shape)
            acc_ref[at, :, HEAD_SIZE:] += value_part.reshape(shape)

    @pl.when(query_row == SIDE - 1)
    def _():
        out_ref[...] = acc_ref[...].astype(out_ref.dtype)


STACKS = [
    pltpu.VMEM((ROWS, HEAD_SIZE), jnp.bfloat16),
    pltpu.VMEM((ROWS, HEAD_SIZE), jnp.bfloat16),
]
PARAMS = pltpu.CompilerParams(vmem_limit_bytes=40 * 1024 * 1024)
ROW_SHAPE = (1, 2, BLOCK_TOKENS, GROUP * HEAD_SIZE)
ROW_SPEC = pl.BlockSpec(ROW_SHAPE, lambda step, info: (step, 0, 0, 0))
STATS_SPEC = pl.BlockSpec((SIDE, 1, STATS, ROWS), lambda step, info: (0, step, 0, 0))


def whole(shape):
    return pl.BlockSpec(shape, lambda step, info: (0,) * len(shape))


def stats_pass(info, rows, kv):
    spec = pltpu.PrefetchScalarGridSpec(
        num_scalar_prefetch=1,
        grid=(SIDE,),
        in_specs=[ROW_SPEC, whole(kv.shape)],
        out_specs=STATS_SPEC,
        scratch_shapes=STACKS + [pltpu.VMEM((8, ROWS), jnp.float32)],
    )
    return pl.pallas_call(
        stats_kernel,
        out_shape=jax.ShapeDtypeStruct((SIDE, SIDE, STATS, ROWS), jnp.float32),
        grid_spec=spec,
        compiler_params=PARAMS,
        name="stats",
    )(info, rows, kv)


def grads_pass(groups, dtype, info, rows, kv, stats):
    shape = (groups[-1][1] - groups[0][0], BLOCK_TOKENS, 2 * HEAD_SIZE)
    spec = pltpu.PrefetchScalarGridSpec(
        num_scalar_prefetch=1,
        grid=(SIDE,),
        in_specs=[ROW_SPEC, whole(kv.shape), STATS_SPEC],
        out_specs=whole(shape),
        scratch_shapes=STACKS + [pltpu.VMEM(shape, jnp.float32)],
    )
    return pl.pallas_call(
        functools.partial(grads_kernel, groups),
        out_shape=jax.ShapeDtypeStruct(shape, dtype),
        grid_spec=spec,
        compiler_params=PARAMS,
        name="grads" + str(groups[0][0]),
    )(info, rows, kv, stats)


def pick_kernel(pick_ref, left_ref, right_ref, out_ref):
    out_ref[0, :, :128] = left_ref[...]
    out_ref[0, :, 128:] = right_ref[...]


def pick_features(hidden, head):
    pick = jnp.stack([2 * (head % 2), head // 2]).astype(jnp.int32)

    def half_spec(half):
        return pl.BlockSpec(
            (BLOCK_TOKENS, 128), lambda lo, pick: (0, (pick[0] + half) * 16 + lo * 4 + pick[1])
        )

    spec = pltpu.PrefetchScalarGridSpec(
        num_scalar_prefetch=1,
        grid=(SIDE,),
        in_specs=[half_spec(0), half_spec(1)],
        out_specs=pl.BlockSpec((1, BLOCK_TOKENS, 256), lambda lo, pick: (lo, 0, 0)),
    )
    return pl.pallas_call(
        pick_kernel,
        out_shape=jax.ShapeDtypeStruct((SIDE, BLOCK_TOKENS, 256), hidden.dtype),
        grid_spec=spec,
        name="pick",
    )(pick, hidden, hidden)


def square_kernel(parts_ref, weight_ref, spread_ref):
    weight = sum(parts_ref[source].astype(jnp.float32) for source in range(SIDE))
    weight_ref[...] = weight
    squares = jnp.sum((weight * weight).reshape(16, 8, 256), axis=0)
    squares = squares[:, :128] + squares[:, 128:]
    spread_ref[...] = jnp.broadcast_to(squares, spread_ref.shape)


def square_pass(parts):
    return pl.pallas_call(
        square_kernel,
        out_shape=(
            jax.ShapeDtypeStruct((BLOCK_TOKENS, 256), jnp.float32),
            jax.ShapeDtypeStruct((32, 8, 128), jnp.float32),
        ),
        name="square",
    )(parts)


def spread_kernel(parts_ref, out_ref):
    out_ref[...] = jnp.broadcast_to(jnp.sum(parts_ref[...], axis=0), out_ref.shape)


def spread_pass(parts):
    return pl.pallas_call(
        spread_kernel, out_shape=jax.ShapeDtypeStruct((16, 8, 128), jnp.float32), name="spread"
    )(parts)


def finish_kernel(parts_ref, weight_ref, key_ref, value_ref):
    total = jnp.sum(jnp.sum(parts_ref[...], axis=0))
    mean_square = total / (2.0 * MODEL_WIDTH * KEY_VALUE_HEADS * HEAD_SIZE)
    factor = 1.0 / jnp.sqrt(jnp.full((1, HEAD_SIZE), mean_square + 1e-06, jnp.float32))
    key_ref[...] = weight_ref[:, :HEAD_SIZE] * factor
    value_ref[...] = weight_ref[:, HEAD_SIZE:] * factor


def finish_pass(parts, weight):
    shape = jax.ShapeDtypeStruct((BLOCK_TOKENS, HEAD_SIZE), jnp.float32)
    return pl.pallas_call(finish_kernel, out_shape=(shape, shape), name="finish")(parts, weight)


def fan_kernel(src_ref, out_ref):
    out_ref[0] = src_ref[...]


def fan_out(tokens, copies):
    rows, width = tokens.shape
    return pl.pallas_call(
        fan_kernel,
        grid=(copies,),
        out_shape=jax.ShapeDtypeStruct((copies, rows, width), tokens.dtype),
        in_specs=[pl.BlockSpec((rows, width), lambda copy: (0, 0))],
        out_specs=pl.BlockSpec((1, rows, width), lambda copy: (copy, 0, 0)),
        name="fan",
    )(tokens)


def rotary_tables(positions):
    half = HEAD_SIZE // 2
    freqs = 500000.0 ** (-(jnp.arange(half, dtype=jnp.float32) * 2.0) / HEAD_SIZE)
    angles = positions.astype(jnp.float32)[:, None] * freqs[None, :]
    cosine, sine = jnp.cos(angles), jnp.sin(angles)
    return jnp.concatenate([cosine, cosine], -1), jnp.concatenate([sine, sine], -1)


def exchange(value, axis):
    return lax.all_to_all(value, axis, split_axis=0, concat_axis=0, tiled=True)


def per_device(hidden, queries, keys, values, output_gradient, doc_blocks):
    z = lax.axis_index(Z)
    row = lax.axis_index("y")
    head = lax.axis_index("head")
    ends = jnp.cumsum(doc_blocks)
    blocks = SIDE * z + jnp.arange(SIDE)
    firsts = jnp.max(jnp.where(ends[None, :] <= blocks[:, None], ends[None, :], 0), axis=1)
    info = jnp.concatenate([jnp.stack([z, row]), firsts]).astype(jnp.int32)
    here = SIDE * z + row
    f32 = jnp.float32

    own = jnp.concatenate([keys, values], axis=1)[None]
    four = rotate(own, Z, 4)
    rows = jnp.stack([queries, output_gradient])
    query_rows = exchange(jnp.broadcast_to(rows, (SIDE,) + rows.shape), "y")
    even = jnp.concatenate([own, four])
    two = rotate(even, Z, 2)
    odd = rotate(jnp.concatenate([own, two[0:1], four]), Z, 1)
    column = jnp.concatenate([own, two[0:1], four, two[1:2], odd])

    picked, odd = lax.optimization_barrier((pick_features(hidden, head), odd))
    tokens = exchange(picked, "z_lo").reshape(SIDE * BLOCK_TOKENS, 256)
    stats = stats_pass(info, query_rows, column)
    tokens, stats = lax.optimization_barrier((tokens, stats))
    stats = exchange(stats, "y")
    tokens, stats = lax.optimization_barrier((fan_out(tokens, 8), stats))
    features = exchange(tokens, "head")
    odd_grads = grads_pass(ODD_GROUPS, jnp.bfloat16, info, query_rows, column, stats)
    odd_back = rotate(odd_grads, Z, -1)
    even_grads = grads_pass(EVEN_GROUPS, f32, info, query_rows, column, stats)
    odd_back = odd_back.astype(f32)
    s0 = even_grads[0] + odd_back[0]
    s2 = even_grads[1] + odd_back[1]
    s4 = even_grads[2] + odd_back[2]
    two_back = rotate(jnp.stack([s2, even_grads[3]]).astype(jnp.bfloat16), Z, -2).astype(f32)
    s0 = s0 + two_back[0]
    s4 = s4 + two_back[1]
    four_back = rotate(s4.astype(jnp.bfloat16), Z, -4)
    features, four_back = lax.optimization_barrier((features, four_back))
    s0 = s0 + four_back.astype(f32)

    cosine, sine = rotary_tables(here * BLOCK_TOKENS + jnp.arange(BLOCK_TOKENS))
    key_grad = s0[:, :HEAD_SIZE]
    half = HEAD_SIZE // 2
    turned = jnp.concatenate([-key_grad[:, half:], key_grad[:, :half]], axis=-1)
    pre = jnp.concatenate([key_grad * cosine - turned * sine, s0[:, HEAD_SIZE:]], axis=1)
    pre = pre.astype(jnp.bfloat16)
    gathered = exchange(jnp.broadcast_to(pre, (SIDE,) + pre.shape), "z_lo")
    gathered = gathered.reshape(SIDE * BLOCK_TOKENS, 2 * HEAD_SIZE)

    weight = lax.dot_general(
        features, gathered, (((1,), (0,)), ((), ())), preferred_element_type=f32
    ).astype(jnp.bfloat16)
    weight = exchange(weight.reshape(SIDE, SIDE * BLOCK_TOKENS, 256), "y")
    weight = jnp.sum(weight.astype(f32), axis=0).astype(jnp.bfloat16)
    weight = exchange(weight.reshape(SIDE, BLOCK_TOKENS, 256), "z_hi")
    weight, spread = square_pass(weight)
    spread = spread_pass(exchange(spread, ("y", "head")))
    return finish_pass(exchange(spread, Z), weight)


def solution(mesh):
    devices = mesh.devices.reshape(4, 4, 4, 8)
    split = Mesh(devices, ("z_hi", "z_lo", "y", "head"))
    placed = (P(CTX, None),) + (P(CTX, "head"),) * 4 + (P(),)
    return jax.shard_map(
        per_device,
        mesh=split,
        in_specs=placed,
        out_specs=(P(CTX, "head"), P(CTX, "head")),
        check_vma=False,
    )
```

time: 208 us -> 207 us (level)
  starting transfers between devices: 51.2 us -> 67.4 us
  between operations: 15 us -> 0.9 us
  Pallas kernels: 15.1 us -> 22.1 us
  other arithmetic: 6.16 us -> 3.09 us
  waiting for transfers between devices: 21.8 us -> 18.8 us
  local copies, waits for them, and re-layouts: 3.82 us -> 1.68 us
    all_to_all x1 -> x4, starting transfers between devices: 3.41 us -> 22.2 us  [exchange(): return lax.all_to_all(value, axis, split_axis=0, concat_axis=0, tiled=True)]
    pallas_call x3 -> x7, Pallas kernels: 10.1 us -> 18.5 us  [the longest x2 5.33 us: grads_pass(): pl.pallas_call(functools.partial(grads_kernel, groups), out_shape=jax.Sha...]
    all_to_all x1 -> x4, waiting for transfers between devices: 5.25 us -> 1.81 us  [exchange(): return lax.all_to_all(value, axis, split_axis=0, concat_axis=0, tiled=True)]
    ppermute x6, starting transfers between devices: 47.7 us -> 45.1 us  [rotate(): lax.ppermute(value, axis, [(at, (at + steps) % count) for at in range(cou...]
    all_to_all x6 -> x5, blocking collectives: 91.7 us -> 89.7 us  [exchange(): return lax.all_to_all(value, axis, split_axis=0, concat_axis=0, tiled=True)]
  transfers between devices with their start and end apart: 9 -> 10, of which waited for: 6 -> 7; matrix products, arithmetic and copies ran while one was open for 2% -> 1% of each run, Pallas kernels for 7% -> 8%
where the time goes in v3:
time: 207 us; the launch traced here: 206 us
  blocking collectives  89.7 us (43%)
  starting transfers between devices  67.4 us (33%)
  Pallas kernels  22.1 us (11%)
  waiting for transfers between devices  18.8 us (9%)
  other arithmetic  3.09 us (1%)
  matrix products  2.34 us (1%)
    all_to_all x5, blocking collectives, exchange(): return lax.all_to_all(value, axis, split_axis=0, concat_axis=0, tiled=True)  89.7 us
    ppermute x6, starting transfers between devices, rotate(): lax.ppermute(value, axis, [(at, (at + steps) % count) for at in range(cou...  45.1 us
    all_to_all x4, starting transfers between devices, exchange(): return lax.all_to_all(value, axis, split_axis=0, concat_axis=0, tiled=True)  22.2 us
    ppermute x6, waiting for transfers between devices, rotate(): lax.ppermute(value, axis, [(at, (at + steps) % count) for at in range(cou...  17 us
    pallas_call x2, Pallas kernels, grads_pass(): pl.pallas_call(functools.partial(grads_kernel, groups), out_shape=jax.Sha...  5.33 us
    pallas_call x1, Pallas kernels, stats_pass(): pl.pallas_call(stats_kernel, out_shape=jax.ShapeDtypeStruct((SIDE, SIDE,...  4.19 us
  transfers between devices with their start and end apart: 10, of which 7 were waited for; matrix products, arithmetic and copies ran while one was open for 1% of the time, Pallas kernels for 8%

profile of v3, /device:TPU:1, one launch (start us, length us, event | category | flops | bytes accessed | tf_op | source)
XLA Modules:
  0.0 206.0 jit_solution(15961638608232013760)
XLA Ops:
  0.6 1.1 pad_maximum_fusion
  1.7 1.6 broadcast_in_dim.26
  3.3 5.1 %all-to-all-start.1 = ((bf16[4,2,128,1024]{3,2,1,0:T(8,128)(2,1)}), bf16[4,2,128,1024]{3,2,1,0:T(8,128)(2,1)S(1)}, u32[]{:S(2)}, u32[]{:S(2)}) async-start(bf16[4,2,128,1024]{3,2,1,0:T(8,128)(2,1)} %broadcast_in_dim.26), calls=%async_computation.1 | async-start | bytes 4194304 | tf_op jit(solution)/shard_map/all_to_all | solution.py:305
  8.5 0.0 copy-done.1
  8.5 0.0 copy-done.2
  8.5 8.8 %collective-permute-start = (bf16[1,128,256]{2,1,0:T(8,128)(2,1)S(1)}, bf16[1,128,256]{2,1,0:T(8,128)(2,1)S(1)}, u32[]{:S(2)}, u32[]{:S(2)}) collective-permute-start(bf16[1,128,256]{2,1,0:T(8,128)(2,1)S(1)} %maximum_bitcast_fusion), channel_id=1, source_target_pairs={{0,128},{32,160},{64,192},{96,224},{128,256},{160,288},{192,320},{... | collective-permute-start | bytes 196616 | tf_op jit(solution)/shard_map/ppermute | solution.py:45
  17.3 5.6 %collective-permute-done = bf16[1,128,256]{2,1,0:T(8,128)(2,1)S(1)} collective-permute-done((bf16[1,128,256]{2,1,0:T(8,128)(2,1)S(1)}, bf16[1,128,256]{2,1,0:T(8,128)(2,1)S(1)}, u32[]{:S(2)}, u32[]{:S(2)}) %collective-permute-start) | collective-permute-done | bytes 65568 | tf_op jit(solution)/shard_map/ppermute | solution.py:45
  22.9 6.1 %collective-permute-start.1 = (bf16[2,128,256]{2,1,0:T(8,128)(2,1)S(1)}, bf16[2,128,256]{2,1,0:T(8,128)(2,1)S(1)}, u32[]{:S(2)}, u32[]{:S(2)}) collective-permute-start(bf16[2,128,256]{2,1,0:T(8,128)(2,1)S(1)} %pad_maximum_fusion.2), channel_id=1, source_target_pairs={{0,64},{32,96},{64,128},{96,160},{128,192},{160,224},{192,256},{22... | collective-permute-start | bytes 393224 | tf_op jit(solution)/shard_map/ppermute | solution.py:45
  29.0 5.9 %collective-permute-done.1 = bf16[2,128,256]{2,1,0:T(8,128)(2,1)S(1)} collective-permute-done((bf16[2,128,256]{2,1,0:T(8,128)(2,1)S(1)}, bf16[2,128,256]{2,1,0:T(8,128)(2,1)S(1)}, u32[]{:S(2)}, u32[]{:S(2)}) %collective-permute-start.1) | collective-permute-done | bytes 131104 | tf_op jit(solution)/shard_map/ppermute | solution.py:45
  34.9 5.6 %collective-permute-start.2 = (bf16[3,128,256]{2,1,0:T(8,128)(2,1)S(1)}, bf16[3,128,256]{2,1,0:T(8,128)(2,1)S(1)}, u32[]{:S(2)}, u32[]{:S(2)}) collective-permute-start(bf16[3,128,256]{2,1,0:T(8,128)(2,1)S(1)} %pad_maximum_fusion.1), channel_id=1, source_target_pairs={{0,32},{32,64},{64,96},{96,128},{128,160},{160,192},{192,224},{224... | collective-permute-start | bytes 589832 | tf_op jit(solution)/shard_map/ppermute | solution.py:45
  40.5 0.6 pad_add_fusion.pick_ref
  41.1 3.6 %pick.1 = bf16[4,128,256]{2,1,0:T(8,128)(2,1)} custom-call(s32[2]{0:T(128)} %pad_add_fusion.pick_ref, bf16[128,8192]{1,0:T(8,128)(2,1)} %right_ref.1, bf16[128,8192]{1,0:T(8,128)(2,1)} %right_ref.1), custom_call_target="tpu_custom_call" | custom-call | tf_op jit(solution)/shard_map/pick/pallas_call | solution.py:230
  44.8 0.0 collective-permute-done.2
  44.8 0.0 all-to-all-done.1.row_ref
  44.8 3.4 %all-to-all-start = ((bf16[4,128,256]{2,1,0:T(8,128)(2,1)}), bf16[4,128,256]{2,1,0:T(8,128)(2,1)S(1)}, u32[]{:S(2)}, u32[]{:S(2)}) async-start(bf16[4,128,256]{2,1,0:T(8,128)(2,1)} %pick.1), calls=%async_computation | async-start | bytes 524288 | tf_op jit(solution)/shard_map/all_to_all | solution.py:305
  48.2 0.0 copy-done.3
  48.2 0.2 reduce-window.8
  48.4 0.2 select_reduce_fusion
  48.6 0.1 pad_add_fusion.1.info_ref
  48.7 4.2 %stats.1 = f32[4,4,2,1024]{3,2,1,0:T(2,128)} custom-call(s32[6]{0:T(128)S(1)} %pad_add_fusion.1.info_ref, bf16[4,2,128,1024]{3,2,1,0:T(8,128)(2,1)S(1)} %all-to-all-done.1.row_ref, bf16[7,128,256]{2,1,0:T(8,128)(2,1)S(1)} %constant_dynamic-update-slice_fusion.kv_ref), custom_call_target="tpu_custom_call" | custom-call | tf_op jit(solution)/shard_map/stats/pallas_call | solution.py:184
  52.9 1.0 all-to-all-done
  53.8 4.2 %all-to-all-start.2 = ((f32[4,4,2,1024]{3,2,1,0:T(2,128)}), f32[4,4,2,1024]{3,2,1,0:T(2,128)S(1)}, u32[]{:S(2)}, u32[]{:S(2)}) async-start(f32[4,4,2,1024]{3,2,1,0:T(2,128)} %stats.1), calls=%async_computation.2 | async-start | bytes 262144 | tf_op jit(solution)/shard_map/all_to_all | solution.py:305
  58.0 0.0 copy-done
  58.0 4.0 %fan.1 = bf16[8,512,256]{2,1,0:T(8,128)(2,1)} custom-call(bf16[512,256]{1,0:T(8,128)(2,1)} %bitcast.26), custom_call_target="tpu_custom_call" | custom-call | tf_op jit(solution)/shard_map/fan/pallas_call | solution.py:286
  62.0 0.9 all-to-all-done.2.stats_ref
  62.8 9.5 %all-to-all-start.3 = ((bf16[8,512,256]{2,1,0:T(8,128)(2,1)}), bf16[8,512,256]{2,1,0:T(8,128)(2,1)}, u32[]{:S(2)}, u32[]{:S(2)}) async-start(bf16[8,512,256]{2,1,0:T(8,128)(2,1)} %fan.1), calls=%async_computation.3 | async-start | bytes 4194304 | tf_op jit(solution)/shard_map/all_to_all | solution.py:305
  72.3 1.2 grads4.1
  73.5 8.2 %collective-permute-start.3 = (bf16[3,128,256]{2,1,0:T(8,128)(2,1)S(1)}, bf16[3,128,256]{2,1,0:T(8,128)(2,1)S(1)}, u32[]{:S(2)}, u32[]{:S(2)}) collective-permute-start(bf16[3,128,256]{2,1,0:T(8,128)(2,1)S(1)} %grads4.1), channel_id=1, source_target_pairs={{0,480},{32,0},{64,32},{96,64},{128,96},{160,128},{192,160},{224,1... | collective-permute-start | bytes 589832 | tf_op jit(solution)/shard_map/ppermute | solution.py:45
  81.7 4.2 %grads0.1 = f32[4,128,256]{2,1,0:T(8,128)S(1)} custom-call(s32[6]{0:T(128)S(1)} %pad_add_fusion.1.info_ref, bf16[4,2,128,1024]{3,2,1,0:T(8,128)(2,1)S(1)} %all-to-all-done.1.row_ref, bf16[7,128,256]{2,1,0:T(8,128)(2,1)S(1)} %constant_dynamic-update-slice_fusion.kv_ref, f32[4,4,2,1024]{3,2,1,0:T(2,128)S(1)} %all-to-all-done.2.stats_ref), custom_call_target="tpu_custom_call" | custom-call | tf_op jit(solution)/shard_map/grads0/pallas_call | solution.py:202
  85.9 0.1 collective-permute-done.3
  86.1 9.9 %collective-permute-start.4 = (bf16[2,128,256]{2,1,0:T(8,128)(2,1)S(1)}, bf16[2,128,256]{2,1,0:T(8,128)(2,1)S(1)}, u32[]{:S(2)}, u32[]{:S(2)}) collective-permute-start(bf16[2,128,256]{2,1,0:T(8,128)(2,1)S(1)} %pad_maximum_fusion.3), channel_id=1, source_target_pairs={{0,448},{32,480},{64,0},{96,32},{128,64},{160,96},{192,128},{224,1... | collective-permute-start | bytes 393224 | tf_op jit(solution)/shard_map/ppermute | solution.py:45
  96.1 3.3 %collective-permute-done.4 = bf16[2,128,256]{2,1,0:T(8,128)(2,1)S(1)} collective-permute-done((bf16[2,128,256]{2,1,0:T(8,128)(2,1)S(1)}, bf16[2,128,256]{2,1,0:T(8,128)(2,1)S(1)}, u32[]{:S(2)}, u32[]{:S(2)}) %collective-permute-start.4) | collective-permute-done | bytes 131104 | tf_op jit(solution)/shard_map/ppermute | solution.py:45
  99.5 6.5 %collective-permute-start.5 = (bf16[128,256]{1,0:T(8,128)(2,1)S(1)}, bf16[128,256]{1,0:T(8,128)(2,1)S(1)}, u32[]{:S(2)}, u32[]{:S(2)}) collective-permute-start(bf16[128,256]{1,0:T(8,128)(2,1)S(1)} %fusion.4), channel_id=1, source_target_pairs={{0,384},{32,416},{64,448},{96,480},{128,0},{160,32},{192,64},{224,... | collective-permute-start | bytes 196616 | tf_op jit(solution)/shard_map/ppermute | solution.py:45
  106.0 0.3 multiply_sine_fusion
  106.3 2.1 %collective-permute-done.5 = bf16[128,256]{1,0:T(8,128)(2,1)S(1)} collective-permute-done((bf16[128,256]{1,0:T(8,128)(2,1)S(1)}, bf16[128,256]{1,0:T(8,128)(2,1)S(1)}, u32[]{:S(2)}, u32[]{:S(2)}) %collective-permute-start.5) | collective-permute-done | bytes 65568 | tf_op jit(solution)/shard_map/ppermute | solution.py:45
  108.4 0.0 all-to-all-done.3
  108.4 0.1 slice_negate_fusion
  108.5 0.1 fusion.6
  108.7 16.4 %all_to_all.45 = bf16[4,128,256]{2,1,0:T(8,128)(2,1)S(1)} all-to-all(bf16[4,128,256]{2,1,0:T(8,128)(2,1)S(1)} %broadcast_in_dim.27), channel_id=1, replica_groups=mesh['z_hi'=4,'z_lo'=4,'y'=4,'head'=8] {'z_lo'}, dimensions={0} | all-to-all | bytes 524288 | tf_op jit(solution)/shard_map/all_to_all | solution.py:305
  125.1 2.3 %convolution_convert_fusion = bf16[8,256,256]{2,1,0:T(8,128)(2,1)S(1)} fusion(bf16[8,512,256]{2,1,0:T(8,128)(2,1)} %all-to-all-done.3, bf16[512,256,1]{1,0,2:T(8,128)(2,1)S(1)} %bitcast.29), kind=kOutput, calls=%fused_computation | convolution fusion | flops 537395200 | bytes 3407872 | tf_op jit(solution)/shard_map/dot_general | solution.py:358
  127.5 15.1 %all_to_all.46 = bf16[4,512,256]{2,1,0:T(8,128)(2,1)S(1)} all-to-all(bf16[4,512,256]{2,1,0:T(8,128)(2,1)S(1)} %bitcast.28), channel_id=1, replica_groups=mesh['z_hi'=4,'z_lo'=4,'y'=4,'head'=8] {'y'}, dimensions={0} | all-to-all | bytes 2097152 | tf_op jit(solution)/shard_map/all_to_all | solution.py:305
  142.6 0.3 reduce_sum.12
  142.9 23.6 %all_to_all.47.parts_ref = bf16[4,128,256]{2,1,0:T(8,128)(2,1)} all-to-all(bf16[4,128,256]{2,1,0:T(8,128)(2,1)S(1)} %bitcast.27), channel_id=1, replica_groups=mesh['z_hi'=4,'z_lo'=4,'y'=4,'head'=8] {'z_hi'}, dimensions={0} | all-to-all | bytes 524288 | tf_op jit(solution)/shard_map/all_to_all | solution.py:305
  166.5 1.7 square.1
  168.1 18.7 %all_to_all.48.parts_ref = f32[32,8,128]{2,1,0:T(8,128)} all-to-all(f32[32,8,128]{2,1,0:T(8,128)} %get-tuple-element.18), channel_id=1, replica_groups=mesh['z_hi'=4,'z_lo'=4,'y'=4,'head'=8] {'y','head'}, dimensions={0} | all-to-all | bytes 262144 | tf_op jit(solution)/shard_map/all_to_all | solution.py:305
  186.9 1.6 spread.1
  188.5 15.8 %all_to_all.49.parts_ref = f32[16,8,128]{2,1,0:T(8,128)} all-to-all(f32[16,8,128]{2,1,0:T(8,128)} %spread.1), channel_id=1, replica_groups=mesh['z_hi'=4,'z_lo'=4,'y'=4,'head'=8] {'z_hi','z_lo'}, dimensions={0} | all-to-all | bytes 131072 | tf_op jit(solution)/shard_map/all_to_all | solution.py:305
  204.3 1.7 finish.1
  (25 shorter events, 0.3 us)
Async XLA Ops:
  3.3 5.2 %copy-start.1 = (bf16[128,128]{1,0:T(8,128)(2,1)S(1)}, bf16[128,128]{1,0:T(8,128)(2,1)}, u32[]{:S(2)}) copy-start(bf16[128,128]{1,0:T(8,128)(2,1)} %param.9) | copy-start | bytes 98308
  3.3 5.2 %copy-start.2 = (bf16[128,128]{1,0:T(8,128)(2,1)S(1)}, bf16[128,128]{1,0:T(8,128)(2,1)}, u32[]{:S(2)}) copy-start(bf16[128,128]{1,0:T(8,128)(2,1)} %param.8) | copy-start | bytes 98308
  3.3 41.5 %all-to-all-start.1 = ((bf16[4,2,128,1024]{3,2,1,0:T(8,128)(2,1)}), bf16[4,2,128,1024]{3,2,1,0:T(8,128)(2,1)S(1)}, u32[]{:S(2)}, u32[]{:S(2)}) async-start(bf16[4,2,128,1024]{3,2,1,0:T(8,128)(2,1)} %broadcast_in_dim.26), calls=%async_computation.1 | async-start | bytes 4194304 | tf_op jit(solution)/shard_map/all_to_all | solution.py:305
  8.5 14.4 %collective-permute-start = (bf16[1,128,256]{2,1,0:T(8,128)(2,1)S(1)}, bf16[1,128,256]{2,1,0:T(8,128)(2,1)S(1)}, u32[]{:S(2)}, u32[]{:S(2)}) collective-permute-start(bf16[1,128,256]{2,1,0:T(8,128)(2,1)S(1)} %maximum_bitcast_fusion), channel_id=1, source_target_pairs={{0,128},{32,160},{64,192},{96,224},{128,256},{160,288},{192,320},{... | collective-permute-start | bytes 196616 | tf_op jit(solution)/shard_map/ppermute | solution.py:45
  22.9 12.0 %collective-permute-start.1 = (bf16[2,128,256]{2,1,0:T(8,128)(2,1)S(1)}, bf16[2,128,256]{2,1,0:T(8,128)(2,1)S(1)}, u32[]{:S(2)}, u32[]{:S(2)}) collective-permute-start(bf16[2,128,256]{2,1,0:T(8,128)(2,1)S(1)} %pad_maximum_fusion.2), channel_id=1, source_target_pairs={{0,64},{32,96},{64,128},{96,160},{128,192},{160,224},{192,256},{22... | collective-permute-start | bytes 393224 | tf_op jit(solution)/shard_map/ppermute | solution.py:45
  34.9 9.8 %collective-permute-start.2 = (bf16[3,128,256]{2,1,0:T(8,128)(2,1)S(1)}, bf16[3,128,256]{2,1,0:T(8,128)(2,1)S(1)}, u32[]{:S(2)}, u32[]{:S(2)}) collective-permute-start(bf16[3,128,256]{2,1,0:T(8,128)(2,1)S(1)} %pad_maximum_fusion.1), channel_id=1, source_target_pairs={{0,32},{32,64},{64,96},{96,128},{128,160},{160,192},{192,224},{224... | collective-permute-start | bytes 589832 | tf_op jit(solution)/shard_map/ppermute | solution.py:45
  41.1 7.1 %copy-start.3 = (s32[5]{0:T(128)S(1)}, s32[5]{0:T(128)}, u32[]{:S(2)}) copy-start(s32[5]{0:T(128)} %param.11) | copy-start | bytes 64
  44.8 9.1 %all-to-all-start = ((bf16[4,128,256]{2,1,0:T(8,128)(2,1)}), bf16[4,128,256]{2,1,0:T(8,128)(2,1)S(1)}, u32[]{:S(2)}, u32[]{:S(2)}) async-start(bf16[4,128,256]{2,1,0:T(8,128)(2,1)} %pick.1), calls=%async_computation | async-start | bytes 524288 | tf_op jit(solution)/shard_map/all_to_all | solution.py:305
  53.8 4.2 %copy-start = (bf16[4,128,256]{2,1,0:T(8,128)(2,1)}, bf16[4,128,256]{2,1,0:T(8,128)(2,1)S(1)}, u32[]{:S(2)}) copy-start(bf16[4,128,256]{2,1,0:T(8,128)(2,1)S(1)} %all-to-all-done) | copy-start | bytes 786436
  53.8 9.0 %all-to-all-start.2 = ((f32[4,4,2,1024]{3,2,1,0:T(2,128)}), f32[4,4,2,1024]{3,2,1,0:T(2,128)S(1)}, u32[]{:S(2)}, u32[]{:S(2)}) async-start(f32[4,4,2,1024]{3,2,1,0:T(2,128)} %stats.1), calls=%async_computation.2 | async-start | bytes 262144 | tf_op jit(solution)/shard_map/all_to_all | solution.py:305
  62.8 45.6 %all-to-all-start.3 = ((bf16[8,512,256]{2,1,0:T(8,128)(2,1)}), bf16[8,512,256]{2,1,0:T(8,128)(2,1)}, u32[]{:S(2)}, u32[]{:S(2)}) async-start(bf16[8,512,256]{2,1,0:T(8,128)(2,1)} %fan.1), calls=%async_computation.3 | async-start | bytes 4194304 | tf_op jit(solution)/shard_map/all_to_all | solution.py:305
  73.5 12.5 %collective-permute-start.3 = (bf16[3,128,256]{2,1,0:T(8,128)(2,1)S(1)}, bf16[3,128,256]{2,1,0:T(8,128)(2,1)S(1)}, u32[]{:S(2)}, u32[]{:S(2)}) collective-permute-start(bf16[3,128,256]{2,1,0:T(8,128)(2,1)S(1)} %grads4.1), channel_id=1, source_target_pairs={{0,480},{32,0},{64,32},{96,64},{128,96},{160,128},{192,160},{224,1... | collective-permute-start | bytes 589832 | tf_op jit(solution)/shard_map/ppermute | solution.py:45
  86.1 13.3 %collective-permute-start.4 = (bf16[2,128,256]{2,1,0:T(8,128)(2,1)S(1)}, bf16[2,128,256]{2,1,0:T(8,128)(2,1)S(1)}, u32[]{:S(2)}, u32[]{:S(2)}) collective-permute-start(bf16[2,128,256]{2,1,0:T(8,128)(2,1)S(1)} %pad_maximum_fusion.3), channel_id=1, source_target_pairs={{0,448},{32,480},{64,0},{96,32},{128,64},{160,96},{192,128},{224,1... | collective-permute-start | bytes 393224 | tf_op jit(solution)/shard_map/ppermute | solution.py:45
  99.5 8.9 %collective-permute-start.5 = (bf16[128,256]{1,0:T(8,128)(2,1)S(1)}, bf16[128,256]{1,0:T(8,128)(2,1)S(1)}, u32[]{:S(2)}, u32[]{:S(2)}) collective-permute-start(bf16[128,256]{1,0:T(8,128)(2,1)S(1)} %fusion.4), channel_id=1, source_target_pairs={{0,384},{32,416},{64,448},{96,480},{128,0},{160,32},{192,64},{224,... | collective-permute-start | bytes 196616 | tf_op jit(solution)/shard_map/ppermute | solution.py:45

commit v4 on v3

--- a/solution.py
+++ b/solution.py
@@ -18,8 +18,8 @@
 SIDE = 4
 STATS = 2
 ORDER = (0, 2, 4, 6, 1, 3, 5)
-EVEN_GROUPS = ((0, 2), (2, 4))
-ODD_GROUPS = ((4, 6), (6, 7))
+EVEN_GROUPS = ((0, 4),)
+ODD_GROUPS = ((4, 7),)
 NEGATIVE = -1e30
 SCALE = HEAD_SIZE ** (-0.5)
 LOG2E = 1.4426950408889634
@@ -86,8 +86,16 @@
     return score, dprob
 
 
-def stats_kernel(info_ref, row_ref, kv_ref, out_ref, qs_ref, gs_ref, run_ref):
-    query_row = pl.program_id(0)
+def stats_kernel(first_turn, info_ref, row_ref, kv_ref, *refs):
+    out_ref, qs_ref, gs_ref, run_ref = refs[-4:]
+    if first_turn:
+
+        @pl.when(pl.program_id(0) == 0)
+        def _():
+            for target in range(SIDE):
+                out_ref[target, info_ref[1]] = refs[0][0]
+
+    query_row = (info_ref[1] - first_turn - pl.program_id(0)) & (SIDE - 1)
     stack_heads(row_ref, 0, qs_ref)
     stack_heads(row_ref, 1, gs_ref)
     run_ref[0:1, :] = jnp.full((1, ROWS), NEGATIVE, jnp.float32)
@@ -114,9 +122,13 @@
     safe = jnp.where(some, total, 1.0)
     lse = jnp.where(some, run_ref[0:1, :] * EXP_SCALE + jnp.log2(safe), NEGATIVE)
     mean = run_ref[2:3, :] / safe
-    for target in range(SIDE):
-        out_ref[target, 0, 0:1, :] = lse
-        out_ref[target, 0, 1:2, :] = mean
+    if first_turn:
+        for target in range(SIDE):
+            out_ref[target, query_row, 0:1, :] = lse
+            out_ref[target, query_row, 1:2, :] = mean
+    else:
+        out_ref[0, 0:1, :] = lse
+        out_ref[0, 1:2, :] = mean
 
 
 def grads_kernel(groups, info_ref, row_ref, kv_ref, stats_ref, out_ref, qs_ref, gs_ref, acc_ref):
@@ -165,29 +177,36 @@
 ]
 PARAMS = pltpu.CompilerParams(vmem_limit_bytes=40 * 1024 * 1024)
 ROW_SHAPE = (1, 2, BLOCK_TOKENS, GROUP * HEAD_SIZE)
-ROW_SPEC = pl.BlockSpec(ROW_SHAPE, lambda step, info: (step, 0, 0, 0))
-STATS_SPEC = pl.BlockSpec((SIDE, 1, STATS, ROWS), lambda step, info: (0, step, 0, 0))
+OWN_STATS = (1, STATS, ROWS)
+ALL_STATS = (SIDE, SIDE, STATS, ROWS)
 
 
 def whole(shape):
     return pl.BlockSpec(shape, lambda step, info: (0,) * len(shape))
 
 
-def stats_pass(info, rows, kv):
+def stats_pass(first_turn, info, rows, kv, *before):
+    shape = ALL_STATS if first_turn else OWN_STATS
+
+    def row_map(step, info):
+        row = (info[1] - first_turn - step) & (SIDE - 1) if first_turn else 0
+        return (row, 0, 0, 0)
+
     spec = pltpu.PrefetchScalarGridSpec(
         num_scalar_prefetch=1,
-        grid=(SIDE,),
-        in_specs=[ROW_SPEC, whole(kv.shape)],
-        out_specs=STATS_SPEC,
+        grid=(SIDE - 1 if first_turn else 1,),
+        in_specs=[pl.BlockSpec(ROW_SHAPE, row_map), whole(kv.shape)]
+        + [whole(OWN_STATS) for _ in before],
+        out_specs=whole(shape),
         scratch_shapes=STACKS + [pltpu.VMEM((8, ROWS), jnp.float32)],
     )
     return pl.pallas_call(
-        stats_kernel,
-        out_shape=jax.ShapeDtypeStruct((SIDE, SIDE, STATS, ROWS), jnp.float32),
+        functools.partial(stats_kernel, first_turn),
+        out_shape=jax.ShapeDtypeStruct(shape, jnp.float32),
         grid_spec=spec,
         compiler_params=PARAMS,
-        name="stats",
-    )(info, rows, kv)
+        name="stats" + str(first_turn),
+    )(info, rows, kv, *before)
 
 
 def grads_pass(groups, dtype, info, rows, kv, stats):
@@ -195,7 +214,11 @@
     spec = pltpu.PrefetchScalarGridSpec(
         num_scalar_prefetch=1,
         grid=(SIDE,),
-        in_specs=[ROW_SPEC, whole(kv.shape), STATS_SPEC],
+        in_specs=[
+            pl.BlockSpec(ROW_SHAPE, lambda step, info: (step, 0, 0, 0)),
+            whole(kv.shape),
+            pl.BlockSpec((SIDE, 1, STATS, ROWS), lambda step, info: (0, step, 0, 0)),
+        ],
         out_specs=whole(shape),
         scratch_shapes=STACKS + [pltpu.VMEM(shape, jnp.float32)],
     )
@@ -277,22 +300,6 @@
     return pl.pallas_call(finish_kernel, out_shape=(shape, shape), name="finish")(parts, weight)
 
 
-def fan_kernel(src_ref, out_ref):
-    out_ref[0] = src_ref[...]
-
-
-def fan_out(tokens, copies):
-    rows, width = tokens.shape
-    return pl.pallas_call(
-        fan_kernel,
-        grid=(copies,),
-        out_shape=jax.ShapeDtypeStruct((copies, rows, width), tokens.dtype),
-        in_specs=[pl.BlockSpec((rows, width), lambda copy: (0, 0))],
-        out_specs=pl.BlockSpec((1, rows, width), lambda copy: (copy, 0, 0)),
-        name="fan",
-    )(tokens)
-
-
 def rotary_tables(positions):
     half = HEAD_SIZE // 2
     freqs = 500000.0 ** (-(jnp.arange(half, dtype=jnp.float32) * 2.0) / HEAD_SIZE)
@@ -310,28 +317,31 @@
     row = lax.axis_index("y")
     head = lax.axis_index("head")
     ends = jnp.cumsum(doc_blocks)
-    blocks = SIDE * z + jnp.arange(SIDE)
-    firsts = jnp.max(jnp.where(ends[None, :] <= blocks[:, None], ends[None, :], 0), axis=1)
+    rows = SIDE * z + jnp.arange(SIDE)
+    firsts = jnp.max(jnp.where(ends[None, :] <= rows[:, None], ends[None, :], 0), axis=1)
     info = jnp.concatenate([jnp.stack([z, row]), firsts]).astype(jnp.int32)
     here = SIDE * z + row
     f32 = jnp.float32
 
     own = jnp.concatenate([keys, values], axis=1)[None]
     four = rotate(own, Z, 4)
-    rows = jnp.stack([queries, output_gradient])
-    query_rows = exchange(jnp.broadcast_to(rows, (SIDE,) + rows.shape), "y")
+    own_row = jnp.stack([queries, output_gradient])
+    query_rows = lax.all_gather(own_row, "y")
+    query_rows = pltpu.with_memory_space_constraint(query_rows, pltpu.HBM)
     even = jnp.concatenate([own, four])
     two = rotate(even, Z, 2)
     odd = rotate(jnp.concatenate([own, two[0:1], four]), Z, 1)
     column = jnp.concatenate([own, two[0:1], four, two[1:2], odd])
 
-    picked, odd = lax.optimization_barrier((pick_features(hidden, head), odd))
-    tokens = exchange(picked, "z_lo").reshape(SIDE * BLOCK_TOKENS, 256)
-    stats = stats_pass(info, query_rows, column)
+    stats = stats_pass(0, info, own_row[None], column)
+    picked = pick_features(hidden, head)
+    picked, _ = lax.optimization_barrier((picked, odd))
+    tokens = exchange(picked, "z_lo")
+    stats = stats_pass(1, info, query_rows, column, stats)
     tokens, stats = lax.optimization_barrier((tokens, stats))
+    features = lax.all_gather(tokens.reshape(SIDE * BLOCK_TOKENS, 256), "head", axis=0)
+
     stats = exchange(stats, "y")
-    tokens, stats = lax.optimization_barrier((fan_out(tokens, 8), stats))
-    features = exchange(tokens, "head")
     odd_grads = grads_pass(ODD_GROUPS, jnp.bfloat16, info, query_rows, column, stats)
     odd_back = rotate(odd_grads, Z, -1)
     even_grads = grads_pass(EVEN_GROUPS, f32, info, query_rows, column, stats)
@@ -342,9 +352,8 @@
     two_back = rotate(jnp.stack([s2, even_grads[3]]).astype(jnp.bfloat16), Z, -2).astype(f32)
     s0 = s0 + two_back[0]
     s4 = s4 + two_back[1]
-    four_back = rotate(s4.astype(jnp.bfloat16), Z, -4)
-    features, four_back = lax.optimization_barrier((features, four_back))
-    s0 = s0 + four_back.astype(f32)
+    four_back = rotate(s4.astype(jnp.bfloat16), Z, -4).astype(f32)
+    s0 = s0 + four_back
 
     cosine, sine = rotary_tables(here * BLOCK_TOKENS + jnp.arange(BLOCK_TOKENS))
     key_grad = s0[:, :HEAD_SIZE]

time: 207 us -> 203 us (0.981)
  starting transfers between devices: 67.4 us -> 47.1 us
  between operations: 0.9 us -> 14.4 us
  Pallas kernels: 22.1 us -> 25.8 us
    all_to_all x4 -> x1, starting transfers between devices: 22.2 us -> 3.41 us  [exchange(): return lax.all_to_all(value, axis, split_axis=0, concat_axis=0, tiled=True)]
    pallas_call x2, Pallas kernels: 5.33 us -> 10.6 us  [grads_pass(): pl.pallas_call(functools.partial(grads_kernel, groups), out_shape=jax.Sha...]
    all_to_all x5 -> x6, blocking collectives: 89.7 us -> 88.3 us  [exchange(): return lax.all_to_all(value, axis, split_axis=0, concat_axis=0, tiled=True)]
  transfers between devices with their start and end apart: 10 -> 9, of which waited for: 7 -> 5; matrix products, arithmetic and copies ran while one was open for 1% -> 1% of each run, Pallas kernels for 8% -> 10%
where the time goes in v4:
time: 203 us; the launch traced here: 202 us
  blocking collectives  88.3 us (43%)
  starting transfers between devices  47.1 us (23%)
  Pallas kernels  25.8 us (13%)
  waiting for transfers between devices  19.8 us (10%)
  between operations  14.4 us (7%)
  other arithmetic  4.01 us (2%)
  matrix products  2.34 us (1%)
    all_to_all x6, blocking collectives, exchange(): return lax.all_to_all(value, axis, split_axis=0, concat_axis=0, tiled=True)  88.3 us
    ppermute x6, starting transfers between devices, rotate(): lax.ppermute(value, axis, [(at, (at + steps) % count) for at in range(cou...  43.6 us
    ppermute x6, waiting for transfers between devices, rotate(): lax.ppermute(value, axis, [(at, (at + steps) % count) for at in range(cou...  17.9 us
    pallas_call x2, Pallas kernels, grads_pass(): pl.pallas_call(functools.partial(grads_kernel, groups), out_shape=jax.Sha...  10.6 us
    pallas_call x2, Pallas kernels, stats_pass(): pl.pallas_call(functools.partial(stats_kernel, first_turn), out_shape=jax...  6.53 us
  transfers between devices with their start and end apart: 9, of which 5 were waited for; matrix products, arithmetic and copies ran while one was open for 1% of the time, Pallas kernels for 10%

profile of v4, /device:TPU:1, one launch (start us, length us, event | category | flops | bytes accessed | tf_op | source)
XLA Modules:
  0.0 202.4 jit_solution(9052849026833768925)
XLA Ops:
  7.2 0.0 copy-start.2
  7.2 0.0 copy-start.1
  7.2 0.0 all-gather.6.cloned.1.call-start
  7.2 1.9 fusion.7
  9.1 0.0 all-gather.6.cloned.1.call-update
  9.2 0.0 copy-done.2
  9.2 0.0 copy-done.1
  9.2 9.6 %collective-permute-start = (bf16[1,128,256]{2,1,0:T(8,128)(2,1)S(1)}, bf16[1,128,256]{2,1,0:T(8,128)(2,1)S(1)}, u32[]{:S(2)}, u32[]{:S(2)}) collective-permute-start(bf16[1,128,256]{2,1,0:T(8,128)(2,1)S(1)} %maximum_bitcast_fusion), channel_id=1, source_target_pairs={{0,128},{32,160},{64,192},{96,224},{128,256},{160,288},{192,320},{... | collective-permute-start | bytes 196616 | tf_op jit(solution)/shard_map/ppermute | solution.py:45
  18.8 5.6 %collective-permute-done = bf16[1,128,256]{2,1,0:T(8,128)(2,1)S(1)} collective-permute-done((bf16[1,128,256]{2,1,0:T(8,128)(2,1)S(1)}, bf16[1,128,256]{2,1,0:T(8,128)(2,1)S(1)}, u32[]{:S(2)}, u32[]{:S(2)}) %collective-permute-start) | collective-permute-done | bytes 65568 | tf_op jit(solution)/shard_map/ppermute | solution.py:45
  24.4 6.1 %collective-permute-start.1 = (bf16[2,128,256]{2,1,0:T(8,128)(2,1)S(1)}, bf16[2,128,256]{2,1,0:T(8,128)(2,1)S(1)}, u32[]{:S(2)}, u32[]{:S(2)}) collective-permute-start(bf16[2,128,256]{2,1,0:T(8,128)(2,1)S(1)} %pad_maximum_fusion.2), channel_id=1, source_target_pairs={{0,64},{32,96},{64,128},{96,160},{128,192},{160,224},{192,256},{22... | collective-permute-start | bytes 393224 | tf_op jit(solution)/shard_map/ppermute | solution.py:45
  30.6 5.5 %collective-permute-done.1 = bf16[2,128,256]{2,1,0:T(8,128)(2,1)S(1)} collective-permute-done((bf16[2,128,256]{2,1,0:T(8,128)(2,1)S(1)}, bf16[2,128,256]{2,1,0:T(8,128)(2,1)S(1)}, u32[]{:S(2)}, u32[]{:S(2)}) %collective-permute-start.1) | collective-permute-done | bytes 131104 | tf_op jit(solution)/shard_map/ppermute | solution.py:45
  36.2 6.0 %collective-permute-start.2 = (bf16[3,128,256]{2,1,0:T(8,128)(2,1)S(1)}, bf16[3,128,256]{2,1,0:T(8,128)(2,1)S(1)}, u32[]{:S(2)}, u32[]{:S(2)}) collective-permute-start(bf16[3,128,256]{2,1,0:T(8,128)(2,1)S(1)} %pad_maximum_fusion.1), channel_id=1, source_target_pairs={{0,32},{32,64},{64,96},{96,128},{128,160},{160,192},{192,224},{224... | collective-permute-start | bytes 589832 | tf_op jit(solution)/shard_map/ppermute | solution.py:45
  42.2 0.7 pad_add_fusion.pick_ref
  42.9 3.6 %pick.1 = bf16[4,128,256]{2,1,0:T(8,128)(2,1)} custom-call(s32[2]{0:T(128)} %pad_add_fusion.pick_ref, bf16[128,8192]{1,0:T(8,128)(2,1)} %right_ref.1, bf16[128,8192]{1,0:T(8,128)(2,1)} %right_ref.1), custom_call_target="tpu_custom_call" | custom-call | tf_op jit(solution)/shard_map/pick/pallas_call | solution.py:253
  46.5 0.0 collective-permute-done.2
  46.5 3.4 %all-to-all-start = ((bf16[4,128,256]{2,1,0:T(8,128)(2,1)}), bf16[4,128,256]{2,1,0:T(8,128)(2,1)S(1)}, u32[]{:S(2)}, u32[]{:S(2)}) async-start(bf16[4,128,256]{2,1,0:T(8,128)(2,1)} %pick.1), calls=%async_computation | async-start | bytes 524288 | tf_op jit(solution)/shard_map/all_to_all | solution.py:312
  49.9 0.0 all-gather.4.cloned.1.call-start
  50.0 0.2 reduce-window.8
  50.2 0.2 select_reduce_fusion
  50.4 0.1 pad_add_fusion.1.info_ref
  50.5 1.6 stats0.1.refs_0_
  52.1 1.9 all-gather.6.cloned.1.call-done
  54.0 4.9 %stats1.1 = f32[4,4,2,1024]{3,2,1,0:T(2,128)S(1)} custom-call(s32[6]{0:T(128)S(1)} %pad_add_fusion.1.info_ref, bf16[4,2,128,1024]{3,2,1,0:T(8,128)(2,1)} %bitcast.29, bf16[7,128,256]{2,1,0:T(8,128)(2,1)S(1)} %constant_dynamic-update-slice_fusion.kv_ref, f32[1,2,1024]{2,1,0:T(2,128)S(1)} %stats0.1.refs_0_), custom_call_target="tpu_custom_call" | custom-call | tf_op jit(solution)/shard_map/stats1/pallas_call | solution.py:203
  58.9 0.0 all-to-all-done
  58.9 0.7 copy-done
  59.6 0.0 all-gather.4.cloned.1.call-update
  59.7 7.2 %all_to_all.35.stats_ref = f32[4,4,2,1024]{3,2,1,0:T(2,128)S(1)} all-to-all(f32[4,4,2,1024]{3,2,1,0:T(2,128)S(1)} %stats1.1), channel_id=1, replica_groups=mesh['z_hi'=4,'z_lo'=4,'y'=4,'head'=8] {'y'}, dimensions={0} | all-to-all | bytes 262144 | tf_op jit(solution)/shard_map/all_to_all | solution.py:312
  66.9 3.1 %grads4.1 = bf16[3,128,256]{2,1,0:T(8,128)(2,1)S(1)} custom-call(s32[6]{0:T(128)S(1)} %pad_add_fusion.1.info_ref, bf16[4,2,128,1024]{3,2,1,0:T(8,128)(2,1)} %bitcast.30, bf16[7,128,256]{2,1,0:T(8,128)(2,1)S(1)} %constant_dynamic-update-slice_fusion.kv_ref, f32[4,4,2,1024]{3,2,1,0:T(2,128)S(1)} %all_to_all.35.stats_ref), custom_call_target="tpu_custom_call" | custom-call | tf_op jit(solution)/shard_map/grads4/pallas_call | solution.py:225
  70.0 11.1 %collective-permute-start.3 = (bf16[3,128,256]{2,1,0:T(8,128)(2,1)S(1)}, bf16[3,128,256]{2,1,0:T(8,128)(2,1)S(1)}, u32[]{:S(2)}, u32[]{:S(2)}) collective-permute-start(bf16[3,128,256]{2,1,0:T(8,128)(2,1)S(1)} %grads4.1), channel_id=1, source_target_pairs={{0,480},{32,0},{64,32},{96,64},{128,96},{160,128},{192,160},{224,1... | collective-permute-start | bytes 589832 | tf_op jit(solution)/shard_map/ppermute | solution.py:45
  81.1 7.5 %grads0.1 = f32[4,128,256]{2,1,0:T(8,128)S(1)} custom-call(s32[6]{0:T(128)S(1)} %pad_add_fusion.1.info_ref, bf16[4,2,128,1024]{3,2,1,0:T(8,128)(2,1)} %bitcast.31, bf16[7,128,256]{2,1,0:T(8,128)(2,1)S(1)} %constant_dynamic-update-slice_fusion.kv_ref, f32[4,4,2,1024]{3,2,1,0:T(2,128)S(1)} %all_to_all.35.stats_ref), custom_call_target="tpu_custom_call" | custom-call | tf_op jit(solution)/shard_map/grads0/pallas_call | solution.py:225
  88.6 0.0 collective-permute-done.3
  88.7 3.8 %collective-permute-start.4 = (bf16[2,128,256]{2,1,0:T(8,128)(2,1)S(1)}, bf16[2,128,256]{2,1,0:T(8,128)(2,1)S(1)}, u32[]{:S(2)}, u32[]{:S(2)}) collective-permute-start(bf16[2,128,256]{2,1,0:T(8,128)(2,1)S(1)} %pad_maximum_fusion.3), channel_id=1, source_target_pairs={{0,448},{32,480},{64,0},{96,32},{128,64},{160,96},{192,128},{224,1... | collective-permute-start | bytes 393224 | tf_op jit(solution)/shard_map/ppermute | solution.py:45
  92.6 2.8 %collective-permute-done.4 = bf16[2,128,256]{2,1,0:T(8,128)(2,1)S(1)} collective-permute-done((bf16[2,128,256]{2,1,0:T(8,128)(2,1)S(1)}, bf16[2,128,256]{2,1,0:T(8,128)(2,1)S(1)}, u32[]{:S(2)}, u32[]{:S(2)}) %collective-permute-start.4) | collective-permute-done | bytes 131104 | tf_op jit(solution)/shard_map/ppermute | solution.py:45
  95.5 6.8 %collective-permute-start.5 = (bf16[128,256]{1,0:T(8,128)(2,1)S(1)}, bf16[128,256]{1,0:T(8,128)(2,1)S(1)}, u32[]{:S(2)}, u32[]{:S(2)}) collective-permute-start(bf16[128,256]{1,0:T(8,128)(2,1)S(1)} %fusion.4), channel_id=1, source_target_pairs={{0,384},{32,416},{64,448},{96,480},{128,0},{160,32},{192,64},{224,... | collective-permute-start | bytes 196616 | tf_op jit(solution)/shard_map/ppermute | solution.py:45
  102.3 0.3 multiply_sine_fusion
  102.6 3.9 %collective-permute-done.5 = bf16[128,256]{1,0:T(8,128)(2,1)S(1)} collective-permute-done((bf16[128,256]{1,0:T(8,128)(2,1)S(1)}, bf16[128,256]{1,0:T(8,128)(2,1)S(1)}, u32[]{:S(2)}, u32[]{:S(2)}) %collective-permute-start.5) | collective-permute-done | bytes 65568 | tf_op jit(solution)/shard_map/ppermute | solution.py:45
  106.6 0.1 slice_negate_fusion
  106.7 0.1 fusion.6
  106.9 8.4 %all_to_all.36 = bf16[4,128,256]{2,1,0:T(8,128)(2,1)S(1)} all-to-all(bf16[4,128,256]{2,1,0:T(8,128)(2,1)S(1)} %broadcast_in_dim.24), channel_id=1, replica_groups=mesh['z_hi'=4,'z_lo'=4,'y'=4,'head'=8] {'z_lo'}, dimensions={0} | all-to-all | bytes 524288 | tf_op jit(solution)/shard_map/all_to_all | solution.py:312
  115.2 2.3 %convolution_convert_fusion = bf16[8,256,256]{2,1,0:T(8,128)(2,1)S(1)} fusion(bf16[8,512,256]{2,1,0:T(8,128)(2,1)} %all-gather.4.cloned.1.call-done, bf16[512,256,1]{1,0,2:T(8,128)(2,1)S(1)} %bitcast.35), kind=kOutput, calls=%fused_computation | convolution fusion | flops 537395200 | bytes 3407872 | tf_op jit(solution)/shard_map/dot_general | solution.py:367
  117.6 13.1 %all_to_all.37 = bf16[4,512,256]{2,1,0:T(8,128)(2,1)S(1)} all-to-all(bf16[4,512,256]{2,1,0:T(8,128)(2,1)S(1)} %bitcast.33), channel_id=1, replica_groups=mesh['z_hi'=4,'z_lo'=4,'y'=4,'head'=8] {'y'}, dimensions={0} | all-to-all | bytes 2097152 | tf_op jit(solution)/shard_map/all_to_all | solution.py:312
  130.6 0.3 reduce_sum.12
  130.9 22.0 %all_to_all.38.parts_ref = bf16[4,128,256]{2,1,0:T(8,128)(2,1)} all-to-all(bf16[4,128,256]{2,1,0:T(8,128)(2,1)S(1)} %bitcast.32), channel_id=1, replica_groups=mesh['z_hi'=4,'z_lo'=4,'y'=4,'head'=8] {'z_hi'}, dimensions={0} | all-to-all | bytes 524288 | tf_op jit(solution)/shard_map/all_to_all | solution.py:312
  152.9 1.7 square.1
  154.6 21.6 %all_to_all.39.parts_ref = f32[32,8,128]{2,1,0:T(8,128)} all-to-all(f32[32,8,128]{2,1,0:T(8,128)} %get-tuple-element.10), channel_id=1, replica_groups=mesh['z_hi'=4,'z_lo'=4,'y'=4,'head'=8] {'y','head'}, dimensions={0} | all-to-all | bytes 262144 | tf_op jit(solution)/shard_map/all_to_all | solution.py:312
  176.2 1.6 spread.1
  177.8 16.0 %all_to_all.40.parts_ref = f32[16,8,128]{2,1,0:T(8,128)} all-to-all(f32[16,8,128]{2,1,0:T(8,128)} %spread.1), channel_id=1, replica_groups=mesh['z_hi'=4,'z_lo'=4,'y'=4,'head'=8] {'z_hi','z_lo'}, dimensions={0} | all-to-all | bytes 131072 | tf_op jit(solution)/shard_map/all_to_all | solution.py:312
  193.8 1.7 finish.1
  (25 shorter events, 0.3 us)
Async XLA Ops:
  7.2 2.0 copy-start.2
  7.2 2.0 copy-start.1
  7.2 46.8 %all-gather.6.cloned.1.call-start = ((), (), s32[]{:S(2)}) async-start(), calls=%async_computation.8 | async-start | bytes 2621440 | tf_op jit(solution)/shard_map/all_gather | solution.py:329
  9.2 15.2 %collective-permute-start = (bf16[1,128,256]{2,1,0:T(8,128)(2,1)S(1)}, bf16[1,128,256]{2,1,0:T(8,128)(2,1)S(1)}, u32[]{:S(2)}, u32[]{:S(2)}) collective-permute-start(bf16[1,128,256]{2,1,0:T(8,128)(2,1)S(1)} %maximum_bitcast_fusion), channel_id=1, source_target_pairs={{0,128},{32,160},{64,192},{96,224},{128,256},{160,288},{192,320},{... | collective-permute-start | bytes 196616 | tf_op jit(solution)/shard_map/ppermute | solution.py:45
  24.4 11.7 %collective-permute-start.1 = (bf16[2,128,256]{2,1,0:T(8,128)(2,1)S(1)}, bf16[2,128,256]{2,1,0:T(8,128)(2,1)S(1)}, u32[]{:S(2)}, u32[]{:S(2)}) collective-permute-start(bf16[2,128,256]{2,1,0:T(8,128)(2,1)S(1)} %pad_maximum_fusion.2), channel_id=1, source_target_pairs={{0,64},{32,96},{64,128},{96,160},{128,192},{160,224},{192,256},{22... | collective-permute-start | bytes 393224 | tf_op jit(solution)/shard_map/ppermute | solution.py:45
  36.2 10.4 %collective-permute-start.2 = (bf16[3,128,256]{2,1,0:T(8,128)(2,1)S(1)}, bf16[3,128,256]{2,1,0:T(8,128)(2,1)S(1)}, u32[]{:S(2)}, u32[]{:S(2)}) collective-permute-start(bf16[3,128,256]{2,1,0:T(8,128)(2,1)S(1)} %pad_maximum_fusion.1), channel_id=1, source_target_pairs={{0,32},{32,64},{64,96},{96,128},{128,160},{160,192},{192,224},{224... | collective-permute-start | bytes 589832 | tf_op jit(solution)/shard_map/ppermute | solution.py:45
  42.9 7.1 %copy-start.3 = (s32[5]{0:T(128)S(1)}, s32[5]{0:T(128)}, u32[]{:S(2)}) copy-start(s32[5]{0:T(128)} %param.11) | copy-start | bytes 64
  46.5 12.4 %all-to-all-start = ((bf16[4,128,256]{2,1,0:T(8,128)(2,1)}), bf16[4,128,256]{2,1,0:T(8,128)(2,1)S(1)}, u32[]{:S(2)}, u32[]{:S(2)}) async-start(bf16[4,128,256]{2,1,0:T(8,128)(2,1)} %pick.1), calls=%async_computation | async-start | bytes 524288 | tf_op jit(solution)/shard_map/all_to_all | solution.py:312
  49.9 65.3 %all-gather.4.cloned.1.call-start = ((), (), s32[]{:S(2)}) async-start(), calls=%async_computation.7 | async-start | bytes 2359296 | tf_op jit(solution)/shard_map/all_gather | solution.py:342
  58.9 0.7 copy-start
  70.0 18.6 %collective-permute-start.3 = (bf16[3,128,256]{2,1,0:T(8,128)(2,1)S(1)}, bf16[3,128,256]{2,1,0:T(8,128)(2,1)S(1)}, u32[]{:S(2)}, u32[]{:S(2)}) collective-permute-start(bf16[3,128,256]{2,1,0:T(8,128)(2,1)S(1)} %grads4.1), channel_id=1, source_target_pairs={{0,480},{32,0},{64,32},{96,64},{128,96},{160,128},{192,160},{224,1... | collective-permute-start | bytes 589832 | tf_op jit(solution)/shard_map/ppermute | solution.py:45
  88.7 6.7 %collective-permute-start.4 = (bf16[2,128,256]{2,1,0:T(8,128)(2,1)S(1)}, bf16[2,128,256]{2,1,0:T(8,128)(2,1)S(1)}, u32[]{:S(2)}, u32[]{:S(2)}) collective-permute-start(bf16[2,128,256]{2,1,0:T(8,128)(2,1)S(1)} %pad_maximum_fusion.3), channel_id=1, source_target_pairs={{0,448},{32,480},{64,0},{96,32},{128,64},{160,96},{192,128},{224,1... | collective-permute-start | bytes 393224 | tf_op jit(solution)/shard_map/ppermute | solution.py:45
  95.5 11.1 %collective-permute-start.5 = (bf16[128,256]{1,0:T(8,128)(2,1)S(1)}, bf16[128,256]{1,0:T(8,128)(2,1)S(1)}, u32[]{:S(2)}, u32[]{:S(2)}) collective-permute-start(bf16[128,256]{1,0:T(8,128)(2,1)S(1)} %fusion.4), channel_id=1, source_target_pairs={{0,384},{32,416},{64,448},{96,480},{128,0},{160,32},{192,64},{224,... | collective-permute-start | bytes 196616 | tf_op jit(solution)/shard_map/ppermute | solution.py:45
Sparse Core Ops, SparseCore 0:
  10.1 43.8 all-gather.5
  59.8 35.1 all-gather.3

commit v5 on v4

--- a/solution.py
+++ b/solution.py
@@ -45,10 +45,10 @@
     return lax.ppermute(value, axis, [(at, (at + steps) % count) for at in range(count)])
 
 
-def stack_heads(row_ref, which, dst_ref):
+def stack_heads(src_ref, dst_ref):
     for head in range(GROUP):
-        dst_ref[head * BLOCK_TOKENS:(head + 1) * BLOCK_TOKENS, :] = row_ref[
-            0, which, :, head * HEAD_SIZE:(head + 1) * HEAD_SIZE
+        dst_ref[head * BLOCK_TOKENS:(head + 1) * BLOCK_TOKENS, :] = src_ref[
+            :, head * HEAD_SIZE:(head + 1) * HEAD_SIZE
         ]
 
 
@@ -86,18 +86,23 @@
     return score, dprob
 
 
-def stats_kernel(first_turn, info_ref, row_ref, kv_ref, *refs):
+def stats_kernel(first_turn, info_ref, *refs):
     out_ref, qs_ref, gs_ref, run_ref = refs[-4:]
     if first_turn:
+        row_ref, kv_ref, own_ref = refs[:3]
+        pair = row_ref.at[0, 0], row_ref.at[0, 1]
 
         @pl.when(pl.program_id(0) == 0)
         def _():
             for target in range(SIDE):
-                out_ref[target, info_ref[1]] = refs[0][0]
-
+                out_ref[target, info_ref[1]] = own_ref[0]
+
+    else:
+        kv_ref = refs[2]
+        pair = refs[:2]
     query_row = (info_ref[1] - first_turn - pl.program_id(0)) & (SIDE - 1)
-    stack_heads(row_ref, 0, qs_ref)
-    stack_heads(row_ref, 1, gs_ref)
+    stack_heads(pair[0], qs_ref)
+    stack_heads(pair[1], gs_ref)
     run_ref[0:1, :] = jnp.full((1, ROWS), NEGATIVE, jnp.float32)
     run_ref[1:, :] = jnp.zeros((7, ROWS), jnp.float32)
     for first, last in EVEN_GROUPS + ODD_GROUPS:
@@ -139,8 +144,8 @@
     def _():
         acc_ref[...] = jnp.zeros(acc_ref.shape, jnp.float32)
 
-    stack_heads(row_ref, 0, qs_ref)
-    stack_heads(row_ref, 1, gs_ref)
+    stack_heads(row_ref.at[0, 0], qs_ref)
+    stack_heads(row_ref.at[0, 1], gs_ref)
     parts = [stats_ref[source, 0, 0:1, :] for source in range(SIDE)]
     top = functools.reduce(jnp.maximum, parts)
     shares = [jnp.exp2(part - top) for part in parts]
@@ -176,6 +181,7 @@
     pltpu.VMEM((ROWS, HEAD_SIZE), jnp.bfloat16),
 ]
 PARAMS = pltpu.CompilerParams(vmem_limit_bytes=40 * 1024 * 1024)
+SMALL = pltpu.CompilerParams(vmem_limit_bytes=8 * 1024 * 1024)
 ROW_SHAPE = (1, 2, BLOCK_TOKENS, GROUP * HEAD_SIZE)
 OWN_STATS = (1, STATS, ROWS)
 ALL_STATS = (SIDE, SIDE, STATS, ROWS)
@@ -185,18 +191,17 @@
     return pl.BlockSpec(shape, lambda step, info: (0,) * len(shape))
 
 
-def stats_pass(first_turn, info, rows, kv, *before):
+def stats_pass(first_turn, info, *arrays):
     shape = ALL_STATS if first_turn else OWN_STATS
-
-    def row_map(step, info):
-        row = (info[1] - first_turn - step) & (SIDE - 1) if first_turn else 0
-        return (row, 0, 0, 0)
-
+    specs = [whole(array.shape) for array in arrays]
+    if first_turn:
+        specs[0] = pl.BlockSpec(
+            ROW_SHAPE, lambda step, info: ((info[1] - first_turn - step) & (SIDE - 1), 0, 0, 0)
+        )
     spec = pltpu.PrefetchScalarGridSpec(
         num_scalar_prefetch=1,
         grid=(SIDE - 1 if first_turn else 1,),
-        in_specs=[pl.BlockSpec(ROW_SHAPE, row_map), whole(kv.shape)]
-        + [whole(OWN_STATS) for _ in before],
+        in_specs=specs,
         out_specs=whole(shape),
         scratch_shapes=STACKS + [pltpu.VMEM((8, ROWS), jnp.float32)],
     )
@@ -206,7 +211,7 @@
         grid_spec=spec,
         compiler_params=PARAMS,
         name="stats" + str(first_turn),
-    )(info, rows, kv, *before)
+    )(info, *arrays)
 
 
 def grads_pass(groups, dtype, info, rows, kv, stats):
@@ -254,8 +259,12 @@
         pick_kernel,
         out_shape=jax.ShapeDtypeStruct((SIDE, BLOCK_TOKENS, 256), hidden.dtype),
         grid_spec=spec,
+        compiler_params=SMALL,
         name="pick",
     )(pick, hidden, hidden)
+
+
+VMEM_SPEC = pl.BlockSpec(memory_space=pltpu.VMEM)
 
 
 def square_kernel(parts_ref, weight_ref, spread_ref):
@@ -273,6 +282,9 @@
             jax.ShapeDtypeStruct((BLOCK_TOKENS, 256), jnp.float32),
             jax.ShapeDtypeStruct((32, 8, 128), jnp.float32),
         ),
+        in_specs=[VMEM_SPEC],
+        out_specs=(VMEM_SPEC, VMEM_SPEC),
+        compiler_params=SMALL,
         name="square",
     )(parts)
 
@@ -283,7 +295,12 @@
 
 def spread_pass(parts):
     return pl.pallas_call(
-        spread_kernel, out_shape=jax.ShapeDtypeStruct((16, 8, 128), jnp.float32), name="spread"
+        spread_kernel,
+        out_shape=jax.ShapeDtypeStruct((16, 8, 128), jnp.float32),
+        in_specs=[VMEM_SPEC],
+        out_specs=VMEM_SPEC,
+        compiler_params=SMALL,
+        name="spread",
     )(parts)
 
 
@@ -297,7 +314,14 @@
 
 def finish_pass(parts, weight):
     shape = jax.ShapeDtypeStruct((BLOCK_TOKENS, HEAD_SIZE), jnp.float32)
-    return pl.pallas_call(finish_kernel, out_shape=(shape, shape), name="finish")(parts, weight)
+    return pl.pallas_call(
+        finish_kernel,
+        out_shape=(shape, shape),
+        in_specs=[VMEM_SPEC, VMEM_SPEC],
+        out_specs=(VMEM_SPEC, VMEM_SPEC),
+        compiler_params=SMALL,
+        name="finish",
+    )(parts, weight)
 
 
 def rotary_tables(positions):
@@ -333,7 +357,7 @@
     odd = rotate(jnp.concatenate([own, two[0:1], four]), Z, 1)
     column = jnp.concatenate([own, two[0:1], four, two[1:2], odd])
 
-    stats = stats_pass(0, info, own_row[None], column)
+    stats = stats_pass(0, info, queries, output_gradient, column)
     picked = pick_features(hidden, head)
     picked, _ = lax.optimization_barrier((picked, odd))
     tokens = exchange(picked, "z_lo")

time: 203 us -> 201 us (level)
  Pallas kernels: 25.8 us -> 20 us
  starting transfers between devices: 47.1 us -> 50.2 us
  waiting for transfers between devices: 19.8 us -> 16.9 us
  blocking collectives: 88.3 us -> 90.9 us
    all_to_all x6, blocking collectives: 88.3 us -> 90.9 us  [exchange(): return lax.all_to_all(value, axis, split_axis=0, concat_axis=0, tiled=True)]
  transfers between devices with their start and end apart: 9 -> 9, of which waited for: 5 -> 6; matrix products, arithmetic and copies ran while one was open for 1% -> 1% of each run, Pallas kernels for 10% -> 10%
where the time goes in v5:
time: 201 us
  blocking collectives  90.9 us (45%)
  starting transfers between devices  50.2 us (25%)
  Pallas kernels  20 us (10%)
  waiting for transfers between devices  16.9 us (8%)
  between operations  14.3 us (7%)
  other arithmetic  5.1 us (3%)
  matrix products  2.35 us (1%)
    all_to_all x6, blocking collectives, exchange(): return lax.all_to_all(value, axis, split_axis=0, concat_axis=0, tiled=True)  90.9 us
    ppermute x6, starting transfers between devices, rotate(): lax.ppermute(value, axis, [(at, (at + steps) % count) for at in range(cou...  45.2 us
    ppermute x6, waiting for transfers between devices, rotate(): lax.ppermute(value, axis, [(at, (at + steps) % count) for at in range(cou...  16 us
    pallas_call x2, Pallas kernels, grads_pass(): pl.pallas_call(functools.partial(grads_kernel, groups), out_shape=jax.Sha...  10.6 us
    pallas_call x2, Pallas kernels, stats_pass(): pl.pallas_call(functools.partial(stats_kernel, first_turn), out_shape=jax...  6.53 us
    all_to_all x1, starting transfers between devices, exchange(): return lax.all_to_all(value, axis, split_axis=0, concat_axis=0, tiled=True)  4.97 us
  transfers between devices with their start and end apart: 9, of which 6 were waited for; matrix products, arithmetic and copies ran while one was open for 1% of the time, Pallas kernels for 10%

profile of v5, /device:TPU:1, one launch (start us, length us, event | category | flops | bytes accessed | tf_op | source)
XLA Modules:
  0.0 200.5 jit_solution(14167367817388872010)
XLA Ops:
  7.2 0.0 copy-start
  7.2 0.0 all-gather.6.cloned.1.call-start
  7.2 2.0 %pad_maximum_fusion = bf16[2,128,1024]{2,1,0:T(8,128)(2,1)} fusion(bf16[1,128,1024]{2,1,0:T(8,128)(2,1)} %bitcast.27, bf16[1,128,1024]{2,1,0:T(8,128)(2,1)} %bitcast.28), kind=kLoop, calls=%fused_computation.1 | loop fusion | flops 262144 | bytes 1048576 | tf_op jit(solution)/shard_map/stack | solution.py:352
  9.2 0.0 all-gather.6.cloned.1.call-update
  9.3 0.8 maximum_bitcast_fusion
  10.0 9.6 %collective-permute-start = (bf16[1,128,256]{2,1,0:T(8,128)(2,1)S(1)}, bf16[1,128,256]{2,1,0:T(8,128)(2,1)S(1)}, u32[]{:S(2)}, u32[]{:S(2)}) collective-permute-start(bf16[1,128,256]{2,1,0:T(8,128)(2,1)S(1)} %maximum_bitcast_fusion), channel_id=1, source_target_pairs={{0,128},{32,160},{64,192},{96,224},{128,256},{160,288},{192,320},{... | collective-permute-start | bytes 196616 | tf_op jit(solution)/shard_map/ppermute | solution.py:45
  19.7 5.6 %collective-permute-done = bf16[1,128,256]{2,1,0:T(8,128)(2,1)S(1)} collective-permute-done((bf16[1,128,256]{2,1,0:T(8,128)(2,1)S(1)}, bf16[1,128,256]{2,1,0:T(8,128)(2,1)S(1)}, u32[]{:S(2)}, u32[]{:S(2)}) %collective-permute-start) | collective-permute-done | bytes 65568 | tf_op jit(solution)/shard_map/ppermute | solution.py:45
  25.3 6.1 %collective-permute-start.1 = (bf16[2,128,256]{2,1,0:T(8,128)(2,1)S(1)}, bf16[2,128,256]{2,1,0:T(8,128)(2,1)S(1)}, u32[]{:S(2)}, u32[]{:S(2)}) collective-permute-start(bf16[2,128,256]{2,1,0:T(8,128)(2,1)S(1)} %pad_maximum_fusion.2), channel_id=1, source_target_pairs={{0,64},{32,96},{64,128},{96,160},{128,192},{160,224},{192,256},{22... | collective-permute-start | bytes 393224 | tf_op jit(solution)/shard_map/ppermute | solution.py:45
  31.4 0.8 constant_dynamic-update-slice_fusion.3
  32.2 4.7 %collective-permute-done.1 = bf16[2,128,256]{2,1,0:T(8,128)(2,1)S(1)} collective-permute-done((bf16[2,128,256]{2,1,0:T(8,128)(2,1)S(1)}, bf16[2,128,256]{2,1,0:T(8,128)(2,1)S(1)}, u32[]{:S(2)}, u32[]{:S(2)}) %collective-permute-start.1) | collective-permute-done | bytes 131104 | tf_op jit(solution)/shard_map/ppermute | solution.py:45
  37.0 6.0 %collective-permute-start.2 = (bf16[3,128,256]{2,1,0:T(8,128)(2,1)S(1)}, bf16[3,128,256]{2,1,0:T(8,128)(2,1)S(1)}, u32[]{:S(2)}, u32[]{:S(2)}) collective-permute-start(bf16[3,128,256]{2,1,0:T(8,128)(2,1)S(1)} %pad_maximum_fusion.1), channel_id=1, source_target_pairs={{0,32},{32,64},{64,96},{96,128},{128,160},{160,192},{192,224},{224... | collective-permute-start | bytes 589832 | tf_op jit(solution)/shard_map/ppermute | solution.py:45
  43.1 0.1 pad_add_fusion.pick_ref
  43.2 0.0 copy-done
  43.2 2.0 pick.1
  45.2 0.8 collective-permute-done.2
  46.0 5.0 %all-to-all-start = ((bf16[4,128,256]{2,1,0:T(8,128)(2,1)}), bf16[4,128,256]{2,1,0:T(8,128)(2,1)S(1)}, u32[]{:S(2)}, u32[]{:S(2)}) async-start(bf16[4,128,256]{2,1,0:T(8,128)(2,1)} %pick.1), calls=%async_computation | async-start | bytes 524288 | tf_op jit(solution)/shard_map/all_to_all | solution.py:336
  51.0 0.0 all-gather.4.cloned.1.call-start
  51.0 0.2 reduce-window.8
  51.1 0.2 select_reduce_fusion
  51.3 0.1 pad_add_fusion.1.info_ref
  51.5 1.6 stats0.1.refs_2_
  53.1 0.9 all-gather.6.cloned.1.call-done
  54.0 4.9 %stats1.1 = f32[4,4,2,1024]{3,2,1,0:T(2,128)S(1)} custom-call(s32[6]{0:T(128)S(1)} %pad_add_fusion.1.info_ref, bf16[4,2,128,1024]{3,2,1,0:T(8,128)(2,1)} %bitcast.29, bf16[7,128,256]{2,1,0:T(8,128)(2,1)S(1)} %constant_dynamic-update-slice_fusion.refs_2_.refs_1_.kv_ref, f32[1,2,1024]{2,1,0:T(2,128)S(1)} %stats0.1.refs_2_), custom_call_target="tpu_custom_call" | custom-call | tf_op jit(solution)/shard_map/stats1/pallas_call | solution.py:208
  58.9 0.0 all-to-all-done
  58.9 0.0 copy-start.3
  58.9 0.7 copy-done.3
  59.6 0.0 all-gather.4.cloned.1.call-update
  59.6 7.2 %all_to_all.35.stats_ref = f32[4,4,2,1024]{3,2,1,0:T(2,128)S(1)} all-to-all(f32[4,4,2,1024]{3,2,1,0:T(2,128)S(1)} %stats1.1), channel_id=1, replica_groups=mesh['z_hi'=4,'z_lo'=4,'y'=4,'head'=8] {'y'}, dimensions={0} | all-to-all | bytes 262144 | tf_op jit(solution)/shard_map/all_to_all | solution.py:336
  66.9 3.1 %grads4.1 = bf16[3,128,256]{2,1,0:T(8,128)(2,1)S(1)} custom-call(s32[6]{0:T(128)S(1)} %pad_add_fusion.1.info_ref, bf16[4,2,128,1024]{3,2,1,0:T(8,128)(2,1)} %bitcast.30, bf16[7,128,256]{2,1,0:T(8,128)(2,1)S(1)} %constant_dynamic-update-slice_fusion.refs_2_.refs_1_.kv_ref, f32[4,4,2,1024]{3,2,1,0:T(2,128)S(1)} %all_to_all.35.stats_ref), custom_call_target="tpu_custom_call" | custom-call | tf_op jit(solution)/shard_map/grads4/pallas_call | solution.py:230
  70.0 11.0 %collective-permute-start.3 = (bf16[3,128,256]{2,1,0:T(8,128)(2,1)S(1)}, bf16[3,128,256]{2,1,0:T(8,128)(2,1)S(1)}, u32[]{:S(2)}, u32[]{:S(2)}) collective-permute-start(bf16[3,128,256]{2,1,0:T(8,128)(2,1)S(1)} %grads4.1), channel_id=1, source_target_pairs={{0,480},{32,0},{64,32},{96,64},{128,96},{160,128},{192,160},{224,1... | collective-permute-start | bytes 589832 | tf_op jit(solution)/shard_map/ppermute | solution.py:45
  80.9 7.5 %grads0.1 = f32[4,128,256]{2,1,0:T(8,128)S(1)} custom-call(s32[6]{0:T(128)S(1)} %pad_add_fusion.1.info_ref, bf16[4,2,128,1024]{3,2,1,0:T(8,128)(2,1)} %bitcast.31, bf16[7,128,256]{2,1,0:T(8,128)(2,1)S(1)} %constant_dynamic-update-slice_fusion.refs_2_.refs_1_.kv_ref, f32[4,4,2,1024]{3,2,1,0:T(2,128)S(1)} %all_to_all.35.stats_ref), custom_call_target="tpu_custom_call" | custom-call | tf_op jit(solution)/shard_map/grads0/pallas_call | solution.py:230
  88.4 0.0 collective-permute-done.3
  88.5 4.0 %collective-permute-start.4 = (bf16[2,128,256]{2,1,0:T(8,128)(2,1)S(1)}, bf16[2,128,256]{2,1,0:T(8,128)(2,1)S(1)}, u32[]{:S(2)}, u32[]{:S(2)}) collective-permute-start(bf16[2,128,256]{2,1,0:T(8,128)(2,1)S(1)} %pad_maximum_fusion.3), channel_id=1, source_target_pairs={{0,448},{32,480},{64,0},{96,32},{128,64},{160,96},{192,128},{224,1... | collective-permute-start | bytes 393224 | tf_op jit(solution)/shard_map/ppermute | solution.py:45
  92.6 3.3 %collective-permute-done.4 = bf16[2,128,256]{2,1,0:T(8,128)(2,1)S(1)} collective-permute-done((bf16[2,128,256]{2,1,0:T(8,128)(2,1)S(1)}, bf16[2,128,256]{2,1,0:T(8,128)(2,1)S(1)}, u32[]{:S(2)}, u32[]{:S(2)}) %collective-permute-start.4) | collective-permute-done | bytes 131104 | tf_op jit(solution)/shard_map/ppermute | solution.py:45
  95.9 8.4 %collective-permute-start.5 = (bf16[128,256]{1,0:T(8,128)(2,1)S(1)}, bf16[128,256]{1,0:T(8,128)(2,1)S(1)}, u32[]{:S(2)}, u32[]{:S(2)}) collective-permute-start(bf16[128,256]{1,0:T(8,128)(2,1)S(1)} %fusion.4), channel_id=1, source_target_pairs={{0,384},{32,416},{64,448},{96,480},{128,0},{160,32},{192,64},{224,... | collective-permute-start | bytes 196616 | tf_op jit(solution)/shard_map/ppermute | solution.py:45
  104.3 0.3 multiply_sine_fusion
  104.6 1.6 collective-permute-done.5
  106.3 0.1 slice_negate_fusion
  106.3 0.1 fusion.6
  106.5 8.4 %all_to_all.36 = bf16[4,128,256]{2,1,0:T(8,128)(2,1)S(1)} all-to-all(bf16[4,128,256]{2,1,0:T(8,128)(2,1)S(1)} %broadcast_in_dim.23), channel_id=1, replica_groups=mesh['z_hi'=4,'z_lo'=4,'y'=4,'head'=8] {'z_lo'}, dimensions={0} | all-to-all | bytes 524288 | tf_op jit(solution)/shard_map/all_to_all | solution.py:336
  114.9 2.3 %convolution_convert_fusion = bf16[8,256,256]{2,1,0:T(8,128)(2,1)S(1)} fusion(bf16[8,512,256]{2,1,0:T(8,128)(2,1)} %all-gather.4.cloned.1.call-done, bf16[512,256,1]{1,0,2:T(8,128)(2,1)S(1)} %bitcast.35), kind=kOutput, calls=%fused_computation | convolution fusion | flops 537395200 | bytes 3407872 | tf_op jit(solution)/shard_map/dot_general | solution.py:391
  117.2 12.2 %all_to_all.37 = bf16[4,512,256]{2,1,0:T(8,128)(2,1)S(1)} all-to-all(bf16[4,512,256]{2,1,0:T(8,128)(2,1)S(1)} %bitcast.33), channel_id=1, replica_groups=mesh['z_hi'=4,'z_lo'=4,'y'=4,'head'=8] {'y'}, dimensions={0} | all-to-all | bytes 2097152 | tf_op jit(solution)/shard_map/all_to_all | solution.py:336
  129.4 0.3 reduce_sum.12
  129.7 23.9 %all_to_all.38.parts_ref = bf16[4,128,256]{2,1,0:T(8,128)(2,1)S(1)} all-to-all(bf16[4,128,256]{2,1,0:T(8,128)(2,1)S(1)} %bitcast.32), channel_id=1, replica_groups=mesh['z_hi'=4,'z_lo'=4,'y'=4,'head'=8] {'z_hi'}, dimensions={0} | all-to-all | bytes 524288 | tf_op jit(solution)/shard_map/all_to_all | solution.py:336
  153.5 0.1 square.1
  153.6 23.1 %all_to_all.39.parts_ref = f32[32,8,128]{2,1,0:T(8,128)S(1)} all-to-all(f32[32,8,128]{2,1,0:T(8,128)S(1)} %get-tuple-element.10), channel_id=1, replica_groups=mesh['z_hi'=4,'z_lo'=4,'y'=4,'head'=8] {'y','head'}, dimensions={0} | all-to-all | bytes 262144 | tf_op jit(solution)/shard_map/all_to_all | solution.py:336
  176.8 16.1 %all_to_all.40.parts_ref = f32[16,8,128]{2,1,0:T(8,128)S(1)} all-to-all(f32[16,8,128]{2,1,0:T(8,128)S(1)} %spread.1), channel_id=1, replica_groups=mesh['z_hi'=4,'z_lo'=4,'y'=4,'head'=8] {'z_hi','z_lo'}, dimensions={0} | all-to-all | bytes 131072 | tf_op jit(solution)/shard_map/all_to_all | solution.py:336
  192.9 0.8 finish.1
  (27 shorter events, 0.3 us)
Async XLA Ops:
  7.2 36.0 %copy-start = (bf16[128,8192]{1,0:T(8,128)(2,1)S(1)}, bf16[128,8192]{1,0:T(8,128)(2,1)}, u32[]{:S(2)}) copy-start(bf16[128,8192]{1,0:T(8,128)(2,1)} %right_ref.1) | copy-start | bytes 6291460
  7.2 46.8 %all-gather.6.cloned.1.call-start = ((), (), s32[]{:S(2)}) async-start(), calls=%async_computation.8 | async-start | bytes 2621440 | tf_op jit(solution)/shard_map/all_gather | solution.py:353
  10.0 15.2 %collective-permute-start = (bf16[1,128,256]{2,1,0:T(8,128)(2,1)S(1)}, bf16[1,128,256]{2,1,0:T(8,128)(2,1)S(1)}, u32[]{:S(2)}, u32[]{:S(2)}) collective-permute-start(bf16[1,128,256]{2,1,0:T(8,128)(2,1)S(1)} %maximum_bitcast_fusion), channel_id=1, source_target_pairs={{0,128},{32,160},{64,192},{96,224},{128,256},{160,288},{192,320},{... | collective-permute-start | bytes 196616 | tf_op jit(solution)/shard_map/ppermute | solution.py:45
  25.3 11.7 %collective-permute-start.1 = (bf16[2,128,256]{2,1,0:T(8,128)(2,1)S(1)}, bf16[2,128,256]{2,1,0:T(8,128)(2,1)S(1)}, u32[]{:S(2)}, u32[]{:S(2)}) collective-permute-start(bf16[2,128,256]{2,1,0:T(8,128)(2,1)S(1)} %pad_maximum_fusion.2), channel_id=1, source_target_pairs={{0,64},{32,96},{64,128},{96,160},{128,192},{160,224},{192,256},{22... | collective-permute-start | bytes 393224 | tf_op jit(solution)/shard_map/ppermute | solution.py:45
  37.0 9.0 %collective-permute-start.2 = (bf16[3,128,256]{2,1,0:T(8,128)(2,1)S(1)}, bf16[3,128,256]{2,1,0:T(8,128)(2,1)S(1)}, u32[]{:S(2)}, u32[]{:S(2)}) collective-permute-start(bf16[3,128,256]{2,1,0:T(8,128)(2,1)S(1)} %pad_maximum_fusion.1), channel_id=1, source_target_pairs={{0,32},{32,64},{64,96},{96,128},{128,160},{160,192},{192,224},{224... | collective-permute-start | bytes 589832 | tf_op jit(solution)/shard_map/ppermute | solution.py:45
  43.2 7.8 %copy-start.4 = (s32[5]{0:T(128)S(1)}, s32[5]{0:T(128)}, u32[]{:S(2)}) copy-start(s32[5]{0:T(128)} %param.11) | copy-start | bytes 64
  43.2 8.3 %copy-start.1 = (bf16[128,1024]{1,0:T(8,128)(2,1)S(1)}, bf16[128,1024]{1,0:T(8,128)(2,1)}, u32[]{:S(2)}) copy-start(bf16[128,1024]{1,0:T(8,128)(2,1)} %refs_1_.1) | copy-start | bytes 786436
  43.2 8.3 %copy-start.2 = (bf16[128,1024]{1,0:T(8,128)(2,1)S(1)}, bf16[128,1024]{1,0:T(8,128)(2,1)}, u32[]{:S(2)}) copy-start(bf16[128,1024]{1,0:T(8,128)(2,1)} %refs_0_.1) | copy-start | bytes 786436
  46.0 12.9 %all-to-all-start = ((bf16[4,128,256]{2,1,0:T(8,128)(2,1)}), bf16[4,128,256]{2,1,0:T(8,128)(2,1)S(1)}, u32[]{:S(2)}, u32[]{:S(2)}) async-start(bf16[4,128,256]{2,1,0:T(8,128)(2,1)} %pick.1), calls=%async_computation | async-start | bytes 524288 | tf_op jit(solution)/shard_map/all_to_all | solution.py:336
  51.0 63.9 %all-gather.4.cloned.1.call-start = ((), (), s32[]{:S(2)}) async-start(), calls=%async_computation.7 | async-start | bytes 2359296 | tf_op jit(solution)/shard_map/all_gather | solution.py:366
  58.9 0.7 copy-start.3
  70.0 18.5 %collective-permute-start.3 = (bf16[3,128,256]{2,1,0:T(8,128)(2,1)S(1)}, bf16[3,128,256]{2,1,0:T(8,128)(2,1)S(1)}, u32[]{:S(2)}, u32[]{:S(2)}) collective-permute-start(bf16[3,128,256]{2,1,0:T(8,128)(2,1)S(1)} %grads4.1), channel_id=1, source_target_pairs={{0,480},{32,0},{64,32},{96,64},{128,96},{160,128},{192,160},{224,1... | collective-permute-start | bytes 589832 | tf_op jit(solution)/shard_map/ppermute | solution.py:45
  88.5 7.3 %collective-permute-start.4 = (bf16[2,128,256]{2,1,0:T(8,128)(2,1)S(1)}, bf16[2,128,256]{2,1,0:T(8,128)(2,1)S(1)}, u32[]{:S(2)}, u32[]{:S(2)}) collective-permute-start(bf16[2,128,256]{2,1,0:T(8,128)(2,1)S(1)} %pad_maximum_fusion.3), channel_id=1, source_target_pairs={{0,448},{32,480},{64,0},{96,32},{128,64},{160,96},{192,128},{224,1... | collective-permute-start | bytes 393224 | tf_op jit(solution)/shard_map/ppermute | solution.py:45
  95.9 10.3 %collective-permute-start.5 = (bf16[128,256]{1,0:T(8,128)(2,1)S(1)}, bf16[128,256]{1,0:T(8,128)(2,1)S(1)}, u32[]{:S(2)}, u32[]{:S(2)}) collective-permute-start(bf16[128,256]{1,0:T(8,128)(2,1)S(1)} %fusion.4), channel_id=1, source_target_pairs={{0,384},{32,416},{64,448},{96,480},{128,0},{160,32},{192,64},{224,... | collective-permute-start | bytes 196616 | tf_op jit(solution)/shard_map/ppermute | solution.py:45
Sparse Core Ops, SparseCore 0:
  10.1 43.8 all-gather.5
  59.8 36.0 all-gather.3

commit v6 on v3

--- a/solution.py
+++ b/solution.py
@@ -18,8 +18,8 @@
 SIDE = 4
 STATS = 2
 ORDER = (0, 2, 4, 6, 1, 3, 5)
-EVEN_GROUPS = ((0, 2), (2, 4))
-ODD_GROUPS = ((4, 6), (6, 7))
+EVEN_GROUPS = ((0, 4),)
+ODD_GROUPS = ((4, 7),)
 NEGATIVE = -1e30
 SCALE = HEAD_SIZE ** (-0.5)
 LOG2E = 1.4426950408889634
@@ -164,6 +164,7 @@
     pltpu.VMEM((ROWS, HEAD_SIZE), jnp.bfloat16),
 ]
 PARAMS = pltpu.CompilerParams(vmem_limit_bytes=40 * 1024 * 1024)
+SMALL = pltpu.CompilerParams(vmem_limit_bytes=8 * 1024 * 1024)
 ROW_SHAPE = (1, 2, BLOCK_TOKENS, GROUP * HEAD_SIZE)
 ROW_SPEC = pl.BlockSpec(ROW_SHAPE, lambda step, info: (step, 0, 0, 0))
 STATS_SPEC = pl.BlockSpec((SIDE, 1, STATS, ROWS), lambda step, info: (0, step, 0, 0))
@@ -231,8 +232,12 @@
         pick_kernel,
         out_shape=jax.ShapeDtypeStruct((SIDE, BLOCK_TOKENS, 256), hidden.dtype),
         grid_spec=spec,
+        compiler_params=SMALL,
         name="pick",
     )(pick, hidden, hidden)
+
+
+VMEM_SPEC = pl.BlockSpec(memory_space=pltpu.VMEM)
 
 
 def square_kernel(parts_ref, weight_ref, spread_ref):
@@ -250,6 +255,9 @@
             jax.ShapeDtypeStruct((BLOCK_TOKENS, 256), jnp.float32),
             jax.ShapeDtypeStruct((32, 8, 128), jnp.float32),
         ),
+        in_specs=[VMEM_SPEC],
+        out_specs=(VMEM_SPEC, VMEM_SPEC),
+        compiler_params=SMALL,
         name="square",
     )(parts)
 
@@ -260,7 +268,12 @@
 
 def spread_pass(parts):
     return pl.pallas_call(
-        spread_kernel, out_shape=jax.ShapeDtypeStruct((16, 8, 128), jnp.float32), name="spread"
+        spread_kernel,
+        out_shape=jax.ShapeDtypeStruct((16, 8, 128), jnp.float32),
+        in_specs=[VMEM_SPEC],
+        out_specs=VMEM_SPEC,
+        compiler_params=SMALL,
+        name="spread",
     )(parts)
 
 
@@ -274,7 +287,14 @@
 
 def finish_pass(parts, weight):
     shape = jax.ShapeDtypeStruct((BLOCK_TOKENS, HEAD_SIZE), jnp.float32)
-    return pl.pallas_call(finish_kernel, out_shape=(shape, shape), name="finish")(parts, weight)
+    return pl.pallas_call(
+        finish_kernel,
+        out_shape=(shape, shape),
+        in_specs=[VMEM_SPEC, VMEM_SPEC],
+        out_specs=(VMEM_SPEC, VMEM_SPEC),
+        compiler_params=SMALL,
+        name="finish",
+    )(parts, weight)
 
 
 def fan_kernel(src_ref, out_ref):
@@ -289,6 +309,7 @@
         out_shape=jax.ShapeDtypeStruct((copies, rows, width), tokens.dtype),
         in_specs=[pl.BlockSpec((rows, width), lambda copy: (0, 0))],
         out_specs=pl.BlockSpec((1, rows, width), lambda copy: (copy, 0, 0)),
+        compiler_params=SMALL,
         name="fan",
     )(tokens)
 

time: 207 us -> 203 us (0.981)
  waiting for transfers between devices: 18.8 us -> 27.2 us
  Pallas kernels: 22.1 us -> 16.3 us
  starting transfers between devices: 67.4 us -> 62.3 us
  blocking collectives: 89.7 us -> 86.3 us
  local copies, waits for them, and re-layouts: 1.68 us -> 4.61 us
    ppermute x6, waiting for transfers between devices: 17 us -> 23.9 us  [rotate(): lax.ppermute(value, axis, [(at, (at + steps) % count) for at in range(cou...]
    ppermute x6, starting transfers between devices: 45.1 us -> 39.9 us  [rotate(): lax.ppermute(value, axis, [(at, (at + steps) % count) for at in range(cou...]
    pallas_call x1, Pallas kernels: 3.97 us -> 0.25 us  [fan_out(): pl.pallas_call(fan_kernel, grid=(copies,), out_shape=jax.ShapeDtypeStruct...]
    all_to_all x5, blocking collectives: 89.7 us -> 86.3 us  [exchange(): return lax.all_to_all(value, axis, split_axis=0, concat_axis=0, tiled=True)]
    unnamed x11 -> x13, local copies, waits for them, and re-layouts: 0.04 us -> 2.96 us
    pallas_call x2, Pallas kernels: 5.33 us -> 7.57 us  [grads_pass(): pl.pallas_call(functools.partial(grads_kernel, groups), out_shape=jax.Sha...]
  transfers between devices with their start and end apart: 10 -> 10, of which waited for: 7 -> 5; matrix products, arithmetic and copies ran while one was open for 1% -> 1% of each run, Pallas kernels for 8% -> 8%
where the time goes in v6:
time: 203 us
  blocking collectives  86.3 us (43%)
  starting transfers between devices  62.3 us (31%)
  waiting for transfers between devices  27.2 us (13%)
  Pallas kernels  16.3 us (8%)
  local copies, waits for them, and re-layouts  4.61 us (2%)
  other arithmetic  2.59 us (1%)
  matrix products  2.35 us (1%)
    all_to_all x5, blocking collectives, exchange(): return lax.all_to_all(value, axis, split_axis=0, concat_axis=0, tiled=True)  86.3 us
    ppermute x6, starting transfers between devices, rotate(): lax.ppermute(value, axis, [(at, (at + steps) % count) for at in range(cou...  39.9 us
    ppermute x6, waiting for transfers between devices, rotate(): lax.ppermute(value, axis, [(at, (at + steps) % count) for at in range(cou...  23.9 us
    all_to_all x4, starting transfers between devices, exchange(): return lax.all_to_all(value, axis, split_axis=0, concat_axis=0, tiled=True)  22.4 us
    pallas_call x2, Pallas kernels, grads_pass(): pl.pallas_call(functools.partial(grads_kernel, groups), out_shape=jax.Sha...  7.57 us
    pallas_call x1, Pallas kernels, stats_pass(): pl.pallas_call(stats_kernel, out_shape=jax.ShapeDtypeStruct((SIDE, SIDE,...  5.56 us
  transfers between devices with their start and end apart: 10, of which 5 were waited for; matrix products, arithmetic and copies ran while one was open for 1% of the time, Pallas kernels for 8%

profile of v6, /device:TPU:1, one launch (start us, length us, event | category | flops | bytes accessed | tf_op | source)
XLA Modules:
  0.0 202.5 jit_solution(6971287098028264808)
XLA Ops:
  0.6 1.1 pad_maximum_fusion
  1.7 1.6 broadcast_in_dim.26
  3.3 5.1 %all-to-all-start.1 = ((bf16[4,2,128,1024]{3,2,1,0:T(8,128)(2,1)}), bf16[4,2,128,1024]{3,2,1,0:T(8,128)(2,1)S(1)}, u32[]{:S(2)}, u32[]{:S(2)}) async-start(bf16[4,2,128,1024]{3,2,1,0:T(8,128)(2,1)} %broadcast_in_dim.26), calls=%async_computation.1 | async-start | bytes 4194304 | tf_op jit(solution)/shard_map/all_to_all | solution.py:326
  8.5 0.0 copy-done.2
  8.5 0.0 copy-done.3
  8.5 8.8 %collective-permute-start = (bf16[1,128,256]{2,1,0:T(8,128)(2,1)S(1)}, bf16[1,128,256]{2,1,0:T(8,128)(2,1)S(1)}, u32[]{:S(2)}, u32[]{:S(2)}) collective-permute-start(bf16[1,128,256]{2,1,0:T(8,128)(2,1)S(1)} %maximum_bitcast_fusion), channel_id=1, source_target_pairs={{0,128},{32,160},{64,192},{96,224},{128,256},{160,288},{192,320},{... | collective-permute-start | bytes 196616 | tf_op jit(solution)/shard_map/ppermute | solution.py:45
  17.3 5.6 %collective-permute-done = bf16[1,128,256]{2,1,0:T(8,128)(2,1)S(1)} collective-permute-done((bf16[1,128,256]{2,1,0:T(8,128)(2,1)S(1)}, bf16[1,128,256]{2,1,0:T(8,128)(2,1)S(1)}, u32[]{:S(2)}, u32[]{:S(2)}) %collective-permute-start) | collective-permute-done | bytes 65568 | tf_op jit(solution)/shard_map/ppermute | solution.py:45
  22.9 6.1 %collective-permute-start.1 = (bf16[2,128,256]{2,1,0:T(8,128)(2,1)S(1)}, bf16[2,128,256]{2,1,0:T(8,128)(2,1)S(1)}, u32[]{:S(2)}, u32[]{:S(2)}) collective-permute-start(bf16[2,128,256]{2,1,0:T(8,128)(2,1)S(1)} %pad_maximum_fusion.2), channel_id=1, source_target_pairs={{0,64},{32,96},{64,128},{96,160},{128,192},{160,224},{192,256},{22... | collective-permute-start | bytes 393224 | tf_op jit(solution)/shard_map/ppermute | solution.py:45
  29.0 5.9 %collective-permute-done.1 = bf16[2,128,256]{2,1,0:T(8,128)(2,1)S(1)} collective-permute-done((bf16[2,128,256]{2,1,0:T(8,128)(2,1)S(1)}, bf16[2,128,256]{2,1,0:T(8,128)(2,1)S(1)}, u32[]{:S(2)}, u32[]{:S(2)}) %collective-permute-start.1) | collective-permute-done | bytes 131104 | tf_op jit(solution)/shard_map/ppermute | solution.py:45
  34.9 5.6 %collective-permute-start.2 = (bf16[3,128,256]{2,1,0:T(8,128)(2,1)S(1)}, bf16[3,128,256]{2,1,0:T(8,128)(2,1)S(1)}, u32[]{:S(2)}, u32[]{:S(2)}) collective-permute-start(bf16[3,128,256]{2,1,0:T(8,128)(2,1)S(1)} %pad_maximum_fusion.1), channel_id=1, source_target_pairs={{0,32},{32,64},{64,96},{96,128},{128,160},{160,192},{192,224},{224... | collective-permute-start | bytes 589832 | tf_op jit(solution)/shard_map/ppermute | solution.py:45
  40.6 0.1 pad_add_fusion.pick_ref
  40.6 1.6 copy-done
  42.2 2.0 pick.1
  44.2 0.0 collective-permute-done.2
  44.2 0.0 all-to-all-done.1.row_ref
  44.2 4.0 %all-to-all-start = ((bf16[4,128,256]{2,1,0:T(8,128)(2,1)}), bf16[4,128,256]{2,1,0:T(8,128)(2,1)S(1)}, u32[]{:S(2)}, u32[]{:S(2)}) async-start(bf16[4,128,256]{2,1,0:T(8,128)(2,1)} %pick.1), calls=%async_computation | async-start | bytes 524288 | tf_op jit(solution)/shard_map/all_to_all | solution.py:326
  48.2 0.0 copy-done.4
  48.2 0.2 reduce-window.8
  48.4 0.2 select_reduce_fusion
  48.6 0.1 pad_add_fusion.1.info_ref
  48.7 5.6 %stats.1 = f32[4,4,2,1024]{3,2,1,0:T(2,128)} custom-call(s32[6]{0:T(128)S(1)} %pad_add_fusion.1.info_ref, bf16[4,2,128,1024]{3,2,1,0:T(8,128)(2,1)S(1)} %all-to-all-done.1.row_ref, bf16[7,128,256]{2,1,0:T(8,128)(2,1)S(1)} %constant_dynamic-update-slice_fusion.kv_ref), custom_call_target="tpu_custom_call" | custom-call | tf_op jit(solution)/shard_map/stats/pallas_call | solution.py:185
  54.2 0.0 all-to-all-done
  54.2 3.8 %all-to-all-start.2 = ((f32[4,4,2,1024]{3,2,1,0:T(2,128)}), f32[4,4,2,1024]{3,2,1,0:T(2,128)S(1)}, u32[]{:S(2)}, u32[]{:S(2)}) async-start(f32[4,4,2,1024]{3,2,1,0:T(2,128)} %stats.1), calls=%async_computation.2 | async-start | bytes 262144 | tf_op jit(solution)/shard_map/all_to_all | solution.py:326
  58.0 0.2 fan.1
  58.3 1.3 copy-done.1
  59.6 3.2 %all-to-all-done.2.stats_ref = f32[4,4,2,1024]{3,2,1,0:T(2,128)S(1)} async-done(((f32[4,4,2,1024]{3,2,1,0:T(2,128)}), f32[4,4,2,1024]{3,2,1,0:T(2,128)S(1)}, u32[]{:S(2)}, u32[]{:S(2)}) %all-to-all-start.2) | async-done | bytes 131104 | tf_op jit(solution)/shard_map/all_to_all | solution.py:326
  62.8 9.5 %all-to-all-start.3 = ((bf16[8,512,256]{2,1,0:T(8,128)(2,1)}), bf16[8,512,256]{2,1,0:T(8,128)(2,1)}, u32[]{:S(2)}, u32[]{:S(2)}) async-start(bf16[8,512,256]{2,1,0:T(8,128)(2,1)} %copy-done.1), calls=%async_computation.3 | async-start | bytes 4194304 | tf_op jit(solution)/shard_map/all_to_all | solution.py:326
  72.3 1.1 grads4.1
  73.5 15.6 %collective-permute-start.3 = (bf16[3,128,256]{2,1,0:T(8,128)(2,1)S(1)}, bf16[3,128,256]{2,1,0:T(8,128)(2,1)S(1)}, u32[]{:S(2)}, u32[]{:S(2)}) collective-permute-start(bf16[3,128,256]{2,1,0:T(8,128)(2,1)S(1)} %grads4.1), channel_id=1, source_target_pairs={{0,480},{32,0},{64,32},{96,64},{128,96},{160,128},{192,160},{224,1... | collective-permute-start | bytes 589832 | tf_op jit(solution)/shard_map/ppermute | solution.py:45
  89.1 6.4 %grads0.1 = f32[4,128,256]{2,1,0:T(8,128)S(1)} custom-call(s32[6]{0:T(128)S(1)} %pad_add_fusion.1.info_ref, bf16[4,2,128,1024]{3,2,1,0:T(8,128)(2,1)S(1)} %all-to-all-done.1.row_ref, bf16[7,128,256]{2,1,0:T(8,128)(2,1)S(1)} %constant_dynamic-update-slice_fusion.kv_ref, f32[4,4,2,1024]{3,2,1,0:T(2,128)S(1)} %all-to-all-done.2.stats_ref), custom_call_target="tpu_custom_call" | custom-call | tf_op jit(solution)/shard_map/grads0/pallas_call | solution.py:203
  95.5 0.0 collective-permute-done.3
  95.6 1.9 collective-permute-start.4
  97.6 5.6 %collective-permute-done.4 = bf16[2,128,256]{2,1,0:T(8,128)(2,1)S(1)} collective-permute-done((bf16[2,128,256]{2,1,0:T(8,128)(2,1)S(1)}, bf16[2,128,256]{2,1,0:T(8,128)(2,1)S(1)}, u32[]{:S(2)}, u32[]{:S(2)}) %collective-permute-start.4) | collective-permute-done | bytes 131104 | tf_op jit(solution)/shard_map/ppermute | solution.py:45
  103.2 1.9 collective-permute-start.5
  105.2 0.3 multiply_sine_fusion
  105.5 6.9 %collective-permute-done.5 = bf16[128,256]{1,0:T(8,128)(2,1)S(1)} collective-permute-done((bf16[128,256]{1,0:T(8,128)(2,1)S(1)}, bf16[128,256]{1,0:T(8,128)(2,1)S(1)}, u32[]{:S(2)}, u32[]{:S(2)}) %collective-permute-start.5) | collective-permute-done | bytes 65568 | tf_op jit(solution)/shard_map/ppermute | solution.py:45
  112.4 0.0 all-to-all-done.3
  112.4 0.1 slice_negate_fusion
  112.5 0.1 fusion.6
  112.7 12.4 %all_to_all.45 = bf16[4,128,256]{2,1,0:T(8,128)(2,1)S(1)} all-to-all(bf16[4,128,256]{2,1,0:T(8,128)(2,1)S(1)} %broadcast_in_dim.27), channel_id=1, replica_groups=mesh['z_hi'=4,'z_lo'=4,'y'=4,'head'=8] {'z_lo'}, dimensions={0} | all-to-all | bytes 524288 | tf_op jit(solution)/shard_map/all_to_all | solution.py:326
  125.1 2.3 %convolution_convert_fusion = bf16[8,256,256]{2,1,0:T(8,128)(2,1)S(1)} fusion(bf16[8,512,256]{2,1,0:T(8,128)(2,1)} %all-to-all-done.3, bf16[512,256,1]{1,0,2:T(8,128)(2,1)S(1)} %bitcast.29), kind=kOutput, calls=%fused_computation | convolution fusion | flops 537395200 | bytes 3407872 | tf_op jit(solution)/shard_map/dot_general | solution.py:379
  127.4 13.8 %all_to_all.46 = bf16[4,512,256]{2,1,0:T(8,128)(2,1)S(1)} all-to-all(bf16[4,512,256]{2,1,0:T(8,128)(2,1)S(1)} %bitcast.28), channel_id=1, replica_groups=mesh['z_hi'=4,'z_lo'=4,'y'=4,'head'=8] {'y'}, dimensions={0} | all-to-all | bytes 2097152 | tf_op jit(solution)/shard_map/all_to_all | solution.py:326
  141.2 0.3 reduce_sum.12
  141.5 25.0 %all_to_all.47.parts_ref = bf16[4,128,256]{2,1,0:T(8,128)(2,1)S(1)} all-to-all(bf16[4,128,256]{2,1,0:T(8,128)(2,1)S(1)} %bitcast.27), channel_id=1, replica_groups=mesh['z_hi'=4,'z_lo'=4,'y'=4,'head'=8] {'z_hi'}, dimensions={0} | all-to-all | bytes 524288 | tf_op jit(solution)/shard_map/all_to_all | solution.py:326
  166.5 0.1 square.1
  166.5 19.5 %all_to_all.48.parts_ref = f32[32,8,128]{2,1,0:T(8,128)S(1)} all-to-all(f32[32,8,128]{2,1,0:T(8,128)S(1)} %get-tuple-element.18), channel_id=1, replica_groups=mesh['z_hi'=4,'z_lo'=4,'y'=4,'head'=8] {'y','head'}, dimensions={0} | all-to-all | bytes 262144 | tf_op jit(solution)/shard_map/all_to_all | solution.py:326
  186.0 15.7 %all_to_all.49.parts_ref = f32[16,8,128]{2,1,0:T(8,128)S(1)} all-to-all(f32[16,8,128]{2,1,0:T(8,128)S(1)} %spread.1), channel_id=1, replica_groups=mesh['z_hi'=4,'z_lo'=4,'y'=4,'head'=8] {'z_hi','z_lo'}, dimensions={0} | all-to-all | bytes 131072 | tf_op jit(solution)/shard_map/all_to_all | solution.py:326
  201.7 0.8 finish.1
  (27 shorter events, 0.3 us)
Async XLA Ops:
  3.3 5.2 %copy-start.2 = (bf16[128,128]{1,0:T(8,128)(2,1)S(1)}, bf16[128,128]{1,0:T(8,128)(2,1)}, u32[]{:S(2)}) copy-start(bf16[128,128]{1,0:T(8,128)(2,1)} %param.9) | copy-start | bytes 98308
  3.3 5.2 %copy-start.3 = (bf16[128,128]{1,0:T(8,128)(2,1)S(1)}, bf16[128,128]{1,0:T(8,128)(2,1)}, u32[]{:S(2)}) copy-start(bf16[128,128]{1,0:T(8,128)(2,1)} %param.8) | copy-start | bytes 98308
  3.3 40.9 %all-to-all-start.1 = ((bf16[4,2,128,1024]{3,2,1,0:T(8,128)(2,1)}), bf16[4,2,128,1024]{3,2,1,0:T(8,128)(2,1)S(1)}, u32[]{:S(2)}, u32[]{:S(2)}) async-start(bf16[4,2,128,1024]{3,2,1,0:T(8,128)(2,1)} %broadcast_in_dim.26), calls=%async_computation.1 | async-start | bytes 4194304 | tf_op jit(solution)/shard_map/all_to_all | solution.py:326
  8.5 14.4 %collective-permute-start = (bf16[1,128,256]{2,1,0:T(8,128)(2,1)S(1)}, bf16[1,128,256]{2,1,0:T(8,128)(2,1)S(1)}, u32[]{:S(2)}, u32[]{:S(2)}) collective-permute-start(bf16[1,128,256]{2,1,0:T(8,128)(2,1)S(1)} %maximum_bitcast_fusion), channel_id=1, source_target_pairs={{0,128},{32,160},{64,192},{96,224},{128,256},{160,288},{192,320},{... | collective-permute-start | bytes 196616 | tf_op jit(solution)/shard_map/ppermute | solution.py:45
  22.9 12.0 %collective-permute-start.1 = (bf16[2,128,256]{2,1,0:T(8,128)(2,1)S(1)}, bf16[2,128,256]{2,1,0:T(8,128)(2,1)S(1)}, u32[]{:S(2)}, u32[]{:S(2)}) collective-permute-start(bf16[2,128,256]{2,1,0:T(8,128)(2,1)S(1)} %pad_maximum_fusion.2), channel_id=1, source_target_pairs={{0,64},{32,96},{64,128},{96,160},{128,192},{160,224},{192,256},{22... | collective-permute-start | bytes 393224 | tf_op jit(solution)/shard_map/ppermute | solution.py:45
  34.9 9.3 %collective-permute-start.2 = (bf16[3,128,256]{2,1,0:T(8,128)(2,1)S(1)}, bf16[3,128,256]{2,1,0:T(8,128)(2,1)S(1)}, u32[]{:S(2)}, u32[]{:S(2)}) collective-permute-start(bf16[3,128,256]{2,1,0:T(8,128)(2,1)S(1)} %pad_maximum_fusion.1), channel_id=1, source_target_pairs={{0,32},{32,64},{64,96},{96,128},{128,160},{160,192},{192,224},{224... | collective-permute-start | bytes 589832 | tf_op jit(solution)/shard_map/ppermute | solution.py:45
  40.6 1.6 copy-start
  42.2 6.0 %copy-start.4 = (s32[5]{0:T(128)S(1)}, s32[5]{0:T(128)}, u32[]{:S(2)}) copy-start(s32[5]{0:T(128)} %param.11) | copy-start | bytes 64
  44.2 10.0 %all-to-all-start = ((bf16[4,128,256]{2,1,0:T(8,128)(2,1)}), bf16[4,128,256]{2,1,0:T(8,128)(2,1)S(1)}, u32[]{:S(2)}, u32[]{:S(2)}) async-start(bf16[4,128,256]{2,1,0:T(8,128)(2,1)} %pick.1), calls=%async_computation | async-start | bytes 524288 | tf_op jit(solution)/shard_map/all_to_all | solution.py:326
  54.2 8.6 %all-to-all-start.2 = ((f32[4,4,2,1024]{3,2,1,0:T(2,128)}), f32[4,4,2,1024]{3,2,1,0:T(2,128)S(1)}, u32[]{:S(2)}, u32[]{:S(2)}) async-start(f32[4,4,2,1024]{3,2,1,0:T(2,128)} %stats.1), calls=%async_computation.2 | async-start | bytes 262144 | tf_op jit(solution)/shard_map/all_to_all | solution.py:326
  58.3 1.3 copy-start.1
  62.8 49.5 %all-to-all-start.3 = ((bf16[8,512,256]{2,1,0:T(8,128)(2,1)}), bf16[8,512,256]{2,1,0:T(8,128)(2,1)}, u32[]{:S(2)}, u32[]{:S(2)}) async-start(bf16[8,512,256]{2,1,0:T(8,128)(2,1)} %copy-done.1), calls=%async_computation.3 | async-start | bytes 4194304 | tf_op jit(solution)/shard_map/all_to_all | solution.py:326
  73.5 22.0 %collective-permute-start.3 = (bf16[3,128,256]{2,1,0:T(8,128)(2,1)S(1)}, bf16[3,128,256]{2,1,0:T(8,128)(2,1)S(1)}, u32[]{:S(2)}, u32[]{:S(2)}) collective-permute-start(bf16[3,128,256]{2,1,0:T(8,128)(2,1)S(1)} %grads4.1), channel_id=1, source_target_pairs={{0,480},{32,0},{64,32},{96,64},{128,96},{160,128},{192,160},{224,1... | collective-permute-start | bytes 589832 | tf_op jit(solution)/shard_map/ppermute | solution.py:45
  95.6 7.6 %collective-permute-start.4 = (bf16[2,128,256]{2,1,0:T(8,128)(2,1)S(1)}, bf16[2,128,256]{2,1,0:T(8,128)(2,1)S(1)}, u32[]{:S(2)}, u32[]{:S(2)}) collective-permute-start(bf16[2,128,256]{2,1,0:T(8,128)(2,1)S(1)} %pad_maximum_fusion.3), channel_id=1, source_target_pairs={{0,448},{32,480},{64,0},{96,32},{128,64},{160,96},{192,128},{224,1... | collective-permute-start | bytes 393224 | tf_op jit(solution)/shard_map/ppermute | solution.py:45
  103.2 9.1 %collective-permute-start.5 = (bf16[128,256]{1,0:T(8,128)(2,1)S(1)}, bf16[128,256]{1,0:T(8,128)(2,1)S(1)}, u32[]{:S(2)}, u32[]{:S(2)}) collective-permute-start(bf16[128,256]{1,0:T(8,128)(2,1)S(1)} %fusion.4), channel_id=1, source_target_pairs={{0,384},{32,416},{64,448},{96,480},{128,0},{160,32},{192,64},{224,... | collective-permute-start | bytes 196616 | tf_op jit(solution)/shard_map/ppermute | solution.py:45

commit v7 on v6

--- a/solution.py
+++ b/solution.py
@@ -314,6 +314,24 @@
     )(tokens)
 
 
+def pair_kernel(q_ref, g_ref, out_ref):
+    out_ref[0, 0] = q_ref[...]
+    out_ref[0, 1] = g_ref[...]
+
+
+def pair_out(queries, gradients):
+    shape = queries.shape
+    return pl.pallas_call(
+        pair_kernel,
+        grid=(SIDE,),
+        out_shape=jax.ShapeDtypeStruct((SIDE, 2) + shape, queries.dtype),
+        in_specs=[pl.BlockSpec(shape, lambda copy: (0, 0))] * 2,
+        out_specs=pl.BlockSpec((1, 2) + shape, lambda copy: (copy, 0, 0, 0)),
+        compiler_params=SMALL,
+        name="pair",
+    )(queries, gradients)
+
+
 def rotary_tables(positions):
     half = HEAD_SIZE // 2
     freqs = 500000.0 ** (-(jnp.arange(half, dtype=jnp.float32) * 2.0) / HEAD_SIZE)
@@ -339,8 +357,7 @@
 
     own = jnp.concatenate([keys, values], axis=1)[None]
     four = rotate(own, Z, 4)
-    rows = jnp.stack([queries, output_gradient])
-    query_rows = exchange(jnp.broadcast_to(rows, (SIDE,) + rows.shape), "y")
+    query_rows = exchange(pair_out(queries, output_gradient), "y")
     even = jnp.concatenate([own, four])
     two = rotate(even, Z, 2)
     odd = rotate(jnp.concatenate([own, two[0:1], four]), Z, 1)

time: 203 us -> 203 us (level)
  starting transfers between devices: 62.3 us -> 69.8 us
  waiting for transfers between devices: 27.2 us -> 20.9 us
  blocking collectives: 86.3 us -> 83.8 us
    ppermute x6, starting transfers between devices: 39.9 us -> 47.3 us  [rotate(): lax.ppermute(value, axis, [(at, (at + steps) % count) for at in range(cou...]
    ppermute x6, waiting for transfers between devices: 23.9 us -> 17.6 us  [rotate(): lax.ppermute(value, axis, [(at, (at + steps) % count) for at in range(cou...]
    unnamed x13 -> x19, local copies, waits for them, and re-layouts: 2.96 us -> 6.19 us
    all_to_all x5, blocking collectives: 86.3 us -> 83.8 us  [exchange(): return lax.all_to_all(value, axis, split_axis=0, concat_axis=0, tiled=True)]
where the time goes in v7:
time: 203 us; the launch traced here: 202 us
  blocking collectives  83.8 us (41%)
  starting transfers between devices  69.8 us (34%)
  waiting for transfers between devices  20.9 us (10%)
  Pallas kernels  16.4 us (8%)
  local copies, waits for them, and re-layouts  6.24 us (3%)
  matrix products  2.35 us (1%)
    all_to_all x5, blocking collectives, exchange(): return lax.all_to_all(value, axis, split_axis=0, concat_axis=0, tiled=True)  83.8 us
    ppermute x6, starting transfers between devices, rotate(): lax.ppermute(value, axis, [(at, (at + steps) % count) for at in range(cou...  47.3 us
    all_to_all x4, starting transfers between devices, exchange(): return lax.all_to_all(value, axis, split_axis=0, concat_axis=0, tiled=True)  22.4 us
    ppermute x6, waiting for transfers between devices, rotate(): lax.ppermute(value, axis, [(at, (at + steps) % count) for at in range(cou...  17.6 us
    pallas_call x2, Pallas kernels, grads_pass(): pl.pallas_call(functools.partial(grads_kernel, groups), out_shape=jax.Sha...  7.57 us
    unnamed x19, local copies, waits for them, and re-layouts  6.19 us
    pallas_call x1, Pallas kernels, stats_pass(): pl.pallas_call(stats_kernel, out_shape=jax.ShapeDtypeStruct((SIDE, SIDE,...  5.55 us
  transfers between devices with their start and end apart: 10, of which 5 were waited for; matrix products, arithmetic and copies ran while one was open for 1% of the time, Pallas kernels for 8%

profile of v7, /device:TPU:1, one launch (start us, length us, event | category | flops | bytes accessed | tf_op | source)
XLA Modules:
  0.0 201.9 jit_solution(18077410282319733972)
XLA Ops:
  0.6 0.9 copy-done.3
  1.6 0.9 copy-done.4
  2.5 0.2 pair.1
  2.7 0.0 copy-start
  2.7 1.3 copy-done
  4.1 5.1 %all-to-all-start.1 = ((bf16[4,2,128,1024]{3,2,1,0:T(8,128)(2,1)}), bf16[4,2,128,1024]{3,2,1,0:T(8,128)(2,1)S(1)}, u32[]{:S(2)}, u32[]{:S(2)}) async-start(bf16[4,2,128,1024]{3,2,1,0:T(8,128)(2,1)} %copy-done), calls=%async_computation.1 | async-start | bytes 4194304 | tf_op jit(solution)/shard_map/all_to_all | solution.py:344
  9.2 8.8 %collective-permute-start = (bf16[1,128,256]{2,1,0:T(8,128)(2,1)S(1)}, bf16[1,128,256]{2,1,0:T(8,128)(2,1)S(1)}, u32[]{:S(2)}, u32[]{:S(2)}) collective-permute-start(bf16[1,128,256]{2,1,0:T(8,128)(2,1)S(1)} %maximum_bitcast_fusion), channel_id=1, source_target_pairs={{0,128},{32,160},{64,192},{96,224},{128,256},{160,288},{192,320},{... | collective-permute-start | bytes 196616 | tf_op jit(solution)/shard_map/ppermute | solution.py:45
  18.1 5.6 %collective-permute-done = bf16[1,128,256]{2,1,0:T(8,128)(2,1)S(1)} collective-permute-done((bf16[1,128,256]{2,1,0:T(8,128)(2,1)S(1)}, bf16[1,128,256]{2,1,0:T(8,128)(2,1)S(1)}, u32[]{:S(2)}, u32[]{:S(2)}) %collective-permute-start) | collective-permute-done | bytes 65568 | tf_op jit(solution)/shard_map/ppermute | solution.py:45
  23.7 6.1 %collective-permute-start.1 = (bf16[2,128,256]{2,1,0:T(8,128)(2,1)S(1)}, bf16[2,128,256]{2,1,0:T(8,128)(2,1)S(1)}, u32[]{:S(2)}, u32[]{:S(2)}) collective-permute-start(bf16[2,128,256]{2,1,0:T(8,128)(2,1)S(1)} %pad_maximum_fusion.1), channel_id=1, source_target_pairs={{0,64},{32,96},{64,128},{96,160},{128,192},{160,224},{192,256},{22... | collective-permute-start | bytes 393224 | tf_op jit(solution)/shard_map/ppermute | solution.py:45
  29.8 5.9 %collective-permute-done.1 = bf16[2,128,256]{2,1,0:T(8,128)(2,1)S(1)} collective-permute-done((bf16[2,128,256]{2,1,0:T(8,128)(2,1)S(1)}, bf16[2,128,256]{2,1,0:T(8,128)(2,1)S(1)}, u32[]{:S(2)}, u32[]{:S(2)}) %collective-permute-start.1) | collective-permute-done | bytes 131104 | tf_op jit(solution)/shard_map/ppermute | solution.py:45
  35.7 5.6 %collective-permute-start.2 = (bf16[3,128,256]{2,1,0:T(8,128)(2,1)S(1)}, bf16[3,128,256]{2,1,0:T(8,128)(2,1)S(1)}, u32[]{:S(2)}, u32[]{:S(2)}) collective-permute-start(bf16[3,128,256]{2,1,0:T(8,128)(2,1)S(1)} %pad_maximum_fusion), channel_id=1, source_target_pairs={{0,32},{32,64},{64,96},{96,128},{128,160},{160,192},{192,224},{224... | collective-permute-start | bytes 589832 | tf_op jit(solution)/shard_map/ppermute | solution.py:45
  41.3 0.1 pad_add_fusion.pick_ref
  41.4 1.6 copy-done.1
  43.0 2.0 pick.1
  45.0 0.0 collective-permute-done.2
  45.0 0.0 all-to-all-done.1.row_ref
  45.0 4.0 %all-to-all-start = ((bf16[4,128,256]{2,1,0:T(8,128)(2,1)}), bf16[4,128,256]{2,1,0:T(8,128)(2,1)S(1)}, u32[]{:S(2)}, u32[]{:S(2)}) async-start(bf16[4,128,256]{2,1,0:T(8,128)(2,1)} %pick.1), calls=%async_computation | async-start | bytes 524288 | tf_op jit(solution)/shard_map/all_to_all | solution.py:344
  49.0 0.2 reduce-window.8
  49.2 0.2 select_reduce_fusion
  49.3 0.1 pad_add_fusion.1.info_ref
  49.4 5.6 %stats.1 = f32[4,4,2,1024]{3,2,1,0:T(2,128)} custom-call(s32[6]{0:T(128)S(1)} %pad_add_fusion.1.info_ref, bf16[4,2,128,1024]{3,2,1,0:T(8,128)(2,1)S(1)} %all-to-all-done.1.row_ref, bf16[7,128,256]{2,1,0:T(8,128)(2,1)S(1)} %constant_dynamic-update-slice_fusion.kv_ref), custom_call_target="tpu_custom_call" | custom-call | tf_op jit(solution)/shard_map/stats/pallas_call | solution.py:185
  55.0 0.0 all-to-all-done
  55.0 3.8 %all-to-all-start.2 = ((f32[4,4,2,1024]{3,2,1,0:T(2,128)}), f32[4,4,2,1024]{3,2,1,0:T(2,128)S(1)}, u32[]{:S(2)}, u32[]{:S(2)}) async-start(f32[4,4,2,1024]{3,2,1,0:T(2,128)} %stats.1), calls=%async_computation.2 | async-start | bytes 262144 | tf_op jit(solution)/shard_map/all_to_all | solution.py:344
  58.8 0.2 fan.1
  59.0 1.3 copy-done.2
  60.4 3.2 %all-to-all-done.2.stats_ref = f32[4,4,2,1024]{3,2,1,0:T(2,128)S(1)} async-done(((f32[4,4,2,1024]{3,2,1,0:T(2,128)}), f32[4,4,2,1024]{3,2,1,0:T(2,128)S(1)}, u32[]{:S(2)}, u32[]{:S(2)}) %all-to-all-start.2) | async-done | bytes 131104 | tf_op jit(solution)/shard_map/all_to_all | solution.py:344
  63.6 9.5 %all-to-all-start.3 = ((bf16[8,512,256]{2,1,0:T(8,128)(2,1)}), bf16[8,512,256]{2,1,0:T(8,128)(2,1)}, u32[]{:S(2)}, u32[]{:S(2)}) async-start(bf16[8,512,256]{2,1,0:T(8,128)(2,1)} %copy-done.2), calls=%async_computation.3 | async-start | bytes 4194304 | tf_op jit(solution)/shard_map/all_to_all | solution.py:344
  73.1 1.1 grads4.1
  74.2 8.4 %collective-permute-start.3 = (bf16[3,128,256]{2,1,0:T(8,128)(2,1)S(1)}, bf16[3,128,256]{2,1,0:T(8,128)(2,1)S(1)}, u32[]{:S(2)}, u32[]{:S(2)}) collective-permute-start(bf16[3,128,256]{2,1,0:T(8,128)(2,1)S(1)} %grads4.1), channel_id=1, source_target_pairs={{0,480},{32,0},{64,32},{96,64},{128,96},{160,128},{192,160},{224,1... | collective-permute-start | bytes 589832 | tf_op jit(solution)/shard_map/ppermute | solution.py:45
  82.6 6.4 %grads0.1 = f32[4,128,256]{2,1,0:T(8,128)S(1)} custom-call(s32[6]{0:T(128)S(1)} %pad_add_fusion.1.info_ref, bf16[4,2,128,1024]{3,2,1,0:T(8,128)(2,1)S(1)} %all-to-all-done.1.row_ref, bf16[7,128,256]{2,1,0:T(8,128)(2,1)S(1)} %constant_dynamic-update-slice_fusion.kv_ref, f32[4,4,2,1024]{3,2,1,0:T(2,128)S(1)} %all-to-all-done.2.stats_ref), custom_call_target="tpu_custom_call" | custom-call | tf_op jit(solution)/shard_map/grads0/pallas_call | solution.py:203
  89.1 0.0 collective-permute-done.3
  89.2 8.1 %collective-permute-start.4 = (bf16[2,128,256]{2,1,0:T(8,128)(2,1)S(1)}, bf16[2,128,256]{2,1,0:T(8,128)(2,1)S(1)}, u32[]{:S(2)}, u32[]{:S(2)}) collective-permute-start(bf16[2,128,256]{2,1,0:T(8,128)(2,1)S(1)} %pad_maximum_fusion.2), channel_id=1, source_target_pairs={{0,448},{32,480},{64,0},{96,32},{128,64},{160,96},{192,128},{224,1... | collective-permute-start | bytes 393224 | tf_op jit(solution)/shard_map/ppermute | solution.py:45
  97.3 2.5 %collective-permute-done.4 = bf16[2,128,256]{2,1,0:T(8,128)(2,1)S(1)} collective-permute-done((bf16[2,128,256]{2,1,0:T(8,128)(2,1)S(1)}, bf16[2,128,256]{2,1,0:T(8,128)(2,1)S(1)}, u32[]{:S(2)}, u32[]{:S(2)}) %collective-permute-start.4) | collective-permute-done | bytes 131104 | tf_op jit(solution)/shard_map/ppermute | solution.py:45
  99.9 10.4 %collective-permute-start.5 = (bf16[128,256]{1,0:T(8,128)(2,1)S(1)}, bf16[128,256]{1,0:T(8,128)(2,1)S(1)}, u32[]{:S(2)}, u32[]{:S(2)}) collective-permute-start(bf16[128,256]{1,0:T(8,128)(2,1)S(1)} %fusion.4), channel_id=1, source_target_pairs={{0,384},{32,416},{64,448},{96,480},{128,0},{160,32},{192,64},{224,... | collective-permute-start | bytes 196616 | tf_op jit(solution)/shard_map/ppermute | solution.py:45
  110.3 0.3 multiply_sine_fusion
  110.6 3.7 %collective-permute-done.5 = bf16[128,256]{1,0:T(8,128)(2,1)S(1)} collective-permute-done((bf16[128,256]{1,0:T(8,128)(2,1)S(1)}, bf16[128,256]{1,0:T(8,128)(2,1)S(1)}, u32[]{:S(2)}, u32[]{:S(2)}) %collective-permute-start.5) | collective-permute-done | bytes 65568 | tf_op jit(solution)/shard_map/ppermute | solution.py:45
  114.3 0.0 all-to-all-done.3
  114.3 0.1 slice_negate_fusion
  114.4 0.1 fusion.6
  114.6 8.5 %all_to_all.45 = bf16[4,128,256]{2,1,0:T(8,128)(2,1)S(1)} all-to-all(bf16[4,128,256]{2,1,0:T(8,128)(2,1)S(1)} %broadcast_in_dim.23), channel_id=1, replica_groups=mesh['z_hi'=4,'z_lo'=4,'y'=4,'head'=8] {'z_lo'}, dimensions={0} | all-to-all | bytes 524288 | tf_op jit(solution)/shard_map/all_to_all | solution.py:344
  123.0 2.3 %convolution_convert_fusion = bf16[8,256,256]{2,1,0:T(8,128)(2,1)S(1)} fusion(bf16[8,512,256]{2,1,0:T(8,128)(2,1)} %all-to-all-done.3, bf16[512,256,1]{1,0,2:T(8,128)(2,1)S(1)} %bitcast.27), kind=kOutput, calls=%fused_computation | convolution fusion | flops 537395200 | bytes 3407872 | tf_op jit(solution)/shard_map/dot_general | solution.py:396
  125.4 17.0 %all_to_all.46 = bf16[4,512,256]{2,1,0:T(8,128)(2,1)S(1)} all-to-all(bf16[4,512,256]{2,1,0:T(8,128)(2,1)S(1)} %bitcast.26), channel_id=1, replica_groups=mesh['z_hi'=4,'z_lo'=4,'y'=4,'head'=8] {'y'}, dimensions={0} | all-to-all | bytes 2097152 | tf_op jit(solution)/shard_map/all_to_all | solution.py:344
  142.4 0.3 reduce_sum.12
  142.6 26.3 %all_to_all.47.parts_ref = bf16[4,128,256]{2,1,0:T(8,128)(2,1)S(1)} all-to-all(bf16[4,128,256]{2,1,0:T(8,128)(2,1)S(1)} %bitcast.25), channel_id=1, replica_groups=mesh['z_hi'=4,'z_lo'=4,'y'=4,'head'=8] {'z_hi'}, dimensions={0} | all-to-all | bytes 524288 | tf_op jit(solution)/shard_map/all_to_all | solution.py:344
  168.9 0.1 square.1
  169.0 16.1 %all_to_all.48.parts_ref = f32[32,8,128]{2,1,0:T(8,128)S(1)} all-to-all(f32[32,8,128]{2,1,0:T(8,128)S(1)} %get-tuple-element.18), channel_id=1, replica_groups=mesh['z_hi'=4,'z_lo'=4,'y'=4,'head'=8] {'y','head'}, dimensions={0} | all-to-all | bytes 262144 | tf_op jit(solution)/shard_map/all_to_all | solution.py:344
  185.2 16.0 %all_to_all.49.parts_ref = f32[16,8,128]{2,1,0:T(8,128)S(1)} all-to-all(f32[16,8,128]{2,1,0:T(8,128)S(1)} %spread.1), channel_id=1, replica_groups=mesh['z_hi'=4,'z_lo'=4,'y'=4,'head'=8] {'z_hi','z_lo'}, dimensions={0} | all-to-all | bytes 131072 | tf_op jit(solution)/shard_map/all_to_all | solution.py:344
  201.1 0.8 finish.1
  (32 shorter events, 0.4 us)
Async XLA Ops:
  0.6 1.0 copy-start.3
  1.6 0.9 copy-start.4
  2.7 1.3 copy-start
  4.1 5.2 %copy-start.5 = (bf16[128,128]{1,0:T(8,128)(2,1)S(1)}, bf16[128,128]{1,0:T(8,128)(2,1)}, u32[]{:S(2)}) copy-start(bf16[128,128]{1,0:T(8,128)(2,1)} %param.9) | copy-start | bytes 98308
  4.1 5.2 %copy-start.6 = (bf16[128,128]{1,0:T(8,128)(2,1)S(1)}, bf16[128,128]{1,0:T(8,128)(2,1)}, u32[]{:S(2)}) copy-start(bf16[128,128]{1,0:T(8,128)(2,1)} %param.8) | copy-start | bytes 98308
  4.1 40.9 %all-to-all-start.1 = ((bf16[4,2,128,1024]{3,2,1,0:T(8,128)(2,1)}), bf16[4,2,128,1024]{3,2,1,0:T(8,128)(2,1)S(1)}, u32[]{:S(2)}, u32[]{:S(2)}) async-start(bf16[4,2,128,1024]{3,2,1,0:T(8,128)(2,1)} %copy-done), calls=%async_computation.1 | async-start | bytes 4194304 | tf_op jit(solution)/shard_map/all_to_all | solution.py:344
  9.2 14.4 %collective-permute-start = (bf16[1,128,256]{2,1,0:T(8,128)(2,1)S(1)}, bf16[1,128,256]{2,1,0:T(8,128)(2,1)S(1)}, u32[]{:S(2)}, u32[]{:S(2)}) collective-permute-start(bf16[1,128,256]{2,1,0:T(8,128)(2,1)S(1)} %maximum_bitcast_fusion), channel_id=1, source_target_pairs={{0,128},{32,160},{64,192},{96,224},{128,256},{160,288},{192,320},{... | collective-permute-start | bytes 196616 | tf_op jit(solution)/shard_map/ppermute | solution.py:45
  23.7 12.0 %collective-permute-start.1 = (bf16[2,128,256]{2,1,0:T(8,128)(2,1)S(1)}, bf16[2,128,256]{2,1,0:T(8,128)(2,1)S(1)}, u32[]{:S(2)}, u32[]{:S(2)}) collective-permute-start(bf16[2,128,256]{2,1,0:T(8,128)(2,1)S(1)} %pad_maximum_fusion.1), channel_id=1, source_target_pairs={{0,64},{32,96},{64,128},{96,160},{128,192},{160,224},{192,256},{22... | collective-permute-start | bytes 393224 | tf_op jit(solution)/shard_map/ppermute | solution.py:45
  35.7 9.3 %collective-permute-start.2 = (bf16[3,128,256]{2,1,0:T(8,128)(2,1)S(1)}, bf16[3,128,256]{2,1,0:T(8,128)(2,1)S(1)}, u32[]{:S(2)}, u32[]{:S(2)}) collective-permute-start(bf16[3,128,256]{2,1,0:T(8,128)(2,1)S(1)} %pad_maximum_fusion), channel_id=1, source_target_pairs={{0,32},{32,64},{64,96},{96,128},{128,160},{160,192},{192,224},{224... | collective-permute-start | bytes 589832 | tf_op jit(solution)/shard_map/ppermute | solution.py:45
  41.4 1.6 copy-start.1
  43.0 6.0 %copy-start.7 = (s32[5]{0:T(128)S(1)}, s32[5]{0:T(128)}, u32[]{:S(2)}) copy-start(s32[5]{0:T(128)} %param.11) | copy-start | bytes 64
  45.0 10.0 %all-to-all-start = ((bf16[4,128,256]{2,1,0:T(8,128)(2,1)}), bf16[4,128,256]{2,1,0:T(8,128)(2,1)S(1)}, u32[]{:S(2)}, u32[]{:S(2)}) async-start(bf16[4,128,256]{2,1,0:T(8,128)(2,1)} %pick.1), calls=%async_computation | async-start | bytes 524288 | tf_op jit(solution)/shard_map/all_to_all | solution.py:344
  55.0 8.6 %all-to-all-start.2 = ((f32[4,4,2,1024]{3,2,1,0:T(2,128)}), f32[4,4,2,1024]{3,2,1,0:T(2,128)S(1)}, u32[]{:S(2)}, u32[]{:S(2)}) async-start(f32[4,4,2,1024]{3,2,1,0:T(2,128)} %stats.1), calls=%async_computation.2 | async-start | bytes 262144 | tf_op jit(solution)/shard_map/all_to_all | solution.py:344
  59.0 1.3 copy-start.2
  63.6 50.7 %all-to-all-start.3 = ((bf16[8,512,256]{2,1,0:T(8,128)(2,1)}), bf16[8,512,256]{2,1,0:T(8,128)(2,1)}, u32[]{:S(2)}, u32[]{:S(2)}) async-start(bf16[8,512,256]{2,1,0:T(8,128)(2,1)} %copy-done.2), calls=%async_computation.3 | async-start | bytes 4194304 | tf_op jit(solution)/shard_map/all_to_all | solution.py:344
  74.2 14.8 %collective-permute-start.3 = (bf16[3,128,256]{2,1,0:T(8,128)(2,1)S(1)}, bf16[3,128,256]{2,1,0:T(8,128)(2,1)S(1)}, u32[]{:S(2)}, u32[]{:S(2)}) collective-permute-start(bf16[3,128,256]{2,1,0:T(8,128)(2,1)S(1)} %grads4.1), channel_id=1, source_target_pairs={{0,480},{32,0},{64,32},{96,64},{128,96},{160,128},{192,160},{224,1... | collective-permute-start | bytes 589832 | tf_op jit(solution)/shard_map/ppermute | solution.py:45
  89.2 10.6 %collective-permute-start.4 = (bf16[2,128,256]{2,1,0:T(8,128)(2,1)S(1)}, bf16[2,128,256]{2,1,0:T(8,128)(2,1)S(1)}, u32[]{:S(2)}, u32[]{:S(2)}) collective-permute-start(bf16[2,128,256]{2,1,0:T(8,128)(2,1)S(1)} %pad_maximum_fusion.2), channel_id=1, source_target_pairs={{0,448},{32,480},{64,0},{96,32},{128,64},{160,96},{192,128},{224,1... | collective-permute-start | bytes 393224 | tf_op jit(solution)/shard_map/ppermute | solution.py:45
  99.9 14.4 %collective-permute-start.5 = (bf16[128,256]{1,0:T(8,128)(2,1)S(1)}, bf16[128,256]{1,0:T(8,128)(2,1)S(1)}, u32[]{:S(2)}, u32[]{:S(2)}) collective-permute-start(bf16[128,256]{1,0:T(8,128)(2,1)S(1)} %fusion.4), channel_id=1, source_target_pairs={{0,384},{32,416},{64,448},{96,480},{128,0},{160,32},{192,64},{224,... | collective-permute-start | bytes 196616 | tf_op jit(solution)/shard_map/ppermute | solution.py:45
